TPU v7x, 128 devices: a whole 4x4x4 slice. The times are simulated.
128 devices in a mesh: front: 4 (over x_lo, core), row: 8 (over x_hi, y), col: 4 (over z).
Axes of the slice: x: 4 (x_hi: 2, x_lo: 2; x = x_hi * 2 + x_lo), y: 4, z: 4, core: 2. Of those that a mesh axis runs over, the one named last changes fastest.
Arguments:
- parent_entries: float32 [12288, 12288], P('row', ('front', 'col')), as said below
- child_update: float32 [4, 8192, 8192], P('front', 'row', 'col'), as said below
- child_map: int32 [4, 64], replicated, may hold values from 0 to 95, as said below
- child_mask: int32 [4, 64, 64], P('front'), may hold values from 0 to 1, as said below
Outputs:
- schur: float32 [12288, 12288], P('row', ('front', 'col'))
- panel: float32 [12288, 512], P('row')
Inputs may be any that keep to these rules, and one draw needn't show every extreme that they name: `child_update`: each child's update matrix is symmetric. `parent_entries`: Symmetric. `child_mask`: symmetric in its last two dimensions, ones on the diagonal. Distinct within each child. With v = j mod (16), e = v mod (1), r = (v mod 8) div (1), k = (v div 8) * 1 + e and g = r * 2 + k div (1), child_map[f, j] div (6) equals g.
All inputs are finite; a program needn't handle non-finite values.
Results may differ from a plain program's by a relative error of at most 0.000071.
Values sent between devices are 32-bit elements; how exact they have to be, the bound alone decides.
No kernel may reach another device: no remote copies, remote signals or barrier semaphores. Data moves between devices by JAX's collectives and lax.ppermute only.
A program may use at most 128 MiB of HBM per device.

v0:
```python
import jax
import jax.numpy as jnp
from jax import lax
from jax.sharding import PartitionSpec as P

W = 512
BLK = 128


def broadcast(block, axis, holder):
    block = jnp.where(lax.axis_index(axis) == holder, block, jnp.zeros_like(block))
    return lax.psum(block, axis)


def lookup_table(table, wanted, length):
    positions = jnp.arange(length, dtype=jnp.int32)
    return jnp.sum(jnp.where(wanted[..., None] == positions, table, 0), axis=-1)


def body(parent_entries, child_update, child_map, child_mask):
    grid_rows = lax.axis_size("row")
    grid_cols = lax.axis_size("col")
    groups = lax.axis_size(("front", "col"))
    row_index = lax.axis_index("row")
    column_index = lax.axis_index("col")
    group_index = lax.axis_index(("front", "col"))
    local = child_update[0]
    row_blocks = local.shape[0] // BLK
    column_blocks = local.shape[1] // BLK
    total_blocks = child_map.shape[1]
    fronts_count = child_map.shape[0]
    span = min(row_blocks, column_blocks)
    share = span // grid_rows
    per_group = column_blocks // groups
    group_ratio = groups // grid_rows
    front_rows = parent_entries.shape[0]
    front_cols = parent_entries.shape[1]
    parent_row_blocks = front_rows // BLK
    parent_col_blocks = front_cols // BLK
    window = lax.dynamic_slice(
        child_mask[0],
        (row_index * row_blocks, column_index * column_blocks),
        (row_blocks, column_blocks),
    )
    window = window.astype(jnp.float32)
    tiles = local.reshape(row_blocks, BLK, column_blocks, BLK) * window[:, None, :, None]
    tiles = tiles.reshape(
        row_blocks // span, grid_rows, share, BLK, column_blocks // span, grid_rows, share, BLK
    )
    tiles = tiles.transpose(1, 0, 2, 3, 5, 4, 6, 7)
    tiles = tiles.reshape(grid_rows, row_blocks // grid_rows, BLK, groups, per_group, BLK)
    moved = lax.all_to_all(tiles, "row", split_axis=0, concat_axis=0, tiled=True)
    arrived = lax.all_to_all(moved, ("front", "col"), split_axis=3, concat_axis=3, tiled=True)
    sources = jnp.arange(groups, dtype=jnp.int32)
    source_front = sources // grid_cols
    source_column = sources % grid_cols
    picker = source_front[:, None] == jnp.arange(fronts_count, dtype=jnp.int32)[None, :]
    map_rows = jnp.sum(jnp.where(picker[:, :, None], child_map[None, :, :], 0), axis=1)
    from_rows = jnp.arange(grid_rows, dtype=jnp.int32)
    steps_rows = jnp.arange(row_blocks // grid_rows, dtype=jnp.int32)
    child_rows = (
        from_rows[:, None] * row_blocks
        + steps_rows[None, :] // share * span
        + row_index * share
        + steps_rows[None, :] % share
    )
    row_slots = (
        lookup_table(map_rows[:, None, None, :], child_rows[None, :, :], total_blocks)
        - row_index * parent_row_blocks
    )
    steps_cols = jnp.arange(per_group, dtype=jnp.int32)
    ranked = group_index % group_ratio * per_group + steps_cols
    within = ranked // share * span + group_index // group_ratio * share + ranked % share
    child_cols = source_column[:, None] * column_blocks + within[None, :]
    col_slots = (
        lookup_table(map_rows[:, None, :], child_cols, total_blocks)
        - group_index * parent_col_blocks
    )
    row_hits = (
        row_slots[None] == jnp.arange(parent_row_blocks, dtype=jnp.int32)[:, None, None, None]
    )
    col_hits = col_slots[None] == jnp.arange(parent_col_blocks, dtype=jnp.int32)[:, None, None]
    placement = (row_hits[:, None, :, :, :, None] & col_hits[None, :, :, None, None, :]).astype(
        jnp.float32
    )
    assembled = jnp.einsum(
        "absrtw,rtxswy->axby", placement, arrived, precision=lax.Precision.HIGHEST
    )
    front = parent_entries + assembled.reshape(front_rows, front_cols)
    corner = broadcast(front[:W, :W], "row", 0)
    factor = jnp.linalg.cholesky(corner)
    solved = jax.scipy.linalg.solve_triangular(factor, front[:, :W].T, lower=True).T
    panel = broadcast(solved, ("front", "col"), 0)
    piece = lax.dynamic_slice_in_dim(panel, group_index % group_ratio * front_cols, front_cols, 0)
    across = broadcast(piece, "row", group_index // group_ratio)
    schur = front - jnp.dot(panel, across.T, precision=lax.Precision.HIGHEST)
    global_rows = row_index * front_rows + jnp.arange(front_rows, dtype=jnp.int32)
    global_cols = group_index * front_cols + jnp.arange(front_cols, dtype=jnp.int32)
    keep = (global_rows[:, None] >= W) & (global_cols[None, :] >= W)
    return (jnp.where(keep, schur, 0.0), panel)


def solution(mesh):
    placed = (P("row", ("front", "col")), P("front", "row", "col"), P(), P("front", None, None))
    return jax.shard_map(
        body,
        mesh=mesh,
        in_specs=placed,
        out_specs=(P("row", ("front", "col")), P("row", None)),
        check_vma=False,
    )
```

profile of v0, /device:TPU:1, one launch (start us, length us, event | category | flops | bytes accessed | tf_op | source)
XLA Modules:
  0.0 766.9 jit_solution(14635907823872398243)
XLA Ops:
  8.1 5.4 copy.106
  13.5 4.6 copy_multiply_fusion
  18.1 101.5 %all_to_all.10 = f32[8,1,128,16,1,128]{5,3,2,4,1,0:T(8,128)S(1)} all-to-all(f32[8,1,128,16,1,128]{5,3,2,4,1,0:T(8,128)S(1)} %bitcast.83), channel_id=1, replica_groups=mesh['front'=4,'row'=8,'col'=4] {'row'}, dimensions={0} | all-to-all | bytes 16777216 | tf_op jit(solution)/shard_map/all_to_all | solution.py:52
  119.6 8.1 %copy.80 = f32[8,1,128,16,1,128]{5,0,2,4,1,3:T(8,128)} copy(f32[8,1,128,16,1,128]{5,3,2,4,1,0:T(8,128)S(1)} %all_to_all.10) | data formatting | bytes 16777216 | tf_op jit(solution)/shard_map/all_to_all | solution.py:52
  127.7 9.3 %all-to-all-start.1 = ((f32[8,1,128,16,1,128]{5,0,2,4,1,3:T(8,128)}), f32[8,1,128,16,1,128]{5,0,2,4,1,3:T(8,128)}, u32[]{:S(2)}, u32[]{:S(2)}) async-start(f32[8,1,128,16,1,128]{5,0,2,4,1,3:T(8,128)} %copy.80), calls=%async_computation.1 | async-start | bytes 16777216 | tf_op jit(solution)/shard_map/all_to_all | solution.py:53
  137.9 6.1 copy.84
  144.2 92.3 %all-to-all-done.1 = f32[8,1,128,16,1,128]{5,0,2,4,1,3:T(8,128)} async-done(((f32[8,1,128,16,1,128]{5,0,2,4,1,3:T(8,128)}), f32[8,1,128,16,1,128]{5,0,2,4,1,3:T(8,128)}, u32[]{:S(2)}, u32[]{:S(2)}) %all-to-all-start.1) | async-done | bytes 8388640 | tf_op jit(solution)/shard_map/all_to_all | solution.py:53
  236.4 13.4 %fusion.4 = f32[12,128,6,128]{3,0,2,1:T(8,128)} fusion(f32[8,1,128,16,1,128]{5,0,2,4,1,3:T(8,128)} %all-to-all-done.1, pred[6,16]{1,0:T(8,128)(4,1)S(1)} %iota_compare_fusion.5, pred[12,16,8]{1,0,2:T(8,128)(4,1)S(1)} %iota_compare_fusion.3), kind=kOutput, calls=%fused_computation.11 | convolution fusion | flops 1811948544 | bytes 13108832 | tf_op jit(solution)/shard_map/absrtw,rtxswy->axby/dot_general | solution.py:86
  249.9 6.7 copy.103
  256.6 6.8 bitcast_add_fusion
  269.3 80.7 %all-reduce.5.cloned.1.call-done = f32[512,512]{0,1:T(8,128)} async-done(((f32[512,512]{0,1:T(8,128)}), f32[512,512]{0,1:T(8,128)}) %all-reduce.5.cloned.1.call-update) | async-done | bytes 1048592 | tf_op jit(solution)/shard_map/psum | solution.py:12
  355.3 11.7 %cholesky.103 = f32[128,128]{1,0:T(8,128)S(1)} custom-call(f32[128,128]{1,0:T(8,128)S(1)} %cholesky.263), custom_call_target="Cholesky" | custom-call | tf_op jit(solution)/shard_map/jit(cholesky)/cholesky | solution.py:91
  367.6 9.8 %custom-call.31 = f32[1,128,128]{1,2,0:T(8,128)S(1)} custom-call(f32[1,128,128]{2,1,0:T(8,128)S(1)} %get-tuple-element.55), custom_call_target="InvertDiagBlocksLowerTriangular" | custom-call | tf_op jit(solution)/shard_map/jit(cholesky)/cholesky | solution.py:91
  380.6 11.7 %cholesky.215 = f32[128,128]{1,0:T(8,128)S(1)} custom-call(f32[128,128]{1,0:T(8,128)S(1)} %cholesky.267), custom_call_target="Cholesky" | custom-call | tf_op jit(solution)/shard_map/jit(cholesky)/cholesky | solution.py:91
  394.8 10.8 %custom-call.32 = f32[1,128,128]{1,2,0:T(8,128)S(1)} custom-call(f32[1,128,128]{2,1,0:T(8,128)} %get-tuple-element.53), custom_call_target="InvertDiagBlocksLowerTriangular" | custom-call | tf_op jit(solution)/shard_map/jit(cholesky)/cholesky | solution.py:91
  410.3 11.7 %cholesky.236 = f32[128,128]{1,0:T(8,128)S(1)} custom-call(f32[128,128]{1,0:T(8,128)S(1)} %cholesky.272), custom_call_target="Cholesky" | custom-call | tf_op jit(solution)/shard_map/jit(cholesky)/cholesky | solution.py:91
  422.8 9.8 %custom-call.33 = f32[1,128,128]{1,2,0:T(8,128)S(1)} custom-call(f32[1,128,128]{2,1,0:T(8,128)S(1)} %get-tuple-element.51), custom_call_target="InvertDiagBlocksLowerTriangular" | custom-call | tf_op jit(solution)/shard_map/jit(cholesky)/cholesky | solution.py:91
  435.0 11.9 %cholesky.253 = f32[128,128]{1,0:T(8,128)S(1)} custom-call(f32[128,128]{1,0:T(8,128)S(1)} %convolution_subtract_fusion.5), custom_call_target="Cholesky" | custom-call | tf_op jit(solution)/shard_map/jit(cholesky)/cholesky | solution.py:91
  454.0 14.5 %while.1 = (s32[]{:T(128)}, f32[512,512]{0,1:T(8,128)}, s32[4,2]{0,1:T(2,128)S(1)}, f32[4,128,128]{2,1,0:T(8,128)}, s32[]{:T(128)}) while((s32[]{:T(128)}, f32[512,512]{0,1:T(8,128)}, s32[4,2]{0,1:T(2,128)S(1)}, f32[4,128,128]{2,1,0:T(8,128)}, s32[]{:T(128)}) %tuple.37), condition=%wide.while_cond, body=%wide.while_body.sunk | while | flops 2 | bytes 393829 | solution.py:92
  468.5 40.1 %custom-call.34 = f32[4,128,128]{1,2,0:T(8,128)S(1)} custom-call(f32[4,128,128]{2,1,0:T(8,128)} %get-tuple-element.9), custom_call_target="InvertDiagBlocksLowerTriangular" | custom-call | tf_op jit(solution)/shard_map/jit(_solve_triangular)/triangular_solve | solution.py:92
  520.4 132.7 %all-reduce.7.cloned.1.call-done = f32[1536,512]{0,1:T(8,128)} async-done(((f32[1536,512]{0,1:T(8,128)}), f32[1536,512]{0,1:T(8,128)}) %all-reduce.7.cloned.1.call-update) | async-done | bytes 3145744 | tf_op jit(solution)/shard_map/psum | solution.py:12
  658.3 83.9 %all-reduce.9.cloned.1.call-done = f32[768,512]{0,1:T(8,128)} async-done(((f32[768,512]{0,1:T(8,128)}), f32[768,512]{0,1:T(8,128)}) %all-reduce.9.cloned.1.call-update) | async-done | bytes 1572880 | tf_op jit(solution)/shard_map/psum | solution.py:12
  742.2 11.6 %subtract_select_fusion = f32[1536,768]{0,1:T(8,128)} fusion(f32[1536,768]{0,1:T(8,128)} %copy-done, f32[1536,512]{0,1:T(8,128)S(1)} %copy-done.1, f32[768,512]{0,1:T(8,128)} %all-reduce.9.cloned.1.call-done, pred[1536]{0:T(1024)(128)(4,1)S(1)} %add_compare_fusion, pred[768]{0:T(1024)(128)(4,1)S(1)} %add_compare_fusion.1), kind=kOutput, calls=%fused_computation.7 | convolution fusion | flops 7251296256 | bytes 14158080 | tf_op jit(solution)/shard_map/dot_general | solution.py:96
  753.9 6.0 copy.96
  (102 shorter events, 63.1 us)
Async XLA Ops:
  127.7 9.6 %copy-start.6 = (s32[4,64]{1,0:T(4,128)S(1)}, s32[4,64]{1,0:T(4,128)}, u32[]{:S(2)}) copy-start(s32[4,64]{1,0:T(4,128)} %param.6) | copy-start | bytes 3076
  127.7 108.7 %all-to-all-start.1 = ((f32[8,1,128,16,1,128]{5,0,2,4,1,3:T(8,128)}), f32[8,1,128,16,1,128]{5,0,2,4,1,3:T(8,128)}, u32[]{:S(2)}, u32[]{:S(2)}) async-start(f32[8,1,128,16,1,128]{5,0,2,4,1,3:T(8,128)} %copy.80), calls=%async_computation.1 | async-start | bytes 16777216 | tf_op jit(solution)/shard_map/all_to_all | solution.py:53
  137.0 213.0 %all-reduce.5.cloned.1.call-start = ((), (), s32[]{:S(2)}) async-start(), calls=%async_computation.2 | async-start | bytes 2097152 | tf_op jit(solution)/shard_map/psum | solution.py:12
  263.4 2.2 copy-start
  266.7 386.4 %all-reduce.7.cloned.1.call-start = ((), (), s32[]{:S(2)}) async-start(), calls=%async_computation.3 | async-start | bytes 6291456 | tf_op jit(solution)/shard_map/psum | solution.py:12
  354.3 1.0 copy-start.3
  367.0 0.6 copy-start.5
  380.0 0.7 copy-start.4
  407.8 1.0 copy-start.2
  520.1 222.1 %all-reduce.9.cloned.1.call-start = ((), (), s32[]{:S(2)}) async-start(), calls=%async_computation.4 | async-start | bytes 3145728 | tf_op jit(solution)/shard_map/psum | solution.py:12
  653.1 2.9 copy-start.1
Sparse Core Ops, SparseCore 0:
  266.8 83.1 all-reduce.4
  520.2 132.8 all-reduce.6
  656.0 86.1 all-reduce.8
where the time goes:
time: 778 us; the launch traced here: 767 us
  waiting for transfers between devices  390 us (50%)
  other arithmetic  143 us (18%)
  blocking collectives  102 us (13%)
  local copies, waits for them, and re-layouts  63.6 us (8%)
  matrix products  42.2 us (5%)
  between operations  17.1 us (2%)
  starting transfers between devices  10.3 us (1%)
    psum x3, waiting for transfers between devices, broadcast(): return lax.psum(block, axis)  297 us
    all_to_all x1, blocking collectives, body(): lax.all_to_all(tiles, 'row', split_axis=0, concat_axis=0, tiled=True)  102 us
    all_to_all x1, waiting for transfers between devices, body(): lax.all_to_all(moved, ('front', 'col'), split_axis=3, concat_axis=3, tile...  92.3 us
    another operation x15, other arithmetic, body(): factor = jnp.linalg.cholesky(corner)  80.8 us
    another operation x3, other arithmetic, body(): jax.scipy.linalg.solve_triangular(factor, front[:, :W].T, lower=True)  41.2 us
    unnamed x18, local copies, waits for them, and re-layouts  25.2 us
  transfers between devices with their start and end apart: 4, of which 4 were waited for; matrix products, arithmetic and copies ran while one was open for 1% of the time, Pallas kernels for 0%

commit v1 on v0

v1 whole, which is shorter than its diff:
```python
import functools

import jax
import jax.numpy as jnp
from jax import lax
from jax.experimental import pallas as pl
from jax.experimental.pallas import tpu as pltpu
from jax.sharding import PartitionSpec as P

W = 512
BLK = 128
FRONTS = 4
ROWS = 8
COLS = 4
GROUPS = 16
PR = 12
PC = 6
WB = W // BLK
ALL = ("front", "row", "col")
GRP = ("front", "col")
HIGHEST = lax.Precision.HIGHEST


def group_column(group):
    return group // 2 + 8 * (group % 2)


def pack_kernel(mask_ref, x_ref, o_ref):
    step = pl.program_id(0)
    for front in range(FRONTS):
        for col in range(COLS):
            v = group_column(front * COLS + col)
            keep = mask_ref[step, v].astype(jnp.float32)
            o_ref[front, 0, col] = x_ref[:, v * BLK : (v + 1) * BLK] * keep


def pack(window, local):
    return pl.pallas_call(
        pack_kernel,
        name="pack",
        grid_spec=pltpu.PrefetchScalarGridSpec(
            num_scalar_prefetch=1,
            grid=(ROWS,),
            in_specs=[pl.BlockSpec((BLK, GROUPS * BLK), lambda i, m: (i, 0))],
            out_specs=pl.BlockSpec(
                (FRONTS, 1, COLS, BLK, BLK), lambda i, m: (0, i, 0, 0, 0)
            ),
        ),
        out_shape=jax.ShapeDtypeStruct((FRONTS, ROWS, COLS, BLK, BLK), jnp.float32),
        compiler_params=pltpu.CompilerParams(vmem_limit_bytes=32 << 20),
    )(window, local)


def slice_kernel(inv_row_ref, inv_lead_ref, recv_ref, parent_ref, o_ref):
    for a in range(PR):
        for q in range(WB):
            total = parent_ref[a, :, q * BLK : (q + 1) * BLK]
            for front in range(FRONTS):
                r = inv_row_ref[front, a]
                c = inv_lead_ref[front, q]
                ok = jnp.logical_and(r >= 0, c >= 0).astype(jnp.float32)
                source = front * 32 + jnp.maximum(r, 0) * COLS + jnp.maximum(c, 0)
                total = total + recv_ref[source] * ok
            o_ref[a, :, q * BLK : (q + 1) * BLK] = total


def assemble_slices(inv_row, inv_lead, recv, parent):
    smem = pl.BlockSpec(memory_space=pltpu.SMEM)
    vmem = pl.BlockSpec(memory_space=pltpu.VMEM)
    return pl.pallas_call(
        slice_kernel,
        name="slices",
        in_specs=[smem, smem, vmem, vmem],
        out_specs=vmem,
        out_shape=jax.ShapeDtypeStruct((PR, 8, W), jnp.float32),
    )(inv_row, inv_lead, recv, parent)


def final_kernel(inv_row_ref, inv_col_ref, lead_ref, *refs):
    recvs = refs[:FRONTS]
    parent_ref, panel_ref, across_ref, o_ref = refs[FRONTS:]
    a = pl.program_id(0)
    product = lax.dot_general(
        panel_ref[...],
        across_ref[...],
        (((1,), (1,)), ((), ())),
        precision=HIGHEST,
        preferred_element_type=jnp.float32,
    )
    o_ref[...] = parent_ref[...] - product
    for b in range(PC):
        span = slice(b * BLK, (b + 1) * BLK)
        total = o_ref[:, span]
        for front in range(FRONTS):
            r = inv_row_ref[front, a]
            c = inv_col_ref[front, b]
            ok = jnp.logical_and(r >= 0, c >= 0).astype(jnp.float32)
            total = total + recvs[front][jnp.maximum(c, 0)] * ok
        o_ref[:, span] = total
    leading_row = jnp.logical_and(lead_ref[0] == 1, a < WB)

    @pl.when(leading_row)
    def _():
        o_ref[...] = jnp.zeros_like(o_ref)

    @pl.when(lead_ref[1] == 1)
    def _():
        o_ref[:, :W] = jnp.zeros((BLK, W), jnp.float32)


def finish(inv_row, inv_col, lead, recv, parent, panel, across):
    def recv_map(front):
        return lambda a, ir, ic, ld: (front * ROWS + jnp.maximum(ir[front, a], 0), 0, 0)

    return pl.pallas_call(
        final_kernel,
        name="finish",
        grid_spec=pltpu.PrefetchScalarGridSpec(
            num_scalar_prefetch=3,
            grid=(PR,),
            in_specs=[
                pl.BlockSpec((COLS, BLK, BLK), recv_map(front)) for front in range(FRONTS)
            ]
            + [
                pl.BlockSpec((BLK, PC * BLK), lambda a, *_: (a, 0)),
                pl.BlockSpec((BLK, W), lambda a, *_: (a, 0)),
                pl.BlockSpec((PC * BLK, W), lambda a, *_: (0, 0)),
            ],
            out_specs=pl.BlockSpec((BLK, PC * BLK), lambda a, *_: (a, 0)),
        ),
        out_shape=jax.ShapeDtypeStruct((PR * BLK, PC * BLK), jnp.float32),
        compiler_params=pltpu.CompilerParams(vmem_limit_bytes=40 << 20),
    )(inv_row, inv_col, lead, recv, recv, recv, recv, parent, panel, across)


def inverse_places(places, length):
    count = places.shape[1]
    hits = places[:, :, None] == jnp.arange(length, dtype=jnp.int32)
    order = jnp.arange(1, count + 1, dtype=jnp.int32)[None, :, None]
    return jnp.sum(jnp.where(hits, order, 0), axis=1) - 1


def scatter_from_first(x, axis, parts):
    index = lax.axis_index(axis)
    total = jnp.where(index == 0, parts(x, 0), 0.0)
    for k in range(1, lax.axis_size(axis)):
        total = total + lax.ppermute(parts(x, k), axis, [(0, k)])
    return total


def swap_pairs(flip):
    pairs = []
    for front in range(FRONTS):
        for row in range(ROWS):
            for col in range(COLS):
                group = front * COLS + col
                half = group % 2 if flip == 0 else 1 - group % 2
                to_row, to_group = group // 2, 2 * row + half
                target = (to_group // COLS) * 32 + to_row * COLS + to_group % COLS
                pairs.append((front * 32 + row * COLS + col, target))
    return pairs


def body(parent_entries, child_update, child_map, child_mask):
    row = lax.axis_index("row")
    front = lax.axis_index("front")
    col = lax.axis_index("col")
    group = front * COLS + col
    local = child_update[0]
    window = lax.dynamic_slice(child_mask[0], (row * ROWS, col * GROUPS), (ROWS, GROUPS))

    lead_keep = window[:, 0].astype(jnp.float32)
    lead = local[:, :BLK].reshape(ROWS, FRONTS, COLS, 8, BLK) * lead_keep[:, None, None, None, None]
    lead = lead.transpose(1, 0, 2, 3, 4).reshape(128, 8, BLK)
    lead_recv = lax.all_to_all(lead, ALL, 0, 0, tiled=True)

    first = parent_entries[:, :W].reshape(PR, FRONTS, COLS, 8, W)
    first = scatter_from_first(first, "col", lambda x, k: x[:, :, k])
    first = scatter_from_first(first, "front", lambda x, k: x[:, k])

    column = group // 2 + 8 * (group % 2)
    by_row = lax.dynamic_index_in_dim(child_map.reshape(FRONTS, ROWS, 8), row, 2, keepdims=False)
    by_col = lax.dynamic_index_in_dim(
        child_map.reshape(FRONTS, COLS, GROUPS), column, 2, keepdims=False
    )
    inv_row = inverse_places(by_row - row * PR, PR)
    inv_col = inverse_places(by_col - group * PC, PC)
    inv_lead = inverse_places(child_map.reshape(FRONTS, COLS, GROUPS)[:, :, 0], WB)

    slices = assemble_slices(inv_row, inv_lead, lead_recv, first)

    corner = jnp.broadcast_to(slices[:WB].reshape(1, WB * 8, W), (ROWS, WB * 8, W))
    corner = lax.all_to_all(corner, "row", 0, 0, tiled=True)[0]
    corner = jnp.broadcast_to(corner[None], (GROUPS, WB * 8, W))
    corner = lax.all_to_all(corner, GRP, 0, 0, tiled=True)
    corner = corner.reshape(GROUPS, WB, 8, W).transpose(1, 0, 2, 3).reshape(W, W)

    packed = pack(window, local).reshape(128, BLK, BLK)
    recv = lax.all_to_all(packed, ALL, 0, 0, tiled=True)

    rows_raw = lax.all_gather(slices.reshape(PR * 8, W), GRP, axis=0, tiled=True)
    rows_raw = rows_raw.reshape(GROUPS, PR, 8, W).transpose(1, 0, 2, 3).reshape(PR * BLK, W)

    even = group % 2 == 0
    one = lax.ppermute(jnp.where(even, slices[:PC], slices[PC:]), ALL, swap_pairs(0))
    two = lax.ppermute(jnp.where(even, slices[PC:], slices[:PC]), ALL, swap_pairs(1))
    mine = jnp.stack([jnp.where(even, one, two), jnp.where(even, two, one)], axis=1)
    cols_raw = lax.all_gather(mine.reshape(PC * 16, W), "row", axis=0, tiled=True)
    cols_raw = cols_raw.reshape(ROWS, PC, 16, W).transpose(1, 0, 2, 3).reshape(PC * BLK, W)

    factor = jnp.linalg.cholesky(corner)
    inverse = jax.scipy.linalg.solve_triangular(factor, jnp.eye(W, dtype=jnp.float32), lower=True)
    panel = jnp.dot(rows_raw, inverse.T, precision=HIGHEST)
    across = jnp.dot(cols_raw, inverse.T, precision=HIGHEST)
    lead_flags = jnp.stack([row == 0, group == 0]).astype(jnp.int32)
    schur = finish(inv_row, inv_col, lead_flags, recv, parent_entries, panel, across)
    return schur, panel


def solution(mesh):
    placed = (P("row", ("front", "col")), P("front", "row", "col"), P(), P("front", None, None))
    return jax.shard_map(
        body,
        mesh=mesh,
        in_specs=placed,
        out_specs=(P("row", ("front", "col")), P("row", None)),
        check_vma=False,
    )
```

time: 778 us -> 332 us (0.43)
  waiting for transfers between devices: 390 us -> 47.2 us
  blocking collectives: 102 us -> 0 us
  starting transfers between devices: 10.3 us -> 53.7 us
  local copies, waits for them, and re-layouts: 63.6 us -> 34.7 us
  Pallas kernels: 0 us -> 28.8 us
  matrix products: 42.2 us -> 19.3 us
  other arithmetic: 143 us -> 126 us
    psum x3 -> x0, waiting for transfers between devices: 297 us -> none  [broadcast(): return lax.psum(block, axis)]
    all_to_all x1 -> x0, blocking collectives: 102 us -> none  [body(): lax.all_to_all(tiles, 'row', split_axis=0, concat_axis=0, tiled=True)]
    all_to_all x1 -> x4, waiting for transfers between devices: 92.3 us -> 14.7 us  [the longest x1 7.96 us: body(): corner = lax.all_to_all(corner, 'row', 0, 0, tiled=True)[0]]
    ppermute x0 -> x8, waiting for transfers between devices: none -> 32.4 us  [the longest x6 32.4 us: scatter_from_first(): total = total + lax.ppermute(parts(x, k), axis, [(0, k)])]
    pallas_call x0 -> x3, Pallas kernels: none -> 28.8 us  [the longest x1 24.5 us: finish(): pl.pallas_call(final_kernel, name='finish', grid_spec=pltpu.PrefetchScala...]
    all_to_all x1 -> x4, starting transfers between devices: 9.27 us -> 32.4 us  [the longest x1 11.5 us: body(): lead_recv = lax.all_to_all(lead, ALL, 0, 0, tiled=True)]
    ppermute x0 -> x8, starting transfers between devices: none -> 21 us  [the longest x6 13.1 us: scatter_from_first(): total = total + lax.ppermute(parts(x, k), axis, [(0, k)])]
    dot_general x2, matrix products: 25.1 us -> 9 us  [the longest x1 5.19 us: body(): panel = jnp.dot(rows_raw, inverse.T, precision=HIGHEST)]
  transfers between devices with their start and end apart: 4 -> 14, of which waited for: 4 -> 6; matrix products, arithmetic and copies ran while one was open for 1% -> 49% of each run, Pallas kernels for 0% -> 1%
where the time goes in v1:
time: 332 us; the launch traced here: 327 us
  other arithmetic  126 us (38%)
  starting transfers between devices  53.7 us (16%)
  waiting for transfers between devices  47.2 us (14%)
  local copies, waits for them, and re-layouts  34.7 us (10%)
  Pallas kernels  28.8 us (9%)
  matrix products  19.3 us (6%)
  between operations  17.5 us (5%)
    another operation x14, other arithmetic, body(): factor = jnp.linalg.cholesky(corner)  78.8 us
    another operation x3, other arithmetic, body(): jax.scipy.linalg.solve_triangular(factor, jnp.eye(W, dtype=jnp.float32),...  39.6 us
    ppermute x6, waiting for transfers between devices, scatter_from_first(): total = total + lax.ppermute(parts(x, k), axis, [(0, k)])  32.4 us
    pallas_call x1, Pallas kernels, finish(): pl.pallas_call(final_kernel, name='finish', grid_spec=pltpu.PrefetchScala...  24.5 us
    unnamed x42, local copies, waits for them, and re-layouts  14.7 us
    ppermute x6, starting transfers between devices, scatter_from_first(): total = total + lax.ppermute(parts(x, k), axis, [(0, k)])  13.1 us
    all_to_all x1, starting transfers between devices, body(): lead_recv = lax.all_to_all(lead, ALL, 0, 0, tiled=True)  11.5 us
    another operation x12, local copies, waits for them, and re-layouts  8.37 us
  transfers between devices with their start and end apart: 14, of which 6 were waited for; matrix products, arithmetic and copies ran while one was open for 49% of the time, Pallas kernels for 1%

profile of v1, /device:TPU:1, one launch (start us, length us, event | category | flops | bytes accessed | tf_op | source)
XLA Modules:
  0.0 327.1 jit_solution(5285206572594847645)
XLA Ops:
  9.4 11.5 %all-to-all-start.1 = ((f32[128,8,128]{2,1,0:T(8,128)}), f32[128,8,128]{2,1,0:T(8,128)S(1)}, u32[]{:S(2)}, u32[]{:S(2)}) async-start(f32[128,8,128]{2,1,0:T(8,128)} %bitcast.10), calls=%async_computation.1 | async-start | bytes 1048576 | tf_op jit(solution)/shard_map/all_to_all | solution.py:175
  23.2 6.1 %collective-permute-start.2 = (f32[12,4,8,512]{3,2,0,1:T(8,128)S(1)}, f32[12,4,8,512]{3,2,0,1:T(8,128)}, u32[]{:S(2)}, u32[]{:S(2)}) collective-permute-start(f32[12,4,8,512]{3,2,0,1:T(8,128)S(1)} %bitcast.131), channel_id=1, source_target_pairs={{0,3},{4,7},{8,11},{12,15},{16,19},{20,23},{24,27},{28,31},{32,35}... | collective-permute-start | bytes 2359304 | tf_op jit(solution)/shard_map/ppermute | solution.py:147
  36.0 10.5 %collective-permute-done.2 = f32[12,4,8,512]{3,2,0,1:T(8,128)} collective-permute-done((f32[12,4,8,512]{3,2,0,1:T(8,128)S(1)}, f32[12,4,8,512]{3,2,0,1:T(8,128)}, u32[]{:S(2)}, u32[]{:S(2)}) %collective-permute-start.2) | collective-permute-done | bytes 786464 | tf_op jit(solution)/shard_map/ppermute | solution.py:147
  47.3 17.0 %collective-permute-done = f32[12,4,8,512]{3,2,0,1:T(8,128)} collective-permute-done((f32[12,4,8,512]{3,2,0,1:T(8,128)}, f32[12,4,8,512]{3,2,0,1:T(8,128)}, u32[]{:S(2)}, u32[]{:S(2)}) %collective-permute-start) | collective-permute-done | bytes 786464 | tf_op jit(solution)/shard_map/ppermute | solution.py:147
  69.5 4.1 %collective-permute-done.3 = f32[12,8,512]{2,1,0:T(8,128)S(1)} collective-permute-done((f32[12,8,512]{2,1,0:T(8,128)S(1)}, f32[12,8,512]{2,1,0:T(8,128)S(1)}, u32[]{:S(2)}, u32[]{:S(2)}) %collective-permute-start.3) | collective-permute-done | bytes 196640 | tf_op jit(solution)/shard_map/ppermute | solution.py:147
  78.6 5.9 %collective-permute-start.6 = (f32[6,8,512]{2,1,0:T(8,128)S(1)}, f32[6,8,512]{2,1,0:T(8,128)S(1)}, u32[]{:S(2)}, u32[]{:S(2)}) collective-permute-start(f32[6,8,512]{2,1,0:T(8,128)S(1)} %get-tuple-element.29), channel_id=1, source_target_pairs={{0,0},{1,1},{2,4},{3,5},{4,2},{5,3},{6,6},{7,7},{8,32},{9,33},{10,... | collective-permute-start | bytes 294920 | tf_op jit(solution)/shard_map/ppermute | solution.py:205
  88.2 6.5 %all-to-all-start.2 = ((f32[8,32,512]{2,1,0:T(8,128)}), f32[8,32,512]{2,1,0:T(8,128)S(1)}, u32[]{:S(2)}, u32[]{:S(2)}) async-start(f32[8,32,512]{2,1,0:T(8,128)} %broadcast_in_dim.78), calls=%async_computation.2 | async-start | bytes 1048576 | tf_op jit(solution)/shard_map/all_to_all | solution.py:193
  95.5 8.0 %all-to-all-done.2 = f32[8,32,512]{2,1,0:T(8,128)S(1)} async-done(((f32[8,32,512]{2,1,0:T(8,128)}), f32[8,32,512]{2,1,0:T(8,128)S(1)}, u32[]{:S(2)}, u32[]{:S(2)}) %all-to-all-start.2) | async-done | bytes 524320 | tf_op jit(solution)/shard_map/all_to_all | solution.py:193
  104.6 7.5 %all-to-all-start.3 = ((f32[16,32,512]{2,1,0:T(8,128)}), f32[16,32,512]{2,1,0:T(8,128)S(1)}, u32[]{:S(2)}, u32[]{:S(2)}) async-start(f32[16,32,512]{2,1,0:T(8,128)} %broadcast_in_dim.80), calls=%async_computation.3 | async-start | bytes 2097152 | tf_op jit(solution)/shard_map/all_to_all | solution.py:195
  120.6 6.8 %all-to-all-done.3 = f32[16,32,512]{2,1,0:T(8,128)S(1)} async-done(((f32[16,32,512]{2,1,0:T(8,128)}), f32[16,32,512]{2,1,0:T(8,128)S(1)}, u32[]{:S(2)}, u32[]{:S(2)}) %all-to-all-start.3) | async-done | bytes 1048608 | tf_op jit(solution)/shard_map/all_to_all | solution.py:195
  127.4 6.9 %all-to-all-start = ((f32[128,128,128]{2,1,0:T(8,128)}), f32[128,128,128]{2,1,0:T(8,128)}, u32[]{:S(2)}, u32[]{:S(2)}) async-start(f32[128,128,128]{2,1,0:T(8,128)} %bitcast.119), calls=%async_computation | async-start | bytes 16777216 | tf_op jit(solution)/shard_map/all_to_all | solution.py:199
  137.5 11.7 %cholesky.104 = f32[128,128]{1,0:T(8,128)S(1)} custom-call(f32[128,128]{1,0:T(8,128)S(1)} %cholesky.266), custom_call_target="Cholesky" | custom-call | tf_op jit(solution)/shard_map/jit(cholesky)/cholesky | solution.py:211
  149.4 9.8 %custom-call.31 = f32[1,128,128]{1,2,0:T(8,128)S(1)} custom-call(f32[1,128,128]{2,1,0:T(8,128)S(1)} %get-tuple-element.40), custom_call_target="InvertDiagBlocksLowerTriangular" | custom-call | tf_op jit(solution)/shard_map/jit(cholesky)/cholesky | solution.py:211
  161.7 11.7 %cholesky.217 = f32[128,128]{1,0:T(8,128)S(1)} custom-call(f32[128,128]{1,0:T(8,128)S(1)} %cholesky.270), custom_call_target="Cholesky" | custom-call | tf_op jit(solution)/shard_map/jit(cholesky)/cholesky | solution.py:211
  173.5 10.2 %custom-call.32 = f32[1,128,128]{1,2,0:T(8,128)S(1)} custom-call(f32[1,128,128]{2,1,0:T(8,128)S(1)} %get-tuple-element.37), custom_call_target="InvertDiagBlocksLowerTriangular" | custom-call | tf_op jit(solution)/shard_map/jit(cholesky)/cholesky | solution.py:211
  185.2 11.7 %cholesky.238 = f32[128,128]{1,0:T(8,128)S(1)} custom-call(f32[128,128]{1,0:T(8,128)S(1)} %cholesky.275), custom_call_target="Cholesky" | custom-call | tf_op jit(solution)/shard_map/jit(cholesky)/cholesky | solution.py:211
  197.0 9.8 %custom-call.33 = f32[1,128,128]{1,2,0:T(8,128)S(1)} custom-call(f32[1,128,128]{2,1,0:T(8,128)S(1)} %get-tuple-element.34), custom_call_target="InvertDiagBlocksLowerTriangular" | custom-call | tf_op jit(solution)/shard_map/jit(cholesky)/cholesky | solution.py:211
  208.2 11.7 %cholesky.255 = f32[128,128]{1,0:T(8,128)S(1)} custom-call(f32[128,128]{1,0:T(8,128)S(1)} %convolution_subtract_fusion.5), custom_call_target="Cholesky" | custom-call | tf_op jit(solution)/shard_map/jit(cholesky)/cholesky | solution.py:211
  224.8 8.5 %while.1 = (s32[]{:T(128)}, f32[512,512]{1,0:T(8,128)S(1)}, s32[4,2]{0,1:T(2,128)S(1)}, f32[4,128,128]{2,1,0:T(8,128)S(1)}, s32[]{:T(128)}) while((s32[]{:T(128)}, f32[512,512]{1,0:T(8,128)S(1)}, s32[4,2]{0,1:T(2,128)S(1)}, f32[4,128,128]{2,1,0:T(8,128)S(1)}, s32[]{:T(128)}) %tuple.39), condition=%wide.while_cond, body=%wide.while_body.sunk | while | flops 2 | bytes 131189 | solution.py:212
  233.2 39.5 %custom-call.34 = f32[4,128,128]{1,2,0:T(8,128)S(1)} custom-call(f32[4,128,128]{2,1,0:T(8,128)S(1)} %get-tuple-element.9), custom_call_target="InvertDiagBlocksLowerTriangular" | custom-call | tf_op jit(solution)/shard_map/jit(_solve_triangular)/triangular_solve | solution.py:212
  279.3 3.8 %fusion.10.refs_6_ = f32[768,512]{1,0:T(8,128)} fusion(f32[768,512]{1,0:T(8,128)S(1)} %bitcast.125, f32[128,512]{1,0:T(8,128)S(1)} %fusion.30, f32[128,512]{1,0:T(8,128)S(1)} %fusion.31, f32[128,512]{1,0:T(8,128)S(1)} %fusion.33, f32[128,512]{1,0:T(8,128)S(1)} %fusion.17), kind=kOutput, calls=%fused_computation.29 | convolution fusion | flops 2416705536 | bytes 4194304 | tf_op jit(solution)/shard_map/dot_general | solution.py:214
  285.4 5.2 %fusion.11.refs_5_ = f32[1536,512]{1,0:T(8,128)S(1)} fusion(f32[1536,512]{1,0:T(8,128)S(1)} %bitcast.123, f32[128,512]{1,0:T(8,128)S(1)} %copy-done.15, f32[128,512]{1,0:T(8,128)S(1)} %copy-done.11, f32[128,512]{1,0:T(8,128)S(1)} %copy-done.9, f32[128,512]{1,0:T(8,128)S(1)} %fusion.17), kind=kOutput, calls=%fused_computation.30 | convolution fusion | flops 4832624640 | bytes 7340032 | tf_op jit(solution)/shard_map/dot_general | solution.py:213
  290.7 3.5 %copy-done.4 = f32[1536,768]{1,0:T(8,128)S(1)} copy-done((f32[1536,768]{1,0:T(8,128)S(1)}, f32[1536,768]{1,0:T(8,128)}, u32[]{:S(2)}) %copy-start.4) | copy-done | bytes 4718616
  295.5 24.5 %finish.1 = f32[1536,768]{1,0:T(8,128)} custom-call(s32[4,12]{1,0:T(4,128)S(1)} %copy-done.7, s32[4,6]{1,0:T(4,128)S(1)} %broadcast_add_fusion.1.inv_col_ref, s32[2]{0:T(128)S(1)} %add_convert_fusion.lead_ref, f32[128,128,128]{2,1,0:T(8,128)} %all-to-all-done.refs_0_.refs_1_.refs_2_.refs_3_, f32[128,128,128]{2,1,0:T(8,128)} %all-to-all-done.refs_0_.refs_1_.refs_2_.refs_3_, ...), custom_call_target="tpu_custom_call" | custom-call | tf_op jit(solution)/shard_map/finish/pallas_call | solution.py:115
  (141 shorter events, 65.7 us)
Async XLA Ops:
  9.4 65.0 %all-to-all-start.1 = ((f32[128,8,128]{2,1,0:T(8,128)}), f32[128,8,128]{2,1,0:T(8,128)S(1)}, u32[]{:S(2)}, u32[]{:S(2)}) async-start(f32[128,8,128]{2,1,0:T(8,128)} %bitcast.10), calls=%async_computation.1 | async-start | bytes 1048576 | tf_op jit(solution)/shard_map/all_to_all | solution.py:175
  23.2 11.5 %copy-start.17 = (s32[4,64]{1,0:T(4,128)S(1)}, s32[4,64]{1,0:T(4,128)}, u32[]{:S(2)}) copy-start(s32[4,64]{1,0:T(4,128)} %param.6) | copy-start | bytes 3076
  23.2 23.3 %collective-permute-start.2 = (f32[12,4,8,512]{3,2,0,1:T(8,128)S(1)}, f32[12,4,8,512]{3,2,0,1:T(8,128)}, u32[]{:S(2)}, u32[]{:S(2)}) collective-permute-start(f32[12,4,8,512]{3,2,0,1:T(8,128)S(1)} %bitcast.131), channel_id=1, source_target_pairs={{0,3},{4,7},{8,11},{12,15},{16,19},{20,23},{24,27},{28,31},{32,35}... | collective-permute-start | bytes 2359304 | tf_op jit(solution)/shard_map/ppermute | solution.py:147
  29.4 17.9 %collective-permute-start.1 = (f32[12,4,8,512]{3,2,0,1:T(8,128)S(1)}, f32[12,4,8,512]{3,2,0,1:T(8,128)}, u32[]{:S(2)}, u32[]{:S(2)}) collective-permute-start(f32[12,4,8,512]{3,2,0,1:T(8,128)S(1)} %bitcast.132), channel_id=1, source_target_pairs={{0,2},{4,6},{8,10},{12,14},{16,18},{20,22},{24,26},{28,30},{32,34}... | collective-permute-start | bytes 2359304 | tf_op jit(solution)/shard_map/ppermute | solution.py:147
  32.5 31.8 %collective-permute-start = (f32[12,4,8,512]{3,2,0,1:T(8,128)}, f32[12,4,8,512]{3,2,0,1:T(8,128)}, u32[]{:S(2)}, u32[]{:S(2)}) collective-permute-start(f32[12,4,8,512]{3,2,0,1:T(8,128)} %bitcast.112), channel_id=1, source_target_pairs={{0,1},{4,5},{8,9},{12,13},{16,17},{20,21},{24,25},{28,29},{32,33},... | collective-permute-start | bytes 2359304 | tf_op jit(solution)/shard_map/ppermute | solution.py:147
  66.3 3.3 collective-permute-start.5
  67.0 2.6 collective-permute-start.4
  67.6 6.0 %collective-permute-start.3 = (f32[12,8,512]{2,1,0:T(8,128)S(1)}, f32[12,8,512]{2,1,0:T(8,128)S(1)}, u32[]{:S(2)}, u32[]{:S(2)}) collective-permute-start(f32[12,8,512]{2,1,0:T(8,128)S(1)} %get-tuple-element.24), channel_id=1, source_target_pairs={{0,32},{1,33},{2,34},{3,35},{4,36},{5,37},{6,38},{7,39},{8,40},{9,... | collective-permute-start | bytes 589832 | tf_op jit(solution)/shard_map/ppermute | solution.py:147
  78.6 16.1 %collective-permute-start.6 = (f32[6,8,512]{2,1,0:T(8,128)S(1)}, f32[6,8,512]{2,1,0:T(8,128)S(1)}, u32[]{:S(2)}, u32[]{:S(2)}) collective-permute-start(f32[6,8,512]{2,1,0:T(8,128)S(1)} %get-tuple-element.29), channel_id=1, source_target_pairs={{0,0},{1,1},{2,4},{3,5},{4,2},{5,3},{6,6},{7,7},{8,32},{9,33},{10,... | collective-permute-start | bytes 294920 | tf_op jit(solution)/shard_map/ppermute | solution.py:205
  84.5 10.2 %collective-permute-start.7 = (f32[6,8,512]{2,1,0:T(8,128)S(1)}, f32[6,8,512]{2,1,0:T(8,128)S(1)}, u32[]{:S(2)}, u32[]{:S(2)}) collective-permute-start(f32[6,8,512]{2,1,0:T(8,128)S(1)} %get-tuple-element.30), channel_id=1, source_target_pairs={{0,1},{1,0},{2,5},{3,4},{4,3},{5,2},{6,7},{7,6},{8,33},{9,32},{10,... | collective-permute-start | bytes 294920 | tf_op jit(solution)/shard_map/ppermute | solution.py:206
  88.2 15.3 %all-to-all-start.2 = ((f32[8,32,512]{2,1,0:T(8,128)}), f32[8,32,512]{2,1,0:T(8,128)S(1)}, u32[]{:S(2)}, u32[]{:S(2)}) async-start(f32[8,32,512]{2,1,0:T(8,128)} %broadcast_in_dim.78), calls=%async_computation.2 | async-start | bytes 1048576 | tf_op jit(solution)/shard_map/all_to_all | solution.py:193
  94.7 183.0 %all-gather.5.cloned.1.call-start = ((), (), s32[]{:S(2)}) async-start(), calls=%async_computation.5 | async-start | bytes 1769472 | tf_op jit(solution)/shard_map/all_gather | solution.py:208
  104.6 22.8 %all-to-all-start.3 = ((f32[16,32,512]{2,1,0:T(8,128)}), f32[16,32,512]{2,1,0:T(8,128)S(1)}, u32[]{:S(2)}, u32[]{:S(2)}) async-start(f32[16,32,512]{2,1,0:T(8,128)} %broadcast_in_dim.80), calls=%async_computation.3 | async-start | bytes 2097152 | tf_op jit(solution)/shard_map/all_to_all | solution.py:195
  112.1 3.4 %copy-start.5 = (f32[1,1024,2048]{2,1,0:T(8,128)S(1)}, f32[1,1024,2048]{2,1,0:T(8,128)}, u32[]{:S(2)}) copy-start(f32[1,1024,2048]{2,1,0:T(8,128)} %param.5) | copy-start | bytes 25165828
  127.4 163.2 %all-to-all-start = ((f32[128,128,128]{2,1,0:T(8,128)}), f32[128,128,128]{2,1,0:T(8,128)}, u32[]{:S(2)}, u32[]{:S(2)}) async-start(f32[128,128,128]{2,1,0:T(8,128)} %bitcast.119), calls=%async_computation | async-start | bytes 16777216 | tf_op jit(solution)/shard_map/all_to_all | solution.py:199
  134.4 148.7 %all-gather.3.cloned.1.call-start = ((), (), s32[]{:S(2)}) async-start(), calls=%async_computation.4 | async-start | bytes 3342336 | tf_op jit(solution)/shard_map/all_gather | solution.py:201
  233.2 41.4 %copy-start.12 = (f32[512,512]{1,0:T(8,128)}, f32[512,512]{1,0:T(8,128)S(1)}, u32[]{:S(2)}) copy-start(f32[512,512]{1,0:T(8,128)S(1)} %get-tuple-element.97) | copy-start | bytes 3145732
  274.6 4.6 %copy-start.8 = (f32[128,512]{1,0:T(8,128)}, f32[128,512]{1,0:T(8,128)S(1)}, u32[]{:S(2)}) copy-start(f32[128,512]{1,0:T(8,128)S(1)} %fusion.33) | copy-start | bytes 786436
  275.5 7.6 %copy-start.10 = (f32[128,512]{1,0:T(8,128)}, f32[128,512]{1,0:T(8,128)S(1)}, u32[]{:S(2)}) copy-start(f32[128,512]{1,0:T(8,128)S(1)} %fusion.31) | copy-start | bytes 786436
  277.6 5.5 %copy-start.14 = (f32[128,512]{1,0:T(8,128)}, f32[128,512]{1,0:T(8,128)S(1)}, u32[]{:S(2)}) copy-start(f32[128,512]{1,0:T(8,128)S(1)} %fusion.30) | copy-start | bytes 786436
  285.4 5.2 %copy-start.7 = (s32[4,12]{1,0:T(4,128)S(1)}, s32[4,12]{1,0:T(4,128)}, u32[]{:S(2)}) copy-start(s32[4,12]{1,0:T(4,128)} %broadcast_add_fusion.2.inv_row_ref) | copy-start | bytes 580
  290.6 29.4 %copy-start.3 = (f32[1536,512]{1,0:T(8,128)}, f32[1536,512]{1,0:T(8,128)S(1)}, u32[]{:S(2)}) copy-start(f32[1536,512]{1,0:T(8,128)S(1)} %fusion.11.refs_5_) | copy-start | bytes 9437188
  290.7 3.5 %copy-start.4 = (f32[1536,768]{1,0:T(8,128)S(1)}, f32[1536,768]{1,0:T(8,128)}, u32[]{:S(2)}) copy-start(f32[1536,768]{1,0:T(8,128)} %refs_4_.1) | copy-start | bytes 14155780
  295.5 24.5 %copy-start.1 = (s32[1,64,64]{2,1,0:T(8,128)S(1)}, s32[1,64,64]{2,1,0:T(8,128)}, u32[]{:S(2)}) copy-start(s32[1,64,64]{2,1,0:T(8,128)} %param.7) | copy-start | bytes 49156
  (9 other events, 16.3 us)
Sparse Core Ops, SparseCore 0:
  97.8 88.9 all-gather.4
  188.5 81.6 all-gather.2

commit v2 on v1

--- a/solution.py
+++ b/solution.py
@@ -76,18 +76,197 @@
     )(inv_row, inv_lead, recv, parent)
 
 
+KB = 4
+
+
+def factor_diagonal(get, put):
+    groups = BLK // 8
+    a = [get(g) for g in range(groups)]
+    lanes = lax.broadcasted_iota(jnp.int32, (8, BLK), 1)
+    subs = lax.broadcasted_iota(jnp.int32, (8, BLK), 0)
+    e = [jnp.where(lanes == subs + 8 * g, 1.0, 0.0).astype(jnp.float32) for g in range(groups)]
+    full = (8, BLK)
+    for j0 in range(0, BLK, KB):
+        g0, i0 = j0 // 8, j0 % 8
+        head = [jnp.broadcast_to(a[g0][:, j0 + k : j0 + k + 1], full) for k in range(KB)]
+        small = [[None] * KB for _ in range(KB)]
+        for i in range(KB):
+            for k in range(i + 1):
+                small[i][k] = jnp.broadcast_to(head[k][i0 + i : i0 + i + 1, :], full)
+        inv = [None] * KB
+        low = [[None] * KB for _ in range(KB)]
+        for k in range(KB):
+            root = lax.rsqrt(small[k][k])
+            inv[k] = root * (1.5 - 0.5 * small[k][k] * root * root)
+            for i in range(k + 1, KB):
+                low[i][k] = small[i][k] * inv[k]
+            for i in range(k + 1, KB):
+                for m in range(k + 1, i + 1):
+                    small[i][m] = small[i][m] - low[i][k] * low[m][k]
+        u, w = [], []
+        for k in range(KB):
+            r = jnp.broadcast_to(a[g0][i0 + k : i0 + k + 1, :], full)
+            s = jnp.broadcast_to(e[g0][i0 + k : i0 + k + 1, :], full)
+            for m in range(k):
+                r = r - low[k][m] * u[m]
+                s = s - low[k][m] * w[m]
+            u.append(r * inv[k])
+            w.append(s * inv[k])
+        for g in range(g0, groups):
+            if g == g0 and i0 + KB == 8:
+                pass
+            else:
+                mult = []
+                for k in range(KB):
+                    c = head[k] if g == g0 else jnp.broadcast_to(a[g][:, j0 + k : j0 + k + 1], full)
+                    for m in range(k):
+                        c = c - mult[m] * low[k][m]
+                    mult.append(c * inv[k])
+                if g == g0:
+                    mult = [jnp.where(subs >= i0 + KB, c, 0.0) for c in mult]
+                for k in range(KB):
+                    a[g] = a[g] - mult[k] * u[k]
+                    e[g] = e[g] - mult[k] * w[k]
+            if g == g0:
+                for k in range(KB):
+                    e[g] = jnp.where(subs == i0 + k, w[k], e[g])
+        if i0 + KB == 8:
+            put(g0, e[g0])
+
+
+def factor_kernel(place_ref, *refs):
+    pieces = refs[:COLS]
+    w_ref, m_ref, d_ref = refs[COLS:]
+    for other in range(COLS):
+        for slot in range(FRONTS):
+            source = place_ref[1] ^ (slot * COLS + other)
+            for block in range(WB):
+                start = pl.multiple_of(block * BLK + source * 8, 8)
+                m_ref[pl.ds(start, 8), :W] = pieces[other][slot, block]
+    lanes = lax.broadcasted_iota(jnp.int32, (BLK, BLK), 1)
+    subs = lax.broadcasted_iota(jnp.int32, (BLK, BLK), 0)
+    eye = jnp.where(lanes == subs, 1.0, 0.0).astype(jnp.float32)
+    m_ref[:, W:] = jnp.zeros((W, W), jnp.float32)
+    for block in range(W // BLK):
+        m_ref[block * BLK : (block + 1) * BLK, W + block * BLK : W + (block + 1) * BLK] = eye
+
+    def step(block, carry):
+        base = pl.multiple_of(block * BLK, BLK)
+
+        def get(g):
+            return m_ref[pl.ds(pl.multiple_of(base + g * 8, 8), 8), pl.ds(base, BLK)]
+
+        def put(g, value):
+            d_ref[g * 8 : (g + 1) * 8, :] = value
+
+        factor_diagonal(get, put)
+        rows = jnp.dot(
+            d_ref[...], m_ref[pl.ds(base, BLK), :], precision=HIGHEST, preferred_element_type=jnp.float32
+        )
+        m_ref[pl.ds(base, BLK), :] = rows
+
+        @pl.when(block < W // BLK - 1)
+        def _():
+            column = lax.broadcasted_iota(jnp.int32, (BLK, W), 1)
+            later = jnp.where(column >= base + BLK, rows[:, :W], 0.0)
+            m_ref[...] = m_ref[...] - lax.dot_general(
+                later, rows, (((0,), (0,)), ((), ())), precision=HIGHEST, preferred_element_type=jnp.float32
+            )
+
+        return carry
+
+    lax.fori_loop(0, W // BLK, step, 0)
+    w_ref[...] = m_ref[:, W:]
+
+
+def factor_inverse(place, pieces):
+    vmem = pl.BlockSpec(memory_space=pltpu.VMEM)
+    return pl.pallas_call(
+        factor_kernel,
+        name="factor",
+        in_specs=[pl.BlockSpec(memory_space=pltpu.SMEM)] + [vmem] * COLS,
+        out_specs=vmem,
+        out_shape=jax.ShapeDtypeStruct((W, W), jnp.float32),
+        scratch_shapes=[pltpu.VMEM((W, 2 * W), jnp.float32), pltpu.VMEM((BLK, BLK), jnp.float32)],
+        compiler_params=pltpu.CompilerParams(vmem_limit_bytes=40 << 20),
+    )(place, *pieces)
+
+
+def panel_kernel(place_ref, rows_ref, *refs):
+    cols = refs[:4]
+    inverse_ref, panel_ref, high_ref, low_ref, block_ref = refs[4:]
+    step = pl.program_id(0)
+
+    def times_inverse(x):
+        return lax.dot_general(
+            x,
+            inverse_ref[...],
+            (((1,), (1,)), ((), ())),
+            precision=HIGHEST,
+            preferred_element_type=jnp.float32,
+        )
+
+    @pl.when(step < PR)
+    def _():
+        panel_ref[...] = times_inverse(rows_ref[:, 0].reshape(BLK, W))
+
+    @pl.when(step >= PR)
+    def _():
+        for other in range(4):
+            for slot in range(2):
+                source = place_ref[0] ^ (slot * 4 + other)
+                start = pl.multiple_of(source * 16, 16)
+                block_ref[pl.ds(start, 16), :] = cols[other][slot, 0]
+        value = times_inverse(block_ref[...])
+        high = value.astype(jnp.bfloat16)
+        high_ref[...] = high
+        low_ref[...] = (value - high.astype(jnp.float32)).astype(jnp.bfloat16)
+
+
+def make_panels(place, rows_raw, cols_raw, inverse):
+    def in_rows(i):
+        return jnp.minimum(i, PR - 1)
+
+    def in_cols(i):
+        return jnp.maximum(i - PR, 0)
+
+    half = jax.ShapeDtypeStruct((PC * BLK, W), jnp.bfloat16)
+    return pl.pallas_call(
+        panel_kernel,
+        name="panels",
+        grid_spec=pltpu.PrefetchScalarGridSpec(
+            num_scalar_prefetch=1,
+            grid=(PR + PC,),
+            in_specs=[pl.BlockSpec((GROUPS, 1, 8, W), lambda i, p: (0, in_rows(i), 0, 0))]
+            + [pl.BlockSpec((2, 1, 16, W), lambda i, p: (0, in_cols(i), 0, 0))] * 4
+            + [pl.BlockSpec((W, W), lambda i, p: (0, 0))],
+            out_specs=[
+                pl.BlockSpec((BLK, W), lambda i, p: (in_rows(i), 0)),
+                pl.BlockSpec((BLK, W), lambda i, p: (in_cols(i), 0)),
+                pl.BlockSpec((BLK, W), lambda i, p: (in_cols(i), 0)),
+            ],
+            scratch_shapes=[pltpu.VMEM((BLK, W), jnp.float32)],
+        ),
+        out_shape=[jax.ShapeDtypeStruct((PR * BLK, W), jnp.float32), half, half],
+        compiler_params=pltpu.CompilerParams(vmem_limit_bytes=32 << 20),
+    )(place, rows_raw, *cols_raw, inverse)
+
+
 def final_kernel(inv_row_ref, inv_col_ref, lead_ref, *refs):
     recvs = refs[:FRONTS]
-    parent_ref, panel_ref, across_ref, o_ref = refs[FRONTS:]
+    parent_ref, panel_ref, high_ref, low_ref, o_ref = refs[FRONTS:]
     a = pl.program_id(0)
-    product = lax.dot_general(
-        panel_ref[...],
-        across_ref[...],
-        (((1,), (1,)), ((), ())),
-        precision=HIGHEST,
-        preferred_element_type=jnp.float32,
-    )
-    o_ref[...] = parent_ref[...] - product
+    panel = panel_ref[...]
+    panel_high = panel.astype(jnp.bfloat16)
+    panel_low = (panel - panel_high.astype(jnp.float32)).astype(jnp.bfloat16)
+
+    def product(x, y):
+        return lax.dot_general(
+            x, y, (((1,), (1,)), ((), ())), preferred_element_type=jnp.float32
+        )
+
+    total = product(panel_high, low_ref[...]) + product(panel_low, high_ref[...])
+    o_ref[...] = parent_ref[...] - (total + product(panel_high, high_ref[...]))
     for b in range(PC):
         span = slice(b * BLK, (b + 1) * BLK)
         total = o_ref[:, span]
@@ -108,10 +287,11 @@
         o_ref[:, :W] = jnp.zeros((BLK, W), jnp.float32)
 
 
-def finish(inv_row, inv_col, lead, recv, parent, panel, across):
+def finish(inv_row, inv_col, lead, recv, parent, panel, high, low):
     def recv_map(front):
         return lambda a, ir, ic, ld: (front * ROWS + jnp.maximum(ir[front, a], 0), 0, 0)
 
+    whole = pl.BlockSpec((PC * BLK, W), lambda a, *_: (0, 0))
     return pl.pallas_call(
         final_kernel,
         name="finish",
@@ -124,13 +304,14 @@
             + [
                 pl.BlockSpec((BLK, PC * BLK), lambda a, *_: (a, 0)),
                 pl.BlockSpec((BLK, W), lambda a, *_: (a, 0)),
-                pl.BlockSpec((PC * BLK, W), lambda a, *_: (0, 0)),
+                whole,
+                whole,
             ],
             out_specs=pl.BlockSpec((BLK, PC * BLK), lambda a, *_: (a, 0)),
         ),
         out_shape=jax.ShapeDtypeStruct((PR * BLK, PC * BLK), jnp.float32),
         compiler_params=pltpu.CompilerParams(vmem_limit_bytes=40 << 20),
-    )(inv_row, inv_col, lead, recv, recv, recv, recv, parent, panel, across)
+    )(inv_row, inv_col, lead, recv, recv, recv, recv, parent, panel, high, low)
 
 
 def inverse_places(places, length):
@@ -146,6 +327,11 @@
     for k in range(1, lax.axis_size(axis)):
         total = total + lax.ppermute(parts(x, k), axis, [(0, k)])
     return total
+
+
+def flipped(x, axis, bits):
+    size = lax.axis_size(axis)
+    return lax.ppermute(x, axis, [(i, i ^ bits) for i in range(size)])
 
 
 def swap_pairs(flip):
@@ -189,31 +375,35 @@
 
     slices = assemble_slices(inv_row, inv_lead, lead_recv, first)
 
-    corner = jnp.broadcast_to(slices[:WB].reshape(1, WB * 8, W), (ROWS, WB * 8, W))
-    corner = lax.all_to_all(corner, "row", 0, 0, tiled=True)[0]
-    corner = jnp.broadcast_to(corner[None], (GROUPS, WB * 8, W))
-    corner = lax.all_to_all(corner, GRP, 0, 0, tiled=True)
-    corner = corner.reshape(GROUPS, WB, 8, W).transpose(1, 0, 2, 3).reshape(W, W)
+    corner = slices[:WB]
+    near = jnp.where(row == 0, corner, 0.0)
+    for k in range(1, 4):
+        near = near + lax.ppermute(corner, "row", [(0, k)])
+    far = lax.ppermute(near, "row", [(k, 4 + k) for k in range(4)])
+    corner = jnp.where(row < 4, near, far)
+    corner = jnp.stack([corner, flipped(corner, "front", 1)])
+    corner = jnp.concatenate([corner, flipped(corner, "front", 2)])
+    pieces = [corner] + [flipped(corner, "col", bits) for bits in range(1, COLS)]
+    place = jnp.stack([row, group]).astype(jnp.int32)
+    inverse = factor_inverse(place, pieces)
 
     packed = pack(window, local).reshape(128, BLK, BLK)
     recv = lax.all_to_all(packed, ALL, 0, 0, tiled=True)
 
     rows_raw = lax.all_gather(slices.reshape(PR * 8, W), GRP, axis=0, tiled=True)
-    rows_raw = rows_raw.reshape(GROUPS, PR, 8, W).transpose(1, 0, 2, 3).reshape(PR * BLK, W)
+    rows_raw = rows_raw.reshape(GROUPS, PR, 8, W)
 
     even = group % 2 == 0
     one = lax.ppermute(jnp.where(even, slices[:PC], slices[PC:]), ALL, swap_pairs(0))
     two = lax.ppermute(jnp.where(even, slices[PC:], slices[:PC]), ALL, swap_pairs(1))
     mine = jnp.stack([jnp.where(even, one, two), jnp.where(even, two, one)], axis=1)
-    cols_raw = lax.all_gather(mine.reshape(PC * 16, W), "row", axis=0, tiled=True)
-    cols_raw = cols_raw.reshape(ROWS, PC, 16, W).transpose(1, 0, 2, 3).reshape(PC * BLK, W)
-
-    factor = jnp.linalg.cholesky(corner)
-    inverse = jax.scipy.linalg.solve_triangular(factor, jnp.eye(W, dtype=jnp.float32), lower=True)
-    panel = jnp.dot(rows_raw, inverse.T, precision=HIGHEST)
-    across = jnp.dot(cols_raw, inverse.T, precision=HIGHEST)
+    mine = mine.reshape(PC, 16, W)
+    mine = jnp.stack([mine, flipped(mine, "row", 4)])
+    cols_raw = [mine] + [flipped(mine, "row", bits) for bits in range(1, 4)]
+
+    panel, high, low = make_panels(place, rows_raw, cols_raw, inverse)
     lead_flags = jnp.stack([row == 0, group == 0]).astype(jnp.int32)
-    schur = finish(inv_row, inv_col, lead_flags, recv, parent_entries, panel, across)
+    schur = finish(inv_row, inv_col, lead_flags, recv, parent_entries, panel, high, low)
     return schur, panel
 
 

time: 332 us -> 333 us (level)
  other arithmetic: 126 us -> 7.34 us
  waiting for transfers between devices: 47.2 us -> 141 us
  Pallas kernels: 28.8 us -> 78 us
  matrix products: 19.3 us -> 0 us
  starting transfers between devices: 53.7 us -> 67.3 us
  local copies, waits for them, and re-layouts: 34.7 us -> 22.8 us
    another operation x17 -> x4, other arithmetic: 118 us -> 0.15 us  [the longest x1 0.07 us: body(): place = jnp.stack([row, group]).astype(jnp.int32)]
    ppermute x6, waiting for transfers between devices: 32.4 us -> 117 us  [scatter_from_first(): total = total + lax.ppermute(parts(x, k), axis, [(0, k)])]
    pallas_call x0 -> x2, Pallas kernels: none -> 57.5 us  [the longest x1 34 us: factor_inverse(): pl.pallas_call(factor_kernel, name='factor', in_specs=[pl.BlockSpec(memor...]
    ppermute x0 -> x13, starting transfers between devices: none -> 30 us  [the longest x9 21.4 us: flipped(): return lax.ppermute(x, axis, [(i, i ^ bits) for i in range(size)])]
    ppermute x0 -> x13, waiting for transfers between devices: none -> 19.7 us  [the longest x9 16.7 us: flipped(): return lax.ppermute(x, axis, [(i, i ^ bits) for i in range(size)])]
    all_to_all x2 -> x0, waiting for transfers between devices: 14.7 us -> none  [the longest x1 7.96 us: body(): corner = lax.all_to_all(corner, 'row', 0, 0, tiled=True)[0]]
    all_to_all x2 -> x0, starting transfers between devices: 14 us -> none  [the longest x1 7.53 us: body(): corner = lax.all_to_all(corner, GRP, 0, 0, tiled=True)]
    another operation x13 -> x0, matrix products: 10.3 us -> none  [the longest x6 5.48 us: body(): factor = jnp.linalg.cholesky(corner)]
  transfers between devices with their start and end apart: 14 -> 24, of which waited for: 6 -> 11; matrix products, arithmetic and copies ran while one was open for 49% -> 3% of each run, Pallas kernels for 1% -> 19%
where the time goes in v2:
time: 333 us; the launch traced here: 331 us
  waiting for transfers between devices  141 us (42%)
  Pallas kernels  78 us (23%)
  starting transfers between devices  67.3 us (20%)
  local copies, waits for them, and re-layouts  22.8 us (7%)
  between operations  14.3 us (4%)
  other arithmetic  7.34 us (2%)
    ppermute x6, waiting for transfers between devices, scatter_from_first(): total = total + lax.ppermute(parts(x, k), axis, [(0, k)])  117 us
    pallas_call x1, Pallas kernels, factor_inverse(): pl.pallas_call(factor_kernel, name='factor', in_specs=[pl.BlockSpec(memor...  34 us
    pallas_call x1, Pallas kernels, make_panels(): pl.pallas_call(panel_kernel, name='panels', grid_spec=pltpu.PrefetchScala...  23.6 us
    ppermute x9, starting transfers between devices, flipped(): return lax.ppermute(x, axis, [(i, i ^ bits) for i in range(size)])  21.4 us
    unnamed x34, local copies, waits for them, and re-layouts  17.5 us
    ppermute x9, waiting for transfers between devices, flipped(): return lax.ppermute(x, axis, [(i, i ^ bits) for i in range(size)])  16.7 us
    pallas_call x1, Pallas kernels, finish(): pl.pallas_call(final_kernel, name='finish', grid_spec=pltpu.PrefetchScala...  16.1 us
    ppermute x6, starting transfers between devices, scatter_from_first(): total = total + lax.ppermute(parts(x, k), axis, [(0, k)])  13.2 us
  transfers between devices with their start and end apart: 24, of which 11 were waited for; matrix products, arithmetic and copies ran while one was open for 3% of the time, Pallas kernels for 19%

profile of v2, /device:TPU:1, one launch (start us, length us, event | category | flops | bytes accessed | tf_op | source)
XLA Modules:
  0.0 331.1 jit_solution(14439067376895552790)
XLA Ops:
  9.4 11.5 %all-to-all-start.1 = ((f32[128,8,128]{2,1,0:T(8,128)}), f32[128,8,128]{2,1,0:T(8,128)S(1)}, u32[]{:S(2)}, u32[]{:S(2)}) async-start(f32[128,8,128]{2,1,0:T(8,128)} %bitcast.12), calls=%async_computation.1 | async-start | bytes 1048576 | tf_op jit(solution)/shard_map/all_to_all | solution.py:361
  20.9 3.4 %copy-done.3 = f32[1,1024,2048]{2,1,0:T(8,128)S(1)} copy-done((f32[1,1024,2048]{2,1,0:T(8,128)S(1)}, f32[1,1024,2048]{2,1,0:T(8,128)}, u32[]{:S(2)}) %copy-start.3) | copy-done | bytes 8388632
  26.2 3.2 copy-done.1
  29.4 5.0 %all-to-all-done.1.recv_ref = f32[128,8,128]{2,1,0:T(8,128)S(1)} async-done(((f32[128,8,128]{2,1,0:T(8,128)}), f32[128,8,128]{2,1,0:T(8,128)S(1)}, u32[]{:S(2)}, u32[]{:S(2)}) %all-to-all-start.1) | async-done | bytes 524320 | tf_op jit(solution)/shard_map/all_to_all | solution.py:361
  35.2 5.3 %all-to-all-start = ((f32[128,128,128]{2,1,0:T(8,128)}), f32[128,128,128]{2,1,0:T(8,128)}, u32[]{:S(2)}, u32[]{:S(2)}) async-start(f32[128,128,128]{2,1,0:T(8,128)} %bitcast.61), calls=%async_computation | async-start | bytes 16777216 | tf_op jit(solution)/shard_map/all_to_all | solution.py:391
  43.6 6.2 %collective-permute-start.2 = (f32[12,4,8,512]{3,2,0,1:T(8,128)S(1)}, f32[12,4,8,512]{3,2,0,1:T(8,128)}, u32[]{:S(2)}, u32[]{:S(2)}) collective-permute-start(f32[12,4,8,512]{3,2,0,1:T(8,128)S(1)} %bitcast.68), channel_id=1, source_target_pairs={{0,3},{4,7},{8,11},{12,15},{16,19},{20,23},{24,27},{28,31},{32,35}... | collective-permute-start | bytes 2359304 | tf_op jit(solution)/shard_map/ppermute | solution.py:328
  55.6 90.9 %collective-permute-done.2 = f32[12,4,8,512]{3,2,0,1:T(8,128)} collective-permute-done((f32[12,4,8,512]{3,2,0,1:T(8,128)S(1)}, f32[12,4,8,512]{3,2,0,1:T(8,128)}, u32[]{:S(2)}, u32[]{:S(2)}) %collective-permute-start.2) | collective-permute-done | bytes 786464 | tf_op jit(solution)/shard_map/ppermute | solution.py:328
  146.5 3.5 %collective-permute-done.1 = f32[12,4,8,512]{3,2,0,1:T(8,128)} collective-permute-done((f32[12,4,8,512]{3,2,0,1:T(8,128)S(1)}, f32[12,4,8,512]{3,2,0,1:T(8,128)}, u32[]{:S(2)}, u32[]{:S(2)}) %collective-permute-start.1) | collective-permute-done | bytes 786464 | tf_op jit(solution)/shard_map/ppermute | solution.py:328
  150.0 16.9 %collective-permute-done = f32[12,4,8,512]{3,2,0,1:T(8,128)} collective-permute-done((f32[12,4,8,512]{3,2,0,1:T(8,128)S(1)}, f32[12,4,8,512]{3,2,0,1:T(8,128)}, u32[]{:S(2)}, u32[]{:S(2)}) %collective-permute-start) | collective-permute-done | bytes 786464 | tf_op jit(solution)/shard_map/ppermute | solution.py:328
  172.1 5.2 %collective-permute-done.3 = f32[12,8,512]{2,1,0:T(8,128)S(1)} collective-permute-done((f32[12,8,512]{2,1,0:T(8,128)S(1)}, f32[12,8,512]{2,1,0:T(8,128)S(1)}, u32[]{:S(2)}, u32[]{:S(2)}) %collective-permute-start.3) | collective-permute-done | bytes 196640 | tf_op jit(solution)/shard_map/ppermute | solution.py:328
  181.3 4.7 %collective-permute-start.14 = (f32[4,8,512]{2,1,0:T(8,128)S(1)}, f32[4,8,512]{2,1,0:T(8,128)S(1)}, u32[]{:S(2)}, u32[]{:S(2)}) collective-permute-start(f32[4,8,512]{2,1,0:T(8,128)S(1)} %slice.74), channel_id=1, source_target_pairs={{0,12},{1,13},{2,14},{3,15},{32,44},{33,45},{34,46},{35,47},{64,76... | collective-permute-start | bytes 196616 | tf_op jit(solution)/shard_map/ppermute | solution.py:381
  194.0 2.8 collective-permute-start.16
  197.7 4.1 %collective-permute-start.6 = (f32[6,8,512]{2,1,0:T(8,128)S(1)}, f32[6,8,512]{2,1,0:T(8,128)S(1)}, u32[]{:S(2)}, u32[]{:S(2)}) collective-permute-start(f32[6,8,512]{2,1,0:T(8,128)S(1)} %get-tuple-element.19), channel_id=1, source_target_pairs={{0,0},{1,1},{2,4},{3,5},{4,2},{5,3},{6,6},{7,7},{8,32},{9,33},{10,... | collective-permute-start | bytes 294920 | tf_op jit(solution)/shard_map/ppermute | solution.py:397
  201.8 3.2 collective-permute-start.7
  205.0 3.2 collective-permute-start.17
  208.5 5.7 %collective-permute-start.8 = (f32[6,16,512]{2,1,0:T(8,128)S(1)}, f32[6,16,512]{2,1,0:T(8,128)S(1)}, u32[]{:S(2)}, u32[]{:S(2)}) collective-permute-start(f32[6,16,512]{2,1,0:T(8,128)S(1)} %get-tuple-element.16), channel_id=1, source_target_pairs={{0,16},{4,20},{8,24},{12,28},{16,0},{20,4},{24,8},{28,12},{1,17},{... | collective-permute-start | bytes 589832 | tf_op jit(solution)/shard_map/ppermute | solution.py:334
  216.4 3.9 %collective-permute-done.8 = f32[6,16,512]{2,1,0:T(8,128)S(1)} collective-permute-done((f32[6,16,512]{2,1,0:T(8,128)S(1)}, f32[6,16,512]{2,1,0:T(8,128)S(1)}, u32[]{:S(2)}, u32[]{:S(2)}) %collective-permute-start.8) | collective-permute-done | bytes 196640 | tf_op jit(solution)/shard_map/ppermute | solution.py:334
  220.4 3.5 %collective-permute-start.9 = (f32[2,6,16,512]{3,2,1,0:T(8,128)S(1)}, f32[2,6,16,512]{3,2,1,0:T(8,128)S(1)}, u32[]{:S(2)}, u32[]{:S(2)}) collective-permute-start(f32[2,6,16,512]{3,2,1,0:T(8,128)S(1)} %pad_maximum_fusion.refs_0_), channel_id=1, source_target_pairs={{0,4},{4,0},{8,12},{12,8},{16,20},{20,16},{24,28},{28,24},{1,5},{5... | collective-permute-start | bytes 1179656 | tf_op jit(solution)/shard_map/ppermute | solution.py:334
  223.8 2.5 collective-permute-start.11
  228.2 8.1 %collective-permute-done.19.refs_2_ = f32[4,4,8,512]{3,2,1,0:T(8,128)S(1)} collective-permute-done((f32[4,4,8,512]{3,2,1,0:T(8,128)S(1)}, f32[4,4,8,512]{3,2,1,0:T(8,128)S(1)}, u32[]{:S(2)}, u32[]{:S(2)}) %collective-permute-start.19) | collective-permute-done | bytes 262176 | tf_op jit(solution)/shard_map/ppermute | solution.py:334
  236.3 4.6 %collective-permute-done.20.refs_3_ = f32[4,4,8,512]{3,2,1,0:T(8,128)S(1)} collective-permute-done((f32[4,4,8,512]{3,2,1,0:T(8,128)S(1)}, f32[4,4,8,512]{3,2,1,0:T(8,128)S(1)}, u32[]{:S(2)}, u32[]{:S(2)}) %collective-permute-start.20) | collective-permute-done | bytes 262176 | tf_op jit(solution)/shard_map/ppermute | solution.py:334
  241.0 34.0 %factor.1.refs_4_ = f32[512,512]{1,0:T(8,128)S(1)} custom-call(s32[2]{0:T(128)S(1)} %pad_add_fusion.place_ref, f32[4,4,8,512]{3,2,1,0:T(8,128)S(1)} %pad_maximum_fusion.1.refs_0_, f32[4,4,8,512]{3,2,1,0:T(8,128)S(1)} %collective-permute-done.18.refs_1_, f32[4,4,8,512]{3,2,1,0:T(8,128)S(1)} %collective-permute-done.19.refs_2_, ...), custom_call_target="tpu_custom_call" | custom-call | tf_op jit(solution)/shard_map/factor/pallas_call | solution.py:184
  280.4 23.6 %panels.1 = (f32[1536,512]{1,0:T(8,128)}, bf16[768,512]{1,0:T(8,128)(2,1)S(1)}, bf16[768,512]{1,0:T(8,128)(2,1)S(1)}) custom-call(s32[2]{0:T(128)S(1)} %pad_add_fusion.place_ref, f32[16,12,8,512]{3,2,1,0:T(8,128)S(1)} %bitcast.65, f32[2,6,16,512]{3,2,1,0:T(8,128)S(1)} %pad_maximum_fusion.refs_0_, f32[2,6,16,512]{3,2,1,0:T(8,128)S(1)} %collective-permute-done.9.refs_1_, ...), custom_call_target="tpu_custom_call" | custom-call | tf_op jit(solution)/shard_map/panels/pallas_call | solution.py:234
  308.2 16.1 %finish.1 = f32[1536,768]{1,0:T(8,128)} custom-call(s32[4,12]{1,0:T(4,128)S(1)} %copy-done.10, s32[4,6]{1,0:T(4,128)S(1)} %broadcast_add_fusion.1.inv_col_ref, s32[2]{0:T(128)S(1)} %add_convert_fusion.lead_ref, f32[128,128,128]{2,1,0:T(8,128)} %all-to-all-done.refs_0_.refs_1_.refs_2_.refs_3_, f32[128,128,128]{2,1,0:T(8,128)} %all-to-all-done.refs_0_.refs_1_.refs_2_.refs_3_, ...), custom_call_target="tpu_custom_call" | custom-call | tf_op jit(solution)/shard_map/finish/pallas_call | solution.py:295
  (98 shorter events, 45.9 us)
Async XLA Ops:
  9.4 25.0 %all-to-all-start.1 = ((f32[128,8,128]{2,1,0:T(8,128)}), f32[128,8,128]{2,1,0:T(8,128)S(1)}, u32[]{:S(2)}, u32[]{:S(2)}) async-start(f32[128,8,128]{2,1,0:T(8,128)} %bitcast.12), calls=%async_computation.1 | async-start | bytes 1048576 | tf_op jit(solution)/shard_map/all_to_all | solution.py:361
  35.2 268.8 %all-to-all-start = ((f32[128,128,128]{2,1,0:T(8,128)}), f32[128,128,128]{2,1,0:T(8,128)}, u32[]{:S(2)}, u32[]{:S(2)}) async-start(f32[128,128,128]{2,1,0:T(8,128)} %bitcast.61), calls=%async_computation | async-start | bytes 16777216 | tf_op jit(solution)/shard_map/all_to_all | solution.py:391
  40.5 236.0 %all-gather.2.cloned.1.call-start = ((), (), s32[]{:S(2)}) async-start(), calls=%async_computation.2 | async-start | bytes 3342336 | tf_op jit(solution)/shard_map/all_gather | solution.py:393
  43.6 102.9 %collective-permute-start.2 = (f32[12,4,8,512]{3,2,0,1:T(8,128)S(1)}, f32[12,4,8,512]{3,2,0,1:T(8,128)}, u32[]{:S(2)}, u32[]{:S(2)}) collective-permute-start(f32[12,4,8,512]{3,2,0,1:T(8,128)S(1)} %bitcast.68), channel_id=1, source_target_pairs={{0,3},{4,7},{8,11},{12,15},{16,19},{20,23},{24,27},{28,31},{32,35}... | collective-permute-start | bytes 2359304 | tf_op jit(solution)/shard_map/ppermute | solution.py:328
  49.8 100.2 %collective-permute-start.1 = (f32[12,4,8,512]{3,2,0,1:T(8,128)S(1)}, f32[12,4,8,512]{3,2,0,1:T(8,128)}, u32[]{:S(2)}, u32[]{:S(2)}) collective-permute-start(f32[12,4,8,512]{3,2,0,1:T(8,128)S(1)} %bitcast.69), channel_id=1, source_target_pairs={{0,2},{4,6},{8,10},{12,14},{16,18},{20,22},{24,26},{28,30},{32,34}... | collective-permute-start | bytes 2359304 | tf_op jit(solution)/shard_map/ppermute | solution.py:328
  52.1 114.7 %collective-permute-start = (f32[12,4,8,512]{3,2,0,1:T(8,128)S(1)}, f32[12,4,8,512]{3,2,0,1:T(8,128)}, u32[]{:S(2)}, u32[]{:S(2)}) collective-permute-start(f32[12,4,8,512]{3,2,0,1:T(8,128)S(1)} %bitcast.70), channel_id=1, source_target_pairs={{0,1},{4,5},{8,9},{12,13},{16,17},{20,21},{24,25},{28,29},{32,33},... | collective-permute-start | bytes 2359304 | tf_op jit(solution)/shard_map/ppermute | solution.py:328
  168.8 3.2 collective-permute-start.5
  169.5 2.6 collective-permute-start.4
  170.2 7.1 %collective-permute-start.3 = (f32[12,8,512]{2,1,0:T(8,128)S(1)}, f32[12,8,512]{2,1,0:T(8,128)S(1)}, u32[]{:S(2)}, u32[]{:S(2)}) collective-permute-start(f32[12,8,512]{2,1,0:T(8,128)S(1)} %get-tuple-element.12), channel_id=1, source_target_pairs={{0,32},{1,33},{2,34},{3,35},{4,36},{5,37},{6,38},{7,39},{8,40},{9,... | collective-permute-start | bytes 589832 | tf_op jit(solution)/shard_map/ppermute | solution.py:328
  181.3 7.5 %collective-permute-start.14 = (f32[4,8,512]{2,1,0:T(8,128)S(1)}, f32[4,8,512]{2,1,0:T(8,128)S(1)}, u32[]{:S(2)}, u32[]{:S(2)}) collective-permute-start(f32[4,8,512]{2,1,0:T(8,128)S(1)} %slice.74), channel_id=1, source_target_pairs={{0,12},{1,13},{2,14},{3,15},{32,44},{33,45},{34,46},{35,47},{64,76... | collective-permute-start | bytes 196616 | tf_op jit(solution)/shard_map/ppermute | solution.py:381
  186.1 2.7 collective-permute-start.13
  187.4 2.6 collective-permute-start.12
  190.9 3.1 collective-permute-start.15
  194.0 11.0 %collective-permute-start.16 = (f32[4,8,512]{2,1,0:T(8,128)S(1)}, f32[4,8,512]{2,1,0:T(8,128)S(1)}, u32[]{:S(2)}, u32[]{:S(2)}) collective-permute-start(f32[4,8,512]{2,1,0:T(8,128)S(1)} %broadcast_select_fusion), channel_id=1, source_target_pairs={{0,32},{32,0},{64,96},{96,64},{1,33},{33,1},{65,97},{97,65},{2,34}... | collective-permute-start | bytes 196616 | tf_op jit(solution)/shard_map/ppermute | solution.py:334
  197.7 10.5 %collective-permute-start.6 = (f32[6,8,512]{2,1,0:T(8,128)S(1)}, f32[6,8,512]{2,1,0:T(8,128)S(1)}, u32[]{:S(2)}, u32[]{:S(2)}) collective-permute-start(f32[6,8,512]{2,1,0:T(8,128)S(1)} %get-tuple-element.19), channel_id=1, source_target_pairs={{0,0},{1,1},{2,4},{3,5},{4,2},{5,3},{6,6},{7,7},{8,32},{9,33},{10,... | collective-permute-start | bytes 294920 | tf_op jit(solution)/shard_map/ppermute | solution.py:397
  201.8 6.6 %collective-permute-start.7 = (f32[6,8,512]{2,1,0:T(8,128)S(1)}, f32[6,8,512]{2,1,0:T(8,128)S(1)}, u32[]{:S(2)}, u32[]{:S(2)}) collective-permute-start(f32[6,8,512]{2,1,0:T(8,128)S(1)} %get-tuple-element.20), channel_id=1, source_target_pairs={{0,1},{1,0},{2,5},{3,4},{4,3},{5,2},{6,7},{7,6},{8,33},{9,32},{10,... | collective-permute-start | bytes 294920 | tf_op jit(solution)/shard_map/ppermute | solution.py:398
  205.0 9.2 %collective-permute-start.17 = (f32[2,4,8,512]{3,2,1,0:T(8,128)S(1)}, f32[2,4,8,512]{3,2,1,0:T(8,128)S(1)}, u32[]{:S(2)}, u32[]{:S(2)}) collective-permute-start(f32[2,4,8,512]{3,2,1,0:T(8,128)S(1)} %pad_maximum_fusion.3), channel_id=1, source_target_pairs={{0,64},{32,96},{64,0},{96,32},{1,65},{33,97},{65,1},{97,33},{2,66}... | collective-permute-start | bytes 393224 | tf_op jit(solution)/shard_map/ppermute | solution.py:334
  208.5 11.8 %collective-permute-start.8 = (f32[6,16,512]{2,1,0:T(8,128)S(1)}, f32[6,16,512]{2,1,0:T(8,128)S(1)}, u32[]{:S(2)}, u32[]{:S(2)}) collective-permute-start(f32[6,16,512]{2,1,0:T(8,128)S(1)} %get-tuple-element.16), channel_id=1, source_target_pairs={{0,16},{4,20},{8,24},{12,28},{16,0},{20,4},{24,8},{28,12},{1,17},{... | collective-permute-start | bytes 589832 | tf_op jit(solution)/shard_map/ppermute | solution.py:334
  214.2 12.2 %collective-permute-start.18 = (f32[4,4,8,512]{3,2,1,0:T(8,128)S(1)}, f32[4,4,8,512]{3,2,1,0:T(8,128)S(1)}, u32[]{:S(2)}, u32[]{:S(2)}) collective-permute-start(f32[4,4,8,512]{3,2,1,0:T(8,128)S(1)} %pad_maximum_fusion.1.refs_0_), channel_id=1, source_target_pairs={{0,1},{1,0},{2,3},{3,2},{4,5},{5,4},{6,7},{7,6},{8,9},{9,8},{10,11... | collective-permute-start | bytes 786440 | tf_op jit(solution)/shard_map/ppermute | solution.py:334
  220.4 54.6 %collective-permute-start.9 = (f32[2,6,16,512]{3,2,1,0:T(8,128)S(1)}, f32[2,6,16,512]{3,2,1,0:T(8,128)S(1)}, u32[]{:S(2)}, u32[]{:S(2)}) collective-permute-start(f32[2,6,16,512]{3,2,1,0:T(8,128)S(1)} %pad_maximum_fusion.refs_0_), channel_id=1, source_target_pairs={{0,4},{4,0},{8,12},{12,8},{16,20},{20,16},{24,28},{28,24},{1,5},{5... | collective-permute-start | bytes 1179656 | tf_op jit(solution)/shard_map/ppermute | solution.py:334
  223.8 51.1 %collective-permute-start.10 = (f32[2,6,16,512]{3,2,1,0:T(8,128)S(1)}, f32[2,6,16,512]{3,2,1,0:T(8,128)S(1)}, u32[]{:S(2)}, u32[]{:S(2)}) collective-permute-start(f32[2,6,16,512]{3,2,1,0:T(8,128)S(1)} %pad_maximum_fusion.refs_0_), channel_id=1, source_target_pairs={{0,8},{4,12},{8,0},{12,4},{16,24},{20,28},{24,16},{28,20},{1,9},{5... | collective-permute-start | bytes 1179656 | tf_op jit(solution)/shard_map/ppermute | solution.py:334
  223.8 51.9 %collective-permute-start.11 = (f32[2,6,16,512]{3,2,1,0:T(8,128)S(1)}, f32[2,6,16,512]{3,2,1,0:T(8,128)S(1)}, u32[]{:S(2)}, u32[]{:S(2)}) collective-permute-start(f32[2,6,16,512]{3,2,1,0:T(8,128)S(1)} %pad_maximum_fusion.refs_0_), channel_id=1, source_target_pairs={{0,12},{4,8},{8,4},{12,0},{16,28},{20,24},{24,20},{28,16},{1,13},{... | collective-permute-start | bytes 1179656 | tf_op jit(solution)/shard_map/ppermute | solution.py:334
  226.4 9.9 %collective-permute-start.19 = (f32[4,4,8,512]{3,2,1,0:T(8,128)S(1)}, f32[4,4,8,512]{3,2,1,0:T(8,128)S(1)}, u32[]{:S(2)}, u32[]{:S(2)}) collective-permute-start(f32[4,4,8,512]{3,2,1,0:T(8,128)S(1)} %pad_maximum_fusion.1.refs_0_), channel_id=1, source_target_pairs={{0,2},{1,3},{2,0},{3,1},{4,6},{5,7},{6,4},{7,5},{8,10},{9,11},{10,... | collective-permute-start | bytes 786440 | tf_op jit(solution)/shard_map/ppermute | solution.py:334
  226.4 14.5 %collective-permute-start.20 = (f32[4,4,8,512]{3,2,1,0:T(8,128)S(1)}, f32[4,4,8,512]{3,2,1,0:T(8,128)S(1)}, u32[]{:S(2)}, u32[]{:S(2)}) collective-permute-start(f32[4,4,8,512]{3,2,1,0:T(8,128)S(1)} %pad_maximum_fusion.1.refs_0_), channel_id=1, source_target_pairs={{0,3},{1,2},{2,1},{3,0},{4,7},{5,6},{6,5},{7,4},{8,11},{9,10},{10,... | collective-permute-start | bytes 786440 | tf_op jit(solution)/shard_map/ppermute | solution.py:334
  (15 other events, 250.7 us)
Sparse Core Ops, SparseCore 0:
  180.6 56.2 all-gather.1

commit v3 on v2

--- a/solution.py
+++ b/solution.py
@@ -51,6 +51,40 @@
     )(window, local)
 
 
+def lead_kernel(keep_ref, info_ref, x_ref, parent_ref, o_ref):
+    first = (info_ref[1] == 1).astype(jnp.float32)
+    for row in range(ROWS):
+        keep = keep_ref[row].astype(jnp.float32)
+        for group in range(GROUPS):
+            front, col = group // COLS, group % COLS
+            tile = slice(group * 8, group * 8 + 8)
+            o_ref[front, row, col, 0:8] = x_ref[row * BLK + group * 8 : row * BLK + group * 8 + 8, :] * keep
+            for j in range(2):
+                place = 2 * row + j
+                p, q = place // WB, place % WB
+                here = keep_ref[0] * (info_ref[0] == place).astype(jnp.int32)
+                part = x_ref[tile, :] * here.astype(jnp.float32)
+                extra = parent_ref[p * BLK + group * 8 : p * BLK + group * 8 + 8, q * BLK : (q + 1) * BLK]
+                o_ref[front, row, col, 8 + 8 * j : 16 + 8 * j] = part + extra * first
+
+
+def make_lead(keep, info, local, parent):
+    return pl.pallas_call(
+        lead_kernel,
+        name="lead",
+        grid_spec=pltpu.PrefetchScalarGridSpec(
+            num_scalar_prefetch=2,
+            grid=(1,),
+            in_specs=[
+                pl.BlockSpec((ROWS * BLK, BLK), lambda i, *_: (0, 0)),
+                pl.BlockSpec((W, W), lambda i, *_: (0, 0)),
+            ],
+            out_specs=pl.BlockSpec((FRONTS, ROWS, COLS, 24, BLK), lambda i, *_: (0, 0, 0, 0, 0)),
+        ),
+        out_shape=jax.ShapeDtypeStruct((FRONTS, ROWS, COLS, 24, BLK), jnp.float32),
+    )(keep, info, local, parent)
+
+
 def slice_kernel(inv_row_ref, inv_lead_ref, recv_ref, parent_ref, o_ref):
     for a in range(PR):
         for q in range(WB):
@@ -60,7 +94,7 @@
                 c = inv_lead_ref[front, q]
                 ok = jnp.logical_and(r >= 0, c >= 0).astype(jnp.float32)
                 source = front * 32 + jnp.maximum(r, 0) * COLS + jnp.maximum(c, 0)
-                total = total + recv_ref[source] * ok
+                total = total + recv_ref[source, 0:8] * ok
             o_ref[a, :, q * BLK : (q + 1) * BLK] = total
 
 
@@ -134,15 +168,15 @@
             put(g0, e[g0])
 
 
-def factor_kernel(place_ref, *refs):
-    pieces = refs[:COLS]
-    w_ref, m_ref, d_ref = refs[COLS:]
-    for other in range(COLS):
-        for slot in range(FRONTS):
-            source = place_ref[1] ^ (slot * COLS + other)
-            for block in range(WB):
-                start = pl.multiple_of(block * BLK + source * 8, 8)
-                m_ref[pl.ds(start, 8), :W] = pieces[other][slot, block]
+def factor_kernel(x_ref, high_ref, low_ref, m_ref, d_ref):
+    for source in range(FRONTS * ROWS * COLS):
+        row = source // COLS % ROWS
+        group = source // 32 * COLS + source % COLS
+        for j in range(2):
+            p, q = (2 * row + j) // WB, (2 * row + j) % WB
+            m_ref[p * BLK + group * 8 : p * BLK + group * 8 + 8, q * BLK : (q + 1) * BLK] = x_ref[
+                source, 8 * j : 8 * j + 8
+            ]
     lanes = lax.broadcasted_iota(jnp.int32, (BLK, BLK), 1)
     subs = lax.broadcasted_iota(jnp.int32, (BLK, BLK), 0)
     eye = jnp.where(lanes == subs, 1.0, 0.0).astype(jnp.float32)
@@ -176,35 +210,46 @@
         return carry
 
     lax.fori_loop(0, W // BLK, step, 0)
-    w_ref[...] = m_ref[:, W:]
-
-
-def factor_inverse(place, pieces):
+    inverse = m_ref[:, W:]
+    high = inverse.astype(jnp.bfloat16)
+    high_ref[...] = high
+    low_ref[...] = (inverse - high.astype(jnp.float32)).astype(jnp.bfloat16)
+
+
+def factor_inverse(tiles):
     vmem = pl.BlockSpec(memory_space=pltpu.VMEM)
+    half = jax.ShapeDtypeStruct((W, W), jnp.bfloat16)
     return pl.pallas_call(
         factor_kernel,
         name="factor",
-        in_specs=[pl.BlockSpec(memory_space=pltpu.SMEM)] + [vmem] * COLS,
-        out_specs=vmem,
-        out_shape=jax.ShapeDtypeStruct((W, W), jnp.float32),
+        in_specs=[vmem],
+        out_specs=[vmem, vmem],
+        out_shape=[half, half],
         scratch_shapes=[pltpu.VMEM((W, 2 * W), jnp.float32), pltpu.VMEM((BLK, BLK), jnp.float32)],
         compiler_params=pltpu.CompilerParams(vmem_limit_bytes=40 << 20),
-    )(place, *pieces)
+    )(tiles)
+
+
+def split(x):
+    high = x.astype(jnp.bfloat16)
+    return high, (x - high.astype(jnp.float32)).astype(jnp.bfloat16)
+
+
+def three_products(x, high, low):
+    def product(a, b):
+        return lax.dot_general(a, b, (((1,), (1,)), ((), ())), preferred_element_type=jnp.float32)
+
+    x_high, x_low = split(x)
+    return (product(x_high, low) + product(x_low, high)) + product(x_high, high)
 
 
 def panel_kernel(place_ref, rows_ref, *refs):
     cols = refs[:4]
-    inverse_ref, panel_ref, high_ref, low_ref, block_ref = refs[4:]
+    inverse_high, inverse_low, panel_ref, high_ref, low_ref, block_ref = refs[4:]
     step = pl.program_id(0)
 
     def times_inverse(x):
-        return lax.dot_general(
-            x,
-            inverse_ref[...],
-            (((1,), (1,)), ((), ())),
-            precision=HIGHEST,
-            preferred_element_type=jnp.float32,
-        )
+        return three_products(x, inverse_high[...], inverse_low[...])
 
     @pl.when(step < PR)
     def _():
@@ -218,12 +263,10 @@
                 start = pl.multiple_of(source * 16, 16)
                 block_ref[pl.ds(start, 16), :] = cols[other][slot, 0]
         value = times_inverse(block_ref[...])
-        high = value.astype(jnp.bfloat16)
-        high_ref[...] = high
-        low_ref[...] = (value - high.astype(jnp.float32)).astype(jnp.bfloat16)
-
-
-def make_panels(place, rows_raw, cols_raw, inverse):
+        high_ref[...], low_ref[...] = split(value)
+
+
+def make_panels(place, rows_raw, cols_raw, inverses):
     def in_rows(i):
         return jnp.minimum(i, PR - 1)
 
@@ -239,7 +282,7 @@
             grid=(PR + PC,),
             in_specs=[pl.BlockSpec((GROUPS, 1, 8, W), lambda i, p: (0, in_rows(i), 0, 0))]
             + [pl.BlockSpec((2, 1, 16, W), lambda i, p: (0, in_cols(i), 0, 0))] * 4
-            + [pl.BlockSpec((W, W), lambda i, p: (0, 0))],
+            + [pl.BlockSpec((W, W), lambda i, p: (0, 0))] * 2,
             out_specs=[
                 pl.BlockSpec((BLK, W), lambda i, p: (in_rows(i), 0)),
                 pl.BlockSpec((BLK, W), lambda i, p: (in_cols(i), 0)),
@@ -249,24 +292,14 @@
         ),
         out_shape=[jax.ShapeDtypeStruct((PR * BLK, W), jnp.float32), half, half],
         compiler_params=pltpu.CompilerParams(vmem_limit_bytes=32 << 20),
-    )(place, rows_raw, *cols_raw, inverse)
+    )(place, rows_raw, *cols_raw, *inverses)
 
 
 def final_kernel(inv_row_ref, inv_col_ref, lead_ref, *refs):
     recvs = refs[:FRONTS]
     parent_ref, panel_ref, high_ref, low_ref, o_ref = refs[FRONTS:]
     a = pl.program_id(0)
-    panel = panel_ref[...]
-    panel_high = panel.astype(jnp.bfloat16)
-    panel_low = (panel - panel_high.astype(jnp.float32)).astype(jnp.bfloat16)
-
-    def product(x, y):
-        return lax.dot_general(
-            x, y, (((1,), (1,)), ((), ())), preferred_element_type=jnp.float32
-        )
-
-    total = product(panel_high, low_ref[...]) + product(panel_low, high_ref[...])
-    o_ref[...] = parent_ref[...] - (total + product(panel_high, high_ref[...]))
+    o_ref[...] = parent_ref[...] - three_products(panel_ref[...], high_ref[...], low_ref[...])
     for b in range(PC):
         span = slice(b * BLK, (b + 1) * BLK)
         total = o_ref[:, span]
@@ -355,10 +388,20 @@
     local = child_update[0]
     window = lax.dynamic_slice(child_mask[0], (row * ROWS, col * GROUPS), (ROWS, GROUPS))
 
-    lead_keep = window[:, 0].astype(jnp.float32)
-    lead = local[:, :BLK].reshape(ROWS, FRONTS, COLS, 8, BLK) * lead_keep[:, None, None, None, None]
-    lead = lead.transpose(1, 0, 2, 3, 4).reshape(128, 8, BLK)
+    lead_map = child_map.reshape(FRONTS, COLS, GROUPS)[:, :, 0]
+    mine = lax.dynamic_index_in_dim(lead_map, front, 0, keepdims=False)
+    p = lax.dynamic_index_in_dim(mine, row // 2, 0, keepdims=False)
+    q = lax.dynamic_index_in_dim(mine, col, 0, keepdims=False)
+    inside = (row % 2 == 0) & (p < WB) & (q < WB)
+    corner_place = jnp.where(inside, p * WB + q, -1)
+    holder = (row == 0) & (group == 0)
+    info = jnp.stack([corner_place, holder.astype(jnp.int32)]).astype(jnp.int32)
+    lead = make_lead(window[:, 0], info, local, parent_entries).reshape(128, 24, BLK)
     lead_recv = lax.all_to_all(lead, ALL, 0, 0, tiled=True)
+    tiles = jnp.sum(lead_recv[:, 8:], axis=0)
+    tiles = jnp.broadcast_to(tiles[None], (128, 16, BLK))
+    tiles = lax.all_to_all(tiles, ALL, 0, 0, tiled=True)
+    inverses = factor_inverse(tiles)
 
     first = parent_entries[:, :W].reshape(PR, FRONTS, COLS, 8, W)
     first = scatter_from_first(first, "col", lambda x, k: x[:, :, k])
@@ -371,24 +414,11 @@
     )
     inv_row = inverse_places(by_row - row * PR, PR)
     inv_col = inverse_places(by_col - group * PC, PC)
-    inv_lead = inverse_places(child_map.reshape(FRONTS, COLS, GROUPS)[:, :, 0], WB)
+    inv_lead = inverse_places(lead_map, WB)
 
     slices = assemble_slices(inv_row, inv_lead, lead_recv, first)
 
-    corner = slices[:WB]
-    near = jnp.where(row == 0, corner, 0.0)
-    for k in range(1, 4):
-        near = near + lax.ppermute(corner, "row", [(0, k)])
-    far = lax.ppermute(near, "row", [(k, 4 + k) for k in range(4)])
-    corner = jnp.where(row < 4, near, far)
-    corner = jnp.stack([corner, flipped(corner, "front", 1)])
-    corner = jnp.concatenate([corner, flipped(corner, "front", 2)])
-    pieces = [corner] + [flipped(corner, "col", bits) for bits in range(1, COLS)]
     place = jnp.stack([row, group]).astype(jnp.int32)
-    inverse = factor_inverse(place, pieces)
-
-    packed = pack(window, local).reshape(128, BLK, BLK)
-    recv = lax.all_to_all(packed, ALL, 0, 0, tiled=True)
 
     rows_raw = lax.all_gather(slices.reshape(PR * 8, W), GRP, axis=0, tiled=True)
     rows_raw = rows_raw.reshape(GROUPS, PR, 8, W)
@@ -401,7 +431,11 @@
     mine = jnp.stack([mine, flipped(mine, "row", 4)])
     cols_raw = [mine] + [flipped(mine, "row", bits) for bits in range(1, 4)]
 
-    panel, high, low = make_panels(place, rows_raw, cols_raw, inverse)
+    packed = pack(window, local).reshape(128, BLK, BLK)
+    packed, cols_raw = lax.optimization_barrier((packed, cols_raw))
+    recv = lax.all_to_all(packed, ALL, 0, 0, tiled=True)
+
+    panel, high, low = make_panels(place, rows_raw, cols_raw, inverses)
     lead_flags = jnp.stack([row == 0, group == 0]).astype(jnp.int32)
     schur = finish(inv_row, inv_col, lead_flags, recv, parent_entries, panel, high, low)
     return schur, panel

time: 333 us -> 344 us (1.033); the launches traced: 331 us -> 337 us
  waiting for transfers between devices: 141 us -> 160 us
  starting transfers between devices: 67.3 us -> 56.4 us
  Pallas kernels: 78 us -> 71.7 us
    all_gather x1, waiting for transfers between devices: 0.01 us -> 95.1 us  [body(): lax.all_gather(slices.reshape(PR * 8, W), GRP, axis=0, tiled=True)]
    ppermute x6, waiting for transfers between devices: 117 us -> 40.6 us  [scatter_from_first(): total = total + lax.ppermute(parts(x, k), axis, [(0, k)])]
    ppermute x9 -> x4, starting transfers between devices: 21.4 us -> 6.91 us  [flipped(): return lax.ppermute(x, axis, [(i, i ^ bits) for i in range(size)])]
    pallas_call x1, Pallas kernels: 23.6 us -> 14.1 us  [make_panels(): pl.pallas_call(panel_kernel, name='panels', grid_spec=pltpu.PrefetchScala...]
    all_to_all x0 -> x1, starting transfers between devices: none -> 9.11 us  [body(): tiles = lax.all_to_all(tiles, ALL, 0, 0, tiled=True)]
    ppermute x4 -> x0, starting transfers between devices: 8.61 us -> none  [the longest x3 7.31 us: body(): near = near + lax.ppermute(corner, 'row', [(0, k)])]
    ppermute x9 -> x4, waiting for transfers between devices: 16.7 us -> 23.9 us  [flipped(): return lax.ppermute(x, axis, [(i, i ^ bits) for i in range(size)])]
    all_to_all x1, waiting for transfers between devices: 4.96 us -> 0.01 us  [body(): lead_recv = lax.all_to_all(lead, ALL, 0, 0, tiled=True)]
  transfers between devices with their start and end apart: 24 -> 16, of which waited for: 11 -> 7; matrix products, arithmetic and copies ran while one was open for 3% -> 3% of each run, Pallas kernels for 19% -> 15%
where the time goes in v3:
time: 344 us; the launch traced here: 337 us
  waiting for transfers between devices  160 us (47%)
  Pallas kernels  71.7 us (21%)
  starting transfers between devices  56.4 us (16%)
  local copies, waits for them, and re-layouts  24.9 us (7%)
  between operations  16.9 us (5%)
  other arithmetic  7.36 us (2%)
    all_gather x1, waiting for transfers between devices, body(): lax.all_gather(slices.reshape(PR * 8, W), GRP, axis=0, tiled=True)  95.1 us
    ppermute x6, waiting for transfers between devices, scatter_from_first(): total = total + lax.ppermute(parts(x, k), axis, [(0, k)])  40.6 us
    pallas_call x1, Pallas kernels, factor_inverse(): pl.pallas_call(factor_kernel, name='factor', in_specs=[vmem], out_specs=[...  33.5 us
    ppermute x4, waiting for transfers between devices, flipped(): return lax.ppermute(x, axis, [(i, i ^ bits) for i in range(size)])  23.9 us
    unnamed x36, local copies, waits for them, and re-layouts  18.5 us
    pallas_call x1, Pallas kernels, finish(): pl.pallas_call(final_kernel, name='finish', grid_spec=pltpu.PrefetchScala...  16.1 us
    pallas_call x1, Pallas kernels, make_panels(): pl.pallas_call(panel_kernel, name='panels', grid_spec=pltpu.PrefetchScala...  14.1 us
    ppermute x6, starting transfers between devices, scatter_from_first(): total = total + lax.ppermute(parts(x, k), axis, [(0, k)])  13.2 us
  transfers between devices with their start and end apart: 16, of which 7 were waited for; matrix products, arithmetic and copies ran while one was open for 3% of the time, Pallas kernels for 15%

profile of v3, /device:TPU:1, one launch (start us, length us, event | category | flops | bytes accessed | tf_op | source)
XLA Modules:
  0.0 337.3 jit_solution(11410456595029078283)
XLA Ops:
  12.7 3.4 lead.1
  16.1 11.9 %all-to-all-start = ((f32[128,24,128]{2,1,0:T(8,128)}), f32[128,24,128]{2,1,0:T(8,128)}, u32[]{:S(2)}, u32[]{:S(2)}) async-start(f32[128,24,128]{2,1,0:T(8,128)} %bitcast.66), calls=%async_computation | async-start | bytes 3145728 | tf_op jit(solution)/shard_map/all_to_all | solution.py:400
  31.1 6.2 %collective-permute-start.2 = (f32[12,4,8,512]{3,2,0,1:T(8,128)S(1)}, f32[12,4,8,512]{3,2,0,1:T(8,128)}, u32[]{:S(2)}, u32[]{:S(2)}) collective-permute-start(f32[12,4,8,512]{3,2,0,1:T(8,128)S(1)} %bitcast.68), channel_id=1, source_target_pairs={{0,3},{4,7},{8,11},{12,15},{16,19},{20,23},{24,27},{28,31},{32,35}... | collective-permute-start | bytes 2359304 | tf_op jit(solution)/shard_map/ppermute | solution.py:361
  37.4 2.2 collective-permute-start.1
  39.6 2.2 collective-permute-start
  42.9 20.7 %collective-permute-done.2 = f32[12,4,8,512]{3,2,0,1:T(8,128)} collective-permute-done((f32[12,4,8,512]{3,2,0,1:T(8,128)S(1)}, f32[12,4,8,512]{3,2,0,1:T(8,128)}, u32[]{:S(2)}, u32[]{:S(2)}) %collective-permute-start.2) | collective-permute-done | bytes 786464 | tf_op jit(solution)/shard_map/ppermute | solution.py:361
  63.5 16.3 %collective-permute-done = f32[12,4,8,512]{3,2,0,1:T(8,128)} collective-permute-done((f32[12,4,8,512]{3,2,0,1:T(8,128)S(1)}, f32[12,4,8,512]{3,2,0,1:T(8,128)}, u32[]{:S(2)}, u32[]{:S(2)}) %collective-permute-start) | collective-permute-done | bytes 786464 | tf_op jit(solution)/shard_map/ppermute | solution.py:361
  85.1 3.6 %collective-permute-done.3 = f32[12,8,512]{2,1,0:T(8,128)S(1)} collective-permute-done((f32[12,8,512]{2,1,0:T(8,128)S(1)}, f32[12,8,512]{2,1,0:T(8,128)S(1)}, u32[]{:S(2)}, u32[]{:S(2)}) %collective-permute-start.3) | collective-permute-done | bytes 196640 | tf_op jit(solution)/shard_map/ppermute | solution.py:361
  89.4 2.7 slices.1
  93.1 5.0 %collective-permute-start.6 = (f32[6,8,512]{2,1,0:T(8,128)S(1)}, f32[6,8,512]{2,1,0:T(8,128)S(1)}, u32[]{:S(2)}, u32[]{:S(2)}) collective-permute-start(f32[6,8,512]{2,1,0:T(8,128)S(1)} %get-tuple-element.33), channel_id=1, source_target_pairs={{0,0},{1,1},{2,4},{3,5},{4,2},{5,3},{6,6},{7,7},{8,32},{9,33},{10,... | collective-permute-start | bytes 294920 | tf_op jit(solution)/shard_map/ppermute | solution.py:427
  98.2 2.2 collective-permute-start.7
  102.8 9.1 %all-to-all-start.2 = ((f32[128,16,128]{2,1,0:T(8,128)}), f32[128,16,128]{2,1,0:T(8,128)S(1)}, u32[]{:S(2)}, u32[]{:S(2)}) async-start(f32[128,16,128]{2,1,0:T(8,128)} %broadcast_in_dim.66), calls=%async_computation.2 | async-start | bytes 2097152 | tf_op jit(solution)/shard_map/all_to_all | solution.py:403
  112.0 3.0 collective-permute-start.8
  115.0 15.4 %collective-permute-done.8 = f32[6,16,512]{2,1,0:T(8,128)S(1)} collective-permute-done((f32[6,16,512]{2,1,0:T(8,128)S(1)}, f32[6,16,512]{2,1,0:T(8,128)S(1)}, u32[]{:S(2)}, u32[]{:S(2)}) %collective-permute-start.8) | collective-permute-done | bytes 196640 | tf_op jit(solution)/shard_map/ppermute | solution.py:367
  131.7 2.5 collective-permute-start.10
  134.3 3.4 %copy-done.2 = f32[1,1024,2048]{2,1,0:T(8,128)S(1)} copy-done((f32[1,1024,2048]{2,1,0:T(8,128)S(1)}, f32[1,1024,2048]{2,1,0:T(8,128)}, u32[]{:S(2)}) %copy-start.2) | copy-done | bytes 8388632
  139.6 3.3 copy-done.3
  143.6 7.2 %collective-permute-done.10.refs_2_ = f32[2,6,16,512]{3,2,1,0:T(8,128)S(1)} collective-permute-done((f32[2,6,16,512]{3,2,1,0:T(8,128)S(1)}, f32[2,6,16,512]{3,2,1,0:T(8,128)S(1)}, u32[]{:S(2)}, u32[]{:S(2)}) %collective-permute-start.10) | collective-permute-done | bytes 393248 | tf_op jit(solution)/shard_map/ppermute | solution.py:367
  153.7 7.8 %all-to-all-start.1 = ((f32[128,128,128]{2,1,0:T(8,128)}), f32[128,128,128]{2,1,0:T(8,128)}, u32[]{:S(2)}, u32[]{:S(2)}) async-start(f32[128,128,128]{2,1,0:T(8,128)} %bitcast.64), calls=%async_computation.1 | async-start | bytes 16777216 | tf_op jit(solution)/shard_map/all_to_all | solution.py:436
  162.6 33.5 %factor.1 = (bf16[512,512]{1,0:T(8,128)(2,1)S(1)}, bf16[512,512]{1,0:T(8,128)(2,1)S(1)}) custom-call(f32[128,16,128]{2,1,0:T(8,128)S(1)} %all-to-all-done.2.x_ref), custom_call_target="tpu_custom_call" | custom-call | tf_op jit(solution)/shard_map/factor/pallas_call | solution.py:222
  196.1 95.1 %all-gather.2.cloned.1.call-done = f32[1536,512]{1,0:T(8,128)} async-done(((f32[96,512]{1,0:T(8,128)}), f32[1536,512]{1,0:T(8,128)}) %all-gather.2.cloned.1.call-update) | async-done | bytes 3145744 | tf_op jit(solution)/shard_map/all_gather | solution.py:423
  296.1 14.1 %panels.1 = (f32[1536,512]{1,0:T(8,128)}, bf16[768,512]{1,0:T(8,128)(2,1)S(1)}, bf16[768,512]{1,0:T(8,128)(2,1)S(1)}) custom-call(s32[2]{0:T(128)S(1)} %pad_add_fusion.1.place_ref, f32[16,12,8,512]{3,2,1,0:T(8,128)S(1)} %bitcast.65, f32[2,6,16,512]{3,2,1,0:T(8,128)S(1)} %pad_maximum_fusion.refs_0_, f32[2,6,16,512]{3,2,1,0:T(8,128)S(1)} %copy-done.7, ...), custom_call_target="tpu_custom_call" | custom-call | tf_op jit(solution)/shard_map/panels/pallas_call | solution.py:277
  310.2 2.3 copy-done.1
  314.4 16.1 %finish.1 = f32[1536,768]{1,0:T(8,128)} custom-call(s32[4,12]{1,0:T(4,128)S(1)} %copy-done.12, s32[4,6]{1,0:T(4,128)S(1)} %broadcast_add_fusion.1.inv_col_ref, s32[2]{0:T(128)S(1)} %add_convert_fusion.lead_ref, f32[128,128,128]{2,1,0:T(8,128)} %all-to-all-done.1.refs_0_.refs_1_.refs_2_.refs_3_, ...), custom_call_target="tpu_custom_call" | custom-call | tf_op jit(solution)/shard_map/finish/pallas_call | solution.py:328
  (82 shorter events, 31.4 us)
Async XLA Ops:
  7.2 3.0 copy-start
  16.1 73.4 %all-to-all-start = ((f32[128,24,128]{2,1,0:T(8,128)}), f32[128,24,128]{2,1,0:T(8,128)}, u32[]{:S(2)}, u32[]{:S(2)}) async-start(f32[128,24,128]{2,1,0:T(8,128)} %bitcast.66), calls=%async_computation | async-start | bytes 3145728 | tf_op jit(solution)/shard_map/all_to_all | solution.py:400
  28.0 1.9 slice-start
  31.1 10.8 %copy-start.14 = (s32[4,64]{1,0:T(4,128)S(1)}, s32[4,64]{1,0:T(4,128)}, u32[]{:S(2)}) copy-start(s32[4,64]{1,0:T(4,128)} %param.6) | copy-start | bytes 3076
  31.1 48.7 %copy-start.13 = (f32[12,4,1,8,512]{4,3,2,1,0:T(8,128)S(1)}, f32[12,4,1,8,512]{4,3,2,1,0:T(8,128)}, u32[]{:S(2)}) copy-start(f32[12,4,1,8,512]{4,3,2,1,0:T(8,128)} %get-tuple-element.22) | copy-start | bytes 2359300
  31.1 32.4 %collective-permute-start.2 = (f32[12,4,8,512]{3,2,0,1:T(8,128)S(1)}, f32[12,4,8,512]{3,2,0,1:T(8,128)}, u32[]{:S(2)}, u32[]{:S(2)}) collective-permute-start(f32[12,4,8,512]{3,2,0,1:T(8,128)S(1)} %bitcast.68), channel_id=1, source_target_pairs={{0,3},{4,7},{8,11},{12,15},{16,19},{20,23},{24,27},{28,31},{32,35}... | collective-permute-start | bytes 2359304 | tf_op jit(solution)/shard_map/ppermute | solution.py:361
  37.4 26.1 %collective-permute-start.1 = (f32[12,4,8,512]{3,2,0,1:T(8,128)S(1)}, f32[12,4,8,512]{3,2,0,1:T(8,128)}, u32[]{:S(2)}, u32[]{:S(2)}) collective-permute-start(f32[12,4,8,512]{3,2,0,1:T(8,128)S(1)} %bitcast.69), channel_id=1, source_target_pairs={{0,2},{4,6},{8,10},{12,14},{16,18},{20,22},{24,26},{28,30},{32,34}... | collective-permute-start | bytes 2359304 | tf_op jit(solution)/shard_map/ppermute | solution.py:361
  39.6 40.2 %collective-permute-start = (f32[12,4,8,512]{3,2,0,1:T(8,128)S(1)}, f32[12,4,8,512]{3,2,0,1:T(8,128)}, u32[]{:S(2)}, u32[]{:S(2)}) collective-permute-start(f32[12,4,8,512]{3,2,0,1:T(8,128)S(1)} %bitcast.70), channel_id=1, source_target_pairs={{0,1},{4,5},{8,9},{12,13},{16,17},{20,21},{24,25},{28,29},{32,33},... | collective-permute-start | bytes 2359304 | tf_op jit(solution)/shard_map/ppermute | solution.py:361
  81.8 3.2 collective-permute-start.5
  82.5 2.6 collective-permute-start.4
  83.2 5.5 %collective-permute-start.3 = (f32[12,8,512]{2,1,0:T(8,128)S(1)}, f32[12,8,512]{2,1,0:T(8,128)S(1)}, u32[]{:S(2)}, u32[]{:S(2)}) collective-permute-start(f32[12,8,512]{2,1,0:T(8,128)S(1)} %get-tuple-element.26), channel_id=1, source_target_pairs={{0,32},{1,33},{2,34},{3,35},{4,36},{5,37},{6,38},{7,39},{8,40},{9,... | collective-permute-start | bytes 589832 | tf_op jit(solution)/shard_map/ppermute | solution.py:361
  93.1 18.8 %collective-permute-start.6 = (f32[6,8,512]{2,1,0:T(8,128)S(1)}, f32[6,8,512]{2,1,0:T(8,128)S(1)}, u32[]{:S(2)}, u32[]{:S(2)}) collective-permute-start(f32[6,8,512]{2,1,0:T(8,128)S(1)} %get-tuple-element.33), channel_id=1, source_target_pairs={{0,0},{1,1},{2,4},{3,5},{4,2},{5,3},{6,6},{7,7},{8,32},{9,33},{10,... | collective-permute-start | bytes 294920 | tf_op jit(solution)/shard_map/ppermute | solution.py:427
  98.2 13.8 %collective-permute-start.7 = (f32[6,8,512]{2,1,0:T(8,128)S(1)}, f32[6,8,512]{2,1,0:T(8,128)S(1)}, u32[]{:S(2)}, u32[]{:S(2)}) collective-permute-start(f32[6,8,512]{2,1,0:T(8,128)S(1)} %get-tuple-element.34), channel_id=1, source_target_pairs={{0,1},{1,0},{2,5},{3,4},{4,3},{5,2},{6,7},{7,6},{8,33},{9,32},{10,... | collective-permute-start | bytes 294920 | tf_op jit(solution)/shard_map/ppermute | solution.py:428
  102.8 50.9 %all-to-all-start.2 = ((f32[128,16,128]{2,1,0:T(8,128)}), f32[128,16,128]{2,1,0:T(8,128)S(1)}, u32[]{:S(2)}, u32[]{:S(2)}) async-start(f32[128,16,128]{2,1,0:T(8,128)} %broadcast_in_dim.66), calls=%async_computation.2 | async-start | bytes 2097152 | tf_op jit(solution)/shard_map/all_to_all | solution.py:403
  112.0 18.4 %collective-permute-start.8 = (f32[6,16,512]{2,1,0:T(8,128)S(1)}, f32[6,16,512]{2,1,0:T(8,128)S(1)}, u32[]{:S(2)}, u32[]{:S(2)}) collective-permute-start(f32[6,16,512]{2,1,0:T(8,128)S(1)} %get-tuple-element.30), channel_id=1, source_target_pairs={{0,16},{4,20},{8,24},{12,28},{16,0},{20,4},{24,8},{28,12},{1,17},{... | collective-permute-start | bytes 589832 | tf_op jit(solution)/shard_map/ppermute | solution.py:367
  130.4 12.5 %collective-permute-start.9 = (f32[2,6,16,512]{3,2,1,0:T(8,128)S(1)}, f32[2,6,16,512]{3,2,1,0:T(8,128)S(1)}, u32[]{:S(2)}, u32[]{:S(2)}) collective-permute-start(f32[2,6,16,512]{3,2,1,0:T(8,128)S(1)} %pad_maximum_fusion.refs_0_), channel_id=1, source_target_pairs={{0,4},{4,0},{8,12},{12,8},{16,20},{20,16},{24,28},{28,24},{1,5},{5... | collective-permute-start | bytes 1179656 | tf_op jit(solution)/shard_map/ppermute | solution.py:367
  131.7 19.2 %collective-permute-start.10 = (f32[2,6,16,512]{3,2,1,0:T(8,128)S(1)}, f32[2,6,16,512]{3,2,1,0:T(8,128)S(1)}, u32[]{:S(2)}, u32[]{:S(2)}) collective-permute-start(f32[2,6,16,512]{3,2,1,0:T(8,128)S(1)} %pad_maximum_fusion.refs_0_), channel_id=1, source_target_pairs={{0,8},{4,12},{8,0},{12,4},{16,24},{20,28},{24,16},{28,20},{1,9},{5... | collective-permute-start | bytes 1179656 | tf_op jit(solution)/shard_map/ppermute | solution.py:367
  134.1 18.8 %collective-permute-start.11 = (f32[2,6,16,512]{3,2,1,0:T(8,128)S(1)}, f32[2,6,16,512]{3,2,1,0:T(8,128)S(1)}, u32[]{:S(2)}, u32[]{:S(2)}) collective-permute-start(f32[2,6,16,512]{3,2,1,0:T(8,128)S(1)} %pad_maximum_fusion.refs_0_), channel_id=1, source_target_pairs={{0,12},{4,8},{8,4},{12,0},{16,28},{20,24},{24,20},{28,16},{1,13},{... | collective-permute-start | bytes 1179656 | tf_op jit(solution)/shard_map/ppermute | solution.py:367
  134.3 3.4 %copy-start.2 = (f32[1,1024,2048]{2,1,0:T(8,128)S(1)}, f32[1,1024,2048]{2,1,0:T(8,128)}, u32[]{:S(2)}) copy-start(f32[1,1024,2048]{2,1,0:T(8,128)} %param.5) | copy-start | bytes 25165828
  139.6 3.3 copy-start.3
  153.7 156.4 %all-to-all-start.1 = ((f32[128,128,128]{2,1,0:T(8,128)}), f32[128,128,128]{2,1,0:T(8,128)}, u32[]{:S(2)}, u32[]{:S(2)}) async-start(f32[128,128,128]{2,1,0:T(8,128)} %bitcast.64), calls=%async_computation.1 | async-start | bytes 16777216 | tf_op jit(solution)/shard_map/all_to_all | solution.py:436
  161.5 129.7 %all-gather.2.cloned.1.call-start = ((), (), s32[]{:S(2)}) async-start(), calls=%async_computation.3 | async-start | bytes 3342336 | tf_op jit(solution)/shard_map/all_gather | solution.py:423
  196.1 114.1 %copy-start.12 = (s32[4,12]{1,0:T(4,128)S(1)}, s32[4,12]{1,0:T(4,128)}, u32[]{:S(2)}) copy-start(s32[4,12]{1,0:T(4,128)} %broadcast_add_fusion.2.inv_row_ref) | copy-start | bytes 580
  310.2 2.3 copy-start.1
  (8 other events, 9.0 us)
Sparse Core Ops, SparseCore 0:
  164.0 127.1 all-gather.1

commit v4 on v3

--- a/solution.py
+++ b/solution.py
@@ -243,9 +243,9 @@
     return (product(x_high, low) + product(x_low, high)) + product(x_high, high)
 
 
-def panel_kernel(place_ref, rows_ref, *refs):
-    cols = refs[:4]
-    inverse_high, inverse_low, panel_ref, high_ref, low_ref, block_ref = refs[4:]
+def panel_kernel(place_ref, *refs):
+    rows, cols = refs[:8], refs[8:16]
+    inverse_high, inverse_low, panel_ref, high_ref, low_ref, block_ref = refs[16:]
     step = pl.program_id(0)
 
     def times_inverse(x):
@@ -253,15 +253,19 @@
 
     @pl.when(step < PR)
     def _():
-        panel_ref[...] = times_inverse(rows_ref[:, 0].reshape(BLK, W))
+        for core in range(2):
+            for col in range(COLS):
+                for x in range(2):
+                    source = place_ref[1] ^ (x * 8 + core * 4 + col)
+                    start = pl.multiple_of(source * 8, 8)
+                    block_ref[pl.ds(start, 8), :] = rows[core * COLS + col][x, 0]
+        panel_ref[...] = times_inverse(block_ref[...])
 
     @pl.when(step >= PR)
     def _():
-        for other in range(4):
-            for slot in range(2):
-                source = place_ref[0] ^ (slot * 4 + other)
-                start = pl.multiple_of(source * 16, 16)
-                block_ref[pl.ds(start, 16), :] = cols[other][slot, 0]
+        for other in range(ROWS):
+            start = pl.multiple_of((place_ref[0] ^ other) * 16, 16)
+            block_ref[pl.ds(start, 16), :] = cols[other][0]
         value = times_inverse(block_ref[...])
         high_ref[...], low_ref[...] = split(value)
 
@@ -280,8 +284,8 @@
         grid_spec=pltpu.PrefetchScalarGridSpec(
             num_scalar_prefetch=1,
             grid=(PR + PC,),
-            in_specs=[pl.BlockSpec((GROUPS, 1, 8, W), lambda i, p: (0, in_rows(i), 0, 0))]
-            + [pl.BlockSpec((2, 1, 16, W), lambda i, p: (0, in_cols(i), 0, 0))] * 4
+            in_specs=[pl.BlockSpec((2, 1, 8, W), lambda i, p: (0, in_rows(i), 0, 0))] * 8
+            + [pl.BlockSpec((1, 16, W), lambda i, p: (in_cols(i), 0, 0))] * ROWS
             + [pl.BlockSpec((W, W), lambda i, p: (0, 0))] * 2,
             out_specs=[
                 pl.BlockSpec((BLK, W), lambda i, p: (in_rows(i), 0)),
@@ -292,59 +296,66 @@
         ),
         out_shape=[jax.ShapeDtypeStruct((PR * BLK, W), jnp.float32), half, half],
         compiler_params=pltpu.CompilerParams(vmem_limit_bytes=32 << 20),
-    )(place, rows_raw, *cols_raw, *inverses)
+    )(place, *rows_raw, *cols_raw, *inverses)
+
+
+PAIR = 2
 
 
 def final_kernel(inv_row_ref, inv_col_ref, lead_ref, *refs):
-    recvs = refs[:FRONTS]
-    parent_ref, panel_ref, high_ref, low_ref, o_ref = refs[FRONTS:]
-    a = pl.program_id(0)
+    recvs = refs[: PAIR * FRONTS]
+    parent_ref, panel_ref, high_ref, low_ref, o_ref = refs[PAIR * FRONTS :]
+    step = pl.program_id(0)
     o_ref[...] = parent_ref[...] - three_products(panel_ref[...], high_ref[...], low_ref[...])
-    for b in range(PC):
-        span = slice(b * BLK, (b + 1) * BLK)
-        total = o_ref[:, span]
-        for front in range(FRONTS):
-            r = inv_row_ref[front, a]
-            c = inv_col_ref[front, b]
-            ok = jnp.logical_and(r >= 0, c >= 0).astype(jnp.float32)
-            total = total + recvs[front][jnp.maximum(c, 0)] * ok
-        o_ref[:, span] = total
-    leading_row = jnp.logical_and(lead_ref[0] == 1, a < WB)
-
-    @pl.when(leading_row)
+    for half in range(PAIR):
+        rows = slice(half * BLK, (half + 1) * BLK)
+        for b in range(PC):
+            span = slice(b * BLK, (b + 1) * BLK)
+            total = o_ref[rows, span]
+            for front in range(FRONTS):
+                r = inv_row_ref[front, step * PAIR + half]
+                c = inv_col_ref[front, b]
+                ok = jnp.logical_and(r >= 0, c >= 0).astype(jnp.float32)
+                total = total + recvs[half * FRONTS + front][jnp.maximum(c, 0)] * ok
+            o_ref[rows, span] = total
+
+    @pl.when(jnp.logical_and(lead_ref[0] == 1, step < WB // PAIR))
     def _():
         o_ref[...] = jnp.zeros_like(o_ref)
 
     @pl.when(lead_ref[1] == 1)
     def _():
-        o_ref[:, :W] = jnp.zeros((BLK, W), jnp.float32)
+        o_ref[:, :W] = jnp.zeros((PAIR * BLK, W), jnp.float32)
 
 
 def finish(inv_row, inv_col, lead, recv, parent, panel, high, low):
-    def recv_map(front):
-        return lambda a, ir, ic, ld: (front * ROWS + jnp.maximum(ir[front, a], 0), 0, 0)
+    def recv_map(half, front):
+        return lambda i, ir, ic, ld: (
+            front * ROWS + jnp.maximum(ir[front, i * PAIR + half], 0),
+            0,
+            0,
+        )
 
     whole = pl.BlockSpec((PC * BLK, W), lambda a, *_: (0, 0))
+    block = pl.BlockSpec((PAIR * BLK, PC * BLK), lambda a, *_: (a, 0))
+    recv_specs = [
+        pl.BlockSpec((COLS, BLK, BLK), recv_map(half, front))
+        for half in range(PAIR)
+        for front in range(FRONTS)
+    ]
     return pl.pallas_call(
         final_kernel,
         name="finish",
         grid_spec=pltpu.PrefetchScalarGridSpec(
             num_scalar_prefetch=3,
-            grid=(PR,),
-            in_specs=[
-                pl.BlockSpec((COLS, BLK, BLK), recv_map(front)) for front in range(FRONTS)
-            ]
-            + [
-                pl.BlockSpec((BLK, PC * BLK), lambda a, *_: (a, 0)),
-                pl.BlockSpec((BLK, W), lambda a, *_: (a, 0)),
-                whole,
-                whole,
-            ],
-            out_specs=pl.BlockSpec((BLK, PC * BLK), lambda a, *_: (a, 0)),
+            grid=(PR // PAIR,),
+            in_specs=recv_specs
+            + [block, pl.BlockSpec((PAIR * BLK, W), lambda a, *_: (a, 0)), whole, whole],
+            out_specs=block,
         ),
         out_shape=jax.ShapeDtypeStruct((PR * BLK, PC * BLK), jnp.float32),
         compiler_params=pltpu.CompilerParams(vmem_limit_bytes=40 << 20),
-    )(inv_row, inv_col, lead, recv, recv, recv, recv, parent, panel, high, low)
+    )(inv_row, inv_col, lead, *([recv] * len(recv_specs)), parent, panel, high, low)
 
 
 def inverse_places(places, length):
@@ -352,14 +363,6 @@
     hits = places[:, :, None] == jnp.arange(length, dtype=jnp.int32)
     order = jnp.arange(1, count + 1, dtype=jnp.int32)[None, :, None]
     return jnp.sum(jnp.where(hits, order, 0), axis=1) - 1
-
-
-def scatter_from_first(x, axis, parts):
-    index = lax.axis_index(axis)
-    total = jnp.where(index == 0, parts(x, 0), 0.0)
-    for k in range(1, lax.axis_size(axis)):
-        total = total + lax.ppermute(parts(x, k), axis, [(0, k)])
-    return total
 
 
 def flipped(x, axis, bits):
@@ -396,16 +399,20 @@
     corner_place = jnp.where(inside, p * WB + q, -1)
     holder = (row == 0) & (group == 0)
     info = jnp.stack([corner_place, holder.astype(jnp.int32)]).astype(jnp.int32)
+
+    first = parent_entries[:, :W].reshape(PR, FRONTS, COLS, 8, W)
+    sent = [lax.ppermute(first[:, :, k], "col", [(0, k)]) for k in range(1, COLS)]
+    sent[-1], info = lax.optimization_barrier((sent[-1], info))
+    first = jnp.where(col == 0, first[:, :, 0], (sent[0] + sent[1]) + sent[2])
+    sent = [lax.ppermute(first[:, k], "front", [(0, k)]) for k in range(1, FRONTS)]
+    first = jnp.where(front == 0, first[:, 0], (sent[0] + sent[1]) + sent[2])
+
     lead = make_lead(window[:, 0], info, local, parent_entries).reshape(128, 24, BLK)
     lead_recv = lax.all_to_all(lead, ALL, 0, 0, tiled=True)
     tiles = jnp.sum(lead_recv[:, 8:], axis=0)
     tiles = jnp.broadcast_to(tiles[None], (128, 16, BLK))
     tiles = lax.all_to_all(tiles, ALL, 0, 0, tiled=True)
     inverses = factor_inverse(tiles)
-
-    first = parent_entries[:, :W].reshape(PR, FRONTS, COLS, 8, W)
-    first = scatter_from_first(first, "col", lambda x, k: x[:, :, k])
-    first = scatter_from_first(first, "front", lambda x, k: x[:, k])
 
     column = group // 2 + 8 * (group % 2)
     by_row = lax.dynamic_index_in_dim(child_map.reshape(FRONTS, ROWS, 8), row, 2, keepdims=False)
@@ -420,19 +427,19 @@
 
     place = jnp.stack([row, group]).astype(jnp.int32)
 
-    rows_raw = lax.all_gather(slices.reshape(PR * 8, W), GRP, axis=0, tiled=True)
-    rows_raw = rows_raw.reshape(GROUPS, PR, 8, W)
+    pair = jnp.stack([slices, flipped(slices, "front", 2)])
+    pair = [pair] + [flipped(pair, "col", bits) for bits in range(1, COLS)]
+    rows_raw = pair + [flipped(x, "front", 1) for x in pair]
 
     even = group % 2 == 0
     one = lax.ppermute(jnp.where(even, slices[:PC], slices[PC:]), ALL, swap_pairs(0))
     two = lax.ppermute(jnp.where(even, slices[PC:], slices[:PC]), ALL, swap_pairs(1))
     mine = jnp.stack([jnp.where(even, one, two), jnp.where(even, two, one)], axis=1)
     mine = mine.reshape(PC, 16, W)
-    mine = jnp.stack([mine, flipped(mine, "row", 4)])
-    cols_raw = [mine] + [flipped(mine, "row", bits) for bits in range(1, 4)]
+    cols_raw = [mine] + [flipped(mine, "row", bits) for bits in range(1, ROWS)]
 
     packed = pack(window, local).reshape(128, BLK, BLK)
-    packed, cols_raw = lax.optimization_barrier((packed, cols_raw))
+    packed, cols_raw, rows_raw = lax.optimization_barrier((packed, cols_raw, rows_raw))
     recv = lax.all_to_all(packed, ALL, 0, 0, tiled=True)
 
     panel, high, low = make_panels(place, rows_raw, cols_raw, inverses)

time: 344 us -> 283 us (0.82)
  waiting for transfers between devices: 160 us -> 85.2 us
  starting transfers between devices: 56.4 us -> 80.7 us
  between operations: 16.9 us -> 3.38 us
  local copies, waits for them, and re-layouts: 24.9 us -> 35.4 us
  Pallas kernels: 71.7 us -> 67.4 us
    all_gather x1 -> x0, waiting for transfers between devices: 95.1 us -> none  [body(): lax.all_gather(slices.reshape(PR * 8, W), GRP, axis=0, tiled=True)]
    all_to_all x1, waiting for transfers between devices: 0.01 us -> 43.4 us  [body(): recv = lax.all_to_all(packed, ALL, 0, 0, tiled=True)]
    ppermute x4 -> x15, starting transfers between devices: 6.91 us -> 30.5 us  [flipped(): return lax.ppermute(x, axis, [(i, i ^ bits) for i in range(size)])]
    ppermute x6, waiting for transfers between devices: 40.6 us -> 25.8 us  [the longest x3 23.8 us: body(): lax.ppermute(first[:, :, k], 'col', [(0, k)])]
    unnamed x36 -> x72, local copies, waits for them, and re-layouts: 18.5 us -> 29.7 us
    ppermute x4 -> x15, waiting for transfers between devices: 23.9 us -> 16 us  [flipped(): return lax.ppermute(x, axis, [(i, i ^ bits) for i in range(size)])]
    pallas_call x1, Pallas kernels: 16.1 us -> 11.3 us  [finish(): pl.pallas_call(final_kernel, name='finish', grid_spec=pltpu.PrefetchScala...]
  transfers between devices with their start and end apart: 16 -> 26, of which waited for: 7 -> 7; matrix products, arithmetic and copies ran while one was open for 3% -> 4% of each run, Pallas kernels for 15% -> 19%
where the time goes in v4:
time: 283 us; the launch traced here: 279 us
  waiting for transfers between devices  85.2 us (30%)
  starting transfers between devices  80.7 us (29%)
  Pallas kernels  67.4 us (24%)
  local copies, waits for them, and re-layouts  35.4 us (13%)
  other arithmetic  7.33 us (3%)
  between operations  3.38 us (1%)
    all_to_all x1, waiting for transfers between devices, body(): recv = lax.all_to_all(packed, ALL, 0, 0, tiled=True)  43.4 us
    pallas_call x1, Pallas kernels, factor_inverse(): pl.pallas_call(factor_kernel, name='factor', in_specs=[vmem], out_specs=[...  33.5 us
    ppermute x15, starting transfers between devices, flipped(): return lax.ppermute(x, axis, [(i, i ^ bits) for i in range(size)])  30.5 us
    unnamed x72, local copies, waits for them, and re-layouts  29.7 us
    ppermute x3, waiting for transfers between devices, body(): lax.ppermute(first[:, :, k], 'col', [(0, k)])  23.8 us
    ppermute x15, waiting for transfers between devices, flipped(): return lax.ppermute(x, axis, [(i, i ^ bits) for i in range(size)])  16 us
    pallas_call x1, Pallas kernels, make_panels(): pl.pallas_call(panel_kernel, name='panels', grid_spec=pltpu.PrefetchScala...  14.6 us
    all_to_all x1, starting transfers between devices, body(): tiles = lax.all_to_all(tiles, ALL, 0, 0, tiled=True)  12.5 us
  transfers between devices with their start and end apart: 26, of which 7 were waited for; matrix products, arithmetic and copies ran while one was open for 4% of the time, Pallas kernels for 19%

profile of v4, /device:TPU:1, one launch (start us, length us, event | category | flops | bytes accessed | tf_op | source)
XLA Modules:
  0.0 279.4 jit_solution(18034010302593975114)
XLA Ops:
  3.8 6.5 %collective-permute-start = (f32[12,4,8,512]{3,2,0,1:T(8,128)S(1)}, f32[12,4,8,512]{3,2,0,1:T(8,128)S(1)}, u32[]{:S(2)}, u32[]{:S(2)}) collective-permute-start(f32[12,4,8,512]{3,2,0,1:T(8,128)S(1)} %bitcast.57), channel_id=1, source_target_pairs={{0,3},{4,7},{8,11},{12,15},{16,19},{20,23},{24,27},{28,31},{32,35}... | collective-permute-start | bytes 2359304 | tf_op jit(solution)/shard_map/ppermute | solution.py:404
  20.6 5.9 %collective-permute-done = f32[12,4,8,512]{3,2,0,1:T(8,128)S(1)} collective-permute-done((f32[12,4,8,512]{3,2,0,1:T(8,128)S(1)}, f32[12,4,8,512]{3,2,0,1:T(8,128)S(1)}, u32[]{:S(2)}, u32[]{:S(2)}) %collective-permute-start) | collective-permute-done | bytes 786464 | tf_op jit(solution)/shard_map/ppermute | solution.py:404
  26.5 3.4 %lead.1 = f32[4,8,4,24,128]{4,3,2,1,0:T(8,128)} custom-call(s32[8]{0:T(128)} %slice_reduce_fusion.1.keep_ref, s32[2]{0:T(128)} %pad_add_fusion.info_ref, f32[1024,2048]{1,0:T(8,128)} %bitcast.51, f32[1536,768]{1,0:T(8,128)} %refs_8_.1), custom_call_target="tpu_custom_call" | custom-call | tf_op jit(solution)/shard_map/lead/pallas_call | solution.py:72
  29.8 11.2 %all-to-all-start = ((f32[128,24,128]{2,1,0:T(8,128)}), f32[128,24,128]{2,1,0:T(8,128)S(1)}, u32[]{:S(2)}, u32[]{:S(2)}) async-start(f32[128,24,128]{2,1,0:T(8,128)} %bitcast.54), calls=%async_computation | async-start | bytes 3145728 | tf_op jit(solution)/shard_map/all_to_all | solution.py:411
  41.8 18.0 %collective-permute-done.2 = f32[12,4,8,512]{3,2,0,1:T(8,128)} collective-permute-done((f32[12,4,8,512]{3,2,0,1:T(8,128)}, f32[12,4,8,512]{3,2,0,1:T(8,128)}, u32[]{:S(2)}, u32[]{:S(2)}) %collective-permute-start.2) | collective-permute-done | bytes 786464 | tf_op jit(solution)/shard_map/ppermute | solution.py:404
  68.9 2.7 slices.1
  71.6 8.9 %collective-permute-start.15 = (f32[12,8,512]{2,1,0:T(8,128)}, f32[12,8,512]{2,1,0:T(8,128)S(1)}, u32[]{:S(2)}, u32[]{:S(2)}) collective-permute-start(f32[12,8,512]{2,1,0:T(8,128)} %slices.1), channel_id=1, source_target_pairs={{0,64},{32,96},{64,0},{96,32},{1,65},{33,97},{65,1},{97,33},{2,66}... | collective-permute-start | bytes 589832 | tf_op jit(solution)/shard_map/ppermute | solution.py:370
  81.5 3.6 %collective-permute-start.6 = (f32[6,8,512]{2,1,0:T(8,128)S(1)}, f32[6,8,512]{2,1,0:T(8,128)S(1)}, u32[]{:S(2)}, u32[]{:S(2)}) collective-permute-start(f32[6,8,512]{2,1,0:T(8,128)S(1)} %get-tuple-element.59), channel_id=1, source_target_pairs={{0,0},{1,1},{2,4},{3,5},{4,2},{5,3},{6,6},{7,7},{8,32},{9,33},{10,... | collective-permute-start | bytes 294920 | tf_op jit(solution)/shard_map/ppermute | solution.py:435
  87.6 12.5 %all-to-all-start.2 = ((f32[128,16,128]{2,1,0:T(8,128)}), f32[128,16,128]{2,1,0:T(8,128)S(1)}, u32[]{:S(2)}, u32[]{:S(2)}) async-start(f32[128,16,128]{2,1,0:T(8,128)} %broadcast_in_dim.56), calls=%async_computation.2 | async-start | bytes 2097152 | tf_op jit(solution)/shard_map/all_to_all | solution.py:414
  100.2 2.7 collective-permute-start.10
  102.9 2.7 collective-permute-start.11
  107.2 2.9 %collective-permute-start.17 = (f32[2,12,8,512]{3,2,1,0:T(8,128)S(1)}, f32[2,12,8,512]{3,2,1,0:T(8,128)S(1)}, u32[]{:S(2)}, u32[]{:S(2)}) collective-permute-start(f32[2,12,8,512]{3,2,1,0:T(8,128)S(1)} %pad_maximum_fusion.refs_0_), channel_id=1, source_target_pairs={{0,2},{1,3},{2,0},{3,1},{4,6},{5,7},{6,4},{7,5},{8,10},{9,11},{10,... | collective-permute-start | bytes 1179656 | tf_op jit(solution)/shard_map/ppermute | solution.py:370
  110.2 8.4 %collective-permute-done.10.refs_11_ = f32[6,16,512]{2,1,0:T(8,128)S(1)} collective-permute-done((f32[6,16,512]{2,1,0:T(8,128)S(1)}, f32[6,16,512]{2,1,0:T(8,128)S(1)}, u32[]{:S(2)}, u32[]{:S(2)}) %collective-permute-start.10) | collective-permute-done | bytes 196640 | tf_op jit(solution)/shard_map/ppermute | solution.py:370
  118.5 3.2 %collective-permute-start.18 = (f32[2,12,8,512]{3,2,1,0:T(8,128)S(1)}, f32[2,12,8,512]{3,2,1,0:T(8,128)S(1)}, u32[]{:S(2)}, u32[]{:S(2)}) collective-permute-start(f32[2,12,8,512]{3,2,1,0:T(8,128)S(1)} %pad_maximum_fusion.refs_0_), channel_id=1, source_target_pairs={{0,3},{1,2},{2,1},{3,0},{4,7},{5,6},{6,5},{7,4},{8,11},{9,10},{10,... | collective-permute-start | bytes 1179656 | tf_op jit(solution)/shard_map/ppermute | solution.py:370
  122.4 3.1 %collective-permute-start.13 = (f32[6,16,512]{2,1,0:T(8,128)S(1)}, f32[6,16,512]{2,1,0:T(8,128)S(1)}, u32[]{:S(2)}, u32[]{:S(2)}) collective-permute-start(f32[6,16,512]{2,1,0:T(8,128)S(1)} %copy_bitcast_fusion.4.refs_8_), channel_id=1, source_target_pairs={{0,24},{4,28},{8,16},{12,20},{16,8},{20,12},{24,0},{28,4},{1,25},{... | collective-permute-start | bytes 589832 | tf_op jit(solution)/shard_map/ppermute | solution.py:370
  127.9 3.8 %collective-permute-done.13.refs_14_ = f32[6,16,512]{2,1,0:T(8,128)S(1)} collective-permute-done((f32[6,16,512]{2,1,0:T(8,128)S(1)}, f32[6,16,512]{2,1,0:T(8,128)S(1)}, u32[]{:S(2)}, u32[]{:S(2)}) %collective-permute-start.13) | collective-permute-done | bytes 196640 | tf_op jit(solution)/shard_map/ppermute | solution.py:370
  132.4 3.8 %collective-permute-done.14.refs_15_ = f32[6,16,512]{2,1,0:T(8,128)S(1)} collective-permute-done((f32[6,16,512]{2,1,0:T(8,128)S(1)}, f32[6,16,512]{2,1,0:T(8,128)S(1)}, u32[]{:S(2)}, u32[]{:S(2)}) %collective-permute-start.14) | collective-permute-done | bytes 196640 | tf_op jit(solution)/shard_map/ppermute | solution.py:370
  140.6 3.4 %copy-done.2 = f32[1,1024,2048]{2,1,0:T(8,128)S(1)} copy-done((f32[1,1024,2048]{2,1,0:T(8,128)S(1)}, f32[1,1024,2048]{2,1,0:T(8,128)}, u32[]{:S(2)}) %copy-start.2) | copy-done | bytes 8388632
  146.0 3.3 %copy-done.3 = f32[4,8,4,128,128]{4,3,2,1,0:T(8,128)} copy-done((f32[4,8,4,128,128]{4,3,2,1,0:T(8,128)}, f32[4,8,4,128,128]{4,3,2,1,0:T(8,128)S(1)}, u32[]{:S(2)}) %copy-start.3) | copy-done | bytes 8388632
  152.3 9.2 %all-to-all-start.1 = ((f32[128,128,128]{2,1,0:T(8,128)}), f32[128,128,128]{2,1,0:T(8,128)}, u32[]{:S(2)}, u32[]{:S(2)}) async-start(f32[128,128,128]{2,1,0:T(8,128)} %bitcast.53), calls=%async_computation.1 | async-start | bytes 16777216 | tf_op jit(solution)/shard_map/all_to_all | solution.py:443
  161.8 33.5 %factor.1 = (bf16[512,512]{1,0:T(8,128)(2,1)S(1)}, bf16[512,512]{1,0:T(8,128)(2,1)S(1)}) custom-call(f32[128,16,128]{2,1,0:T(8,128)S(1)} %all-to-all-done.2.x_ref), custom_call_target="tpu_custom_call" | custom-call | tf_op jit(solution)/shard_map/factor/pallas_call | solution.py:222
  205.9 14.6 %panels.1 = (f32[1536,512]{1,0:T(8,128)}, bf16[768,512]{1,0:T(8,128)(2,1)S(1)}, bf16[768,512]{1,0:T(8,128)(2,1)S(1)}) custom-call(s32[2]{0:T(128)S(1)} %pad_add_fusion.1.place_ref, f32[2,12,8,512]{3,2,1,0:T(8,128)S(1)} %pad_maximum_fusion.refs_0_, f32[2,12,8,512]{3,2,1,0:T(8,128)S(1)} %collective-permute-done.16.refs_1_, ...), custom_call_target="tpu_custom_call" | custom-call | tf_op jit(solution)/shard_map/panels/pallas_call | solution.py:281
  220.5 43.4 %all-to-all-done.1.refs_0_.refs_1_.refs_2_.refs_3_.refs_4_.refs_5_.refs_6_.refs_7_ = f32[128,128,128]{2,1,0:T(8,128)} async-done(((f32[128,128,128]{2,1,0:T(8,128)}), f32[128,128,128]{2,1,0:T(8,128)}, u32[]{:S(2)}, u32[]{:S(2)}) %all-to-all-start.1) | async-done | bytes 8388640 | tf_op jit(solution)/shard_map/all_to_all | solution.py:443
  268.1 11.3 %finish.1 = f32[1536,768]{1,0:T(8,128)} custom-call(s32[4,12]{1,0:T(4,128)S(1)} %copy-done.27, s32[4,6]{1,0:T(4,128)S(1)} %broadcast_add_fusion.1.inv_col_ref, s32[2]{0:T(128)S(1)} %add_convert_fusion.lead_ref, f32[128,128,128]{2,1,0:T(8,128)} %all-to-all-done.1.refs_0_.refs_1_.refs_2_.refs_3_.refs_4_.refs_5_.refs_6_.refs_7_, ...), custom_call_target="tpu_custom_call" | custom-call | tf_op jit(solution)/shard_map/finish/pallas_call | solution.py:346
  (137 shorter events, 54.1 us)
Async XLA Ops:
  3.8 22.7 %collective-permute-start = (f32[12,4,8,512]{3,2,0,1:T(8,128)S(1)}, f32[12,4,8,512]{3,2,0,1:T(8,128)S(1)}, u32[]{:S(2)}, u32[]{:S(2)}) collective-permute-start(f32[12,4,8,512]{3,2,0,1:T(8,128)S(1)} %bitcast.57), channel_id=1, source_target_pairs={{0,3},{4,7},{8,11},{12,15},{16,19},{20,23},{24,27},{28,31},{32,35}... | collective-permute-start | bytes 2359304 | tf_op jit(solution)/shard_map/ppermute | solution.py:404
  10.4 31.4 %collective-permute-start.1 = (f32[12,4,8,512]{3,2,0,1:T(8,128)S(1)}, f32[12,4,8,512]{3,2,0,1:T(8,128)}, u32[]{:S(2)}, u32[]{:S(2)}) collective-permute-start(f32[12,4,8,512]{3,2,0,1:T(8,128)S(1)} %bitcast.56), channel_id=1, source_target_pairs={{0,1},{4,5},{8,9},{12,13},{16,17},{20,21},{24,25},{28,29},{32,33},... | collective-permute-start | bytes 2359304 | tf_op jit(solution)/shard_map/ppermute | solution.py:404
  13.5 46.3 %collective-permute-start.2 = (f32[12,4,8,512]{3,2,0,1:T(8,128)}, f32[12,4,8,512]{3,2,0,1:T(8,128)}, u32[]{:S(2)}, u32[]{:S(2)}) collective-permute-start(f32[12,4,8,512]{3,2,0,1:T(8,128)} %bitcast.47), channel_id=1, source_target_pairs={{0,2},{4,6},{8,10},{12,14},{16,18},{20,22},{24,26},{28,30},{32,34}... | collective-permute-start | bytes 2359304 | tf_op jit(solution)/shard_map/ppermute | solution.py:404
  29.8 37.9 %all-to-all-start = ((f32[128,24,128]{2,1,0:T(8,128)}), f32[128,24,128]{2,1,0:T(8,128)S(1)}, u32[]{:S(2)}, u32[]{:S(2)}) async-start(f32[128,24,128]{2,1,0:T(8,128)} %bitcast.54), calls=%async_computation | async-start | bytes 3145728 | tf_op jit(solution)/shard_map/all_to_all | solution.py:411
  61.8 5.2 %collective-permute-start.3 = (f32[12,8,512]{2,1,0:T(8,128)S(1)}, f32[12,8,512]{2,1,0:T(8,128)S(1)}, u32[]{:S(2)}, u32[]{:S(2)}) collective-permute-start(f32[12,8,512]{2,1,0:T(8,128)S(1)} %get-tuple-element.56), channel_id=1, source_target_pairs={{0,32},{1,33},{2,34},{3,35},{4,36},{5,37},{6,38},{7,39},{8,40},{9,... | collective-permute-start | bytes 589832 | tf_op jit(solution)/shard_map/ppermute | solution.py:407
  71.6 34.1 %collective-permute-start.15 = (f32[12,8,512]{2,1,0:T(8,128)}, f32[12,8,512]{2,1,0:T(8,128)S(1)}, u32[]{:S(2)}, u32[]{:S(2)}) collective-permute-start(f32[12,8,512]{2,1,0:T(8,128)} %slices.1), channel_id=1, source_target_pairs={{0,64},{32,96},{64,0},{96,32},{1,65},{33,97},{65,1},{97,33},{2,66}... | collective-permute-start | bytes 589832 | tf_op jit(solution)/shard_map/ppermute | solution.py:370
  81.5 18.7 %collective-permute-start.6 = (f32[6,8,512]{2,1,0:T(8,128)S(1)}, f32[6,8,512]{2,1,0:T(8,128)S(1)}, u32[]{:S(2)}, u32[]{:S(2)}) collective-permute-start(f32[6,8,512]{2,1,0:T(8,128)S(1)} %get-tuple-element.59), channel_id=1, source_target_pairs={{0,0},{1,1},{2,4},{3,5},{4,2},{5,3},{6,6},{7,7},{8,32},{9,33},{10,... | collective-permute-start | bytes 294920 | tf_op jit(solution)/shard_map/ppermute | solution.py:435
  85.1 15.1 %collective-permute-start.7 = (f32[6,8,512]{2,1,0:T(8,128)S(1)}, f32[6,8,512]{2,1,0:T(8,128)S(1)}, u32[]{:S(2)}, u32[]{:S(2)}) collective-permute-start(f32[6,8,512]{2,1,0:T(8,128)S(1)} %get-tuple-element.60), channel_id=1, source_target_pairs={{0,1},{1,0},{2,5},{3,4},{4,3},{5,2},{6,7},{7,6},{8,33},{9,32},{10,... | collective-permute-start | bytes 294920 | tf_op jit(solution)/shard_map/ppermute | solution.py:436
  87.6 64.7 %all-to-all-start.2 = ((f32[128,16,128]{2,1,0:T(8,128)}), f32[128,16,128]{2,1,0:T(8,128)S(1)}, u32[]{:S(2)}, u32[]{:S(2)}) async-start(f32[128,16,128]{2,1,0:T(8,128)} %broadcast_in_dim.56), calls=%async_computation.2 | async-start | bytes 2097152 | tf_op jit(solution)/shard_map/all_to_all | solution.py:414
  100.2 18.3 %collective-permute-start.10 = (f32[6,16,512]{2,1,0:T(8,128)S(1)}, f32[6,16,512]{2,1,0:T(8,128)S(1)}, u32[]{:S(2)}, u32[]{:S(2)}) collective-permute-start(f32[6,16,512]{2,1,0:T(8,128)S(1)} %copy_bitcast_fusion.4.refs_8_), channel_id=1, source_target_pairs={{0,12},{4,8},{8,4},{12,0},{16,28},{20,24},{24,20},{28,16},{1,13},{... | collective-permute-start | bytes 589832 | tf_op jit(solution)/shard_map/ppermute | solution.py:370
  102.9 18.8 %collective-permute-start.11 = (f32[6,16,512]{2,1,0:T(8,128)S(1)}, f32[6,16,512]{2,1,0:T(8,128)S(1)}, u32[]{:S(2)}, u32[]{:S(2)}) collective-permute-start(f32[6,16,512]{2,1,0:T(8,128)S(1)} %copy_bitcast_fusion.4.refs_8_), channel_id=1, source_target_pairs={{0,16},{4,20},{8,24},{12,28},{16,0},{20,4},{24,8},{28,12},{1,17},{... | collective-permute-start | bytes 589832 | tf_op jit(solution)/shard_map/ppermute | solution.py:370
  105.7 19.9 %collective-permute-start.12 = (f32[6,16,512]{2,1,0:T(8,128)S(1)}, f32[6,16,512]{2,1,0:T(8,128)S(1)}, u32[]{:S(2)}, u32[]{:S(2)}) collective-permute-start(f32[6,16,512]{2,1,0:T(8,128)S(1)} %copy_bitcast_fusion.4.refs_8_), channel_id=1, source_target_pairs={{0,20},{4,16},{8,28},{12,24},{16,4},{20,0},{24,12},{28,8},{1,21},{... | collective-permute-start | bytes 589832 | tf_op jit(solution)/shard_map/ppermute | solution.py:370
  105.7 33.3 %collective-permute-start.16 = (f32[2,12,8,512]{3,2,1,0:T(8,128)S(1)}, f32[2,12,8,512]{3,2,1,0:T(8,128)S(1)}, u32[]{:S(2)}, u32[]{:S(2)}) collective-permute-start(f32[2,12,8,512]{3,2,1,0:T(8,128)S(1)} %pad_maximum_fusion.refs_0_), channel_id=1, source_target_pairs={{0,1},{1,0},{2,3},{3,2},{4,5},{5,4},{6,7},{7,6},{8,9},{9,8},{10,11... | collective-permute-start | bytes 1179656 | tf_op jit(solution)/shard_map/ppermute | solution.py:370
  107.2 31.7 %collective-permute-start.17 = (f32[2,12,8,512]{3,2,1,0:T(8,128)S(1)}, f32[2,12,8,512]{3,2,1,0:T(8,128)S(1)}, u32[]{:S(2)}, u32[]{:S(2)}) collective-permute-start(f32[2,12,8,512]{3,2,1,0:T(8,128)S(1)} %pad_maximum_fusion.refs_0_), channel_id=1, source_target_pairs={{0,2},{1,3},{2,0},{3,1},{4,6},{5,7},{6,4},{7,5},{8,10},{9,11},{10,... | collective-permute-start | bytes 1179656 | tf_op jit(solution)/shard_map/ppermute | solution.py:370
  118.5 21.0 %collective-permute-start.18 = (f32[2,12,8,512]{3,2,1,0:T(8,128)S(1)}, f32[2,12,8,512]{3,2,1,0:T(8,128)S(1)}, u32[]{:S(2)}, u32[]{:S(2)}) collective-permute-start(f32[2,12,8,512]{3,2,1,0:T(8,128)S(1)} %pad_maximum_fusion.refs_0_), channel_id=1, source_target_pairs={{0,3},{1,2},{2,1},{3,0},{4,7},{5,6},{6,5},{7,4},{8,11},{9,10},{10,... | collective-permute-start | bytes 1179656 | tf_op jit(solution)/shard_map/ppermute | solution.py:370
  122.4 9.3 %collective-permute-start.13 = (f32[6,16,512]{2,1,0:T(8,128)S(1)}, f32[6,16,512]{2,1,0:T(8,128)S(1)}, u32[]{:S(2)}, u32[]{:S(2)}) collective-permute-start(f32[6,16,512]{2,1,0:T(8,128)S(1)} %copy_bitcast_fusion.4.refs_8_), channel_id=1, source_target_pairs={{0,24},{4,28},{8,16},{12,20},{16,8},{20,12},{24,0},{28,4},{1,25},{... | collective-permute-start | bytes 589832 | tf_op jit(solution)/shard_map/ppermute | solution.py:370
  126.2 10.0 %collective-permute-start.14 = (f32[6,16,512]{2,1,0:T(8,128)S(1)}, f32[6,16,512]{2,1,0:T(8,128)S(1)}, u32[]{:S(2)}, u32[]{:S(2)}) collective-permute-start(f32[6,16,512]{2,1,0:T(8,128)S(1)} %copy_bitcast_fusion.4.refs_8_), channel_id=1, source_target_pairs={{0,28},{4,24},{8,20},{12,16},{16,12},{20,8},{24,4},{28,0},{1,29},{... | collective-permute-start | bytes 589832 | tf_op jit(solution)/shard_map/ppermute | solution.py:370
  132.4 7.8 %collective-permute-start.8 = (f32[6,16,512]{2,1,0:T(8,128)S(1)}, f32[6,16,512]{2,1,0:T(8,128)S(1)}, u32[]{:S(2)}, u32[]{:S(2)}) collective-permute-start(f32[6,16,512]{2,1,0:T(8,128)S(1)} %copy_bitcast_fusion.4.refs_8_), channel_id=1, source_target_pairs={{0,4},{4,0},{8,12},{12,8},{16,20},{20,16},{24,28},{28,24},{1,5},{5... | collective-permute-start | bytes 589832 | tf_op jit(solution)/shard_map/ppermute | solution.py:370
  136.9 13.1 %collective-permute-start.19 = (f32[2,12,8,512]{3,2,1,0:T(8,128)S(1)}, f32[2,12,8,512]{3,2,1,0:T(8,128)S(1)}, u32[]{:S(2)}, u32[]{:S(2)}) collective-permute-start(f32[2,12,8,512]{3,2,1,0:T(8,128)S(1)} %pad_maximum_fusion.refs_0_), channel_id=1, source_target_pairs={{0,32},{32,0},{64,96},{96,64},{1,33},{33,1},{65,97},{97,65},{2,34}... | collective-permute-start | bytes 1179656 | tf_op jit(solution)/shard_map/ppermute | solution.py:370
  139.0 11.0 %collective-permute-start.20 = (f32[2,12,8,512]{3,2,1,0:T(8,128)S(1)}, f32[2,12,8,512]{3,2,1,0:T(8,128)S(1)}, u32[]{:S(2)}, u32[]{:S(2)}) collective-permute-start(f32[2,12,8,512]{3,2,1,0:T(8,128)S(1)} %collective-permute-done.16.refs_1_), channel_id=1, source_target_pairs={{0,32},{32,0},{64,96},{96,64},{1,33},{33,1},{65,97},{97,65},{2,34}... | collective-permute-start | bytes 1179656 | tf_op jit(solution)/shard_map/ppermute | solution.py:370
  139.0 11.8 %collective-permute-start.21 = (f32[2,12,8,512]{3,2,1,0:T(8,128)S(1)}, f32[2,12,8,512]{3,2,1,0:T(8,128)S(1)}, u32[]{:S(2)}, u32[]{:S(2)}) collective-permute-start(f32[2,12,8,512]{3,2,1,0:T(8,128)S(1)} %collective-permute-done.17.refs_2_), channel_id=1, source_target_pairs={{0,32},{32,0},{64,96},{96,64},{1,33},{33,1},{65,97},{97,65},{2,34}... | collective-permute-start | bytes 1179656 | tf_op jit(solution)/shard_map/ppermute | solution.py:370
  139.5 12.0 %collective-permute-start.22 = (f32[2,12,8,512]{3,2,1,0:T(8,128)S(1)}, f32[2,12,8,512]{3,2,1,0:T(8,128)S(1)}, u32[]{:S(2)}, u32[]{:S(2)}) collective-permute-start(f32[2,12,8,512]{3,2,1,0:T(8,128)S(1)} %collective-permute-done.18.refs_3_), channel_id=1, source_target_pairs={{0,32},{32,0},{64,96},{96,64},{1,33},{33,1},{65,97},{97,65},{2,34}... | collective-permute-start | bytes 1179656 | tf_op jit(solution)/shard_map/ppermute | solution.py:370
  140.2 9.1 %collective-permute-start.9 = (f32[6,16,512]{2,1,0:T(8,128)S(1)}, f32[6,16,512]{2,1,0:T(8,128)S(1)}, u32[]{:S(2)}, u32[]{:S(2)}) collective-permute-start(f32[6,16,512]{2,1,0:T(8,128)S(1)} %copy_bitcast_fusion.4.refs_8_), channel_id=1, source_target_pairs={{0,8},{4,12},{8,0},{12,4},{16,24},{20,28},{24,16},{28,20},{1,9},{5... | collective-permute-start | bytes 589832 | tf_op jit(solution)/shard_map/ppermute | solution.py:370
  152.3 111.7 %all-to-all-start.1 = ((f32[128,128,128]{2,1,0:T(8,128)}), f32[128,128,128]{2,1,0:T(8,128)}, u32[]{:S(2)}, u32[]{:S(2)}) async-start(f32[128,128,128]{2,1,0:T(8,128)} %bitcast.53), calls=%async_computation.1 | async-start | bytes 16777216 | tf_op jit(solution)/shard_map/all_to_all | solution.py:443
  (36 other events, 218.4 us)

commit v5 on v3

--- a/solution.py
+++ b/solution.py
@@ -243,108 +243,119 @@
     return (product(x_high, low) + product(x_low, high)) + product(x_high, high)
 
 
-def panel_kernel(place_ref, rows_ref, *refs):
-    cols = refs[:4]
-    inverse_high, inverse_low, panel_ref, high_ref, low_ref, block_ref = refs[4:]
-    step = pl.program_id(0)
-
-    def times_inverse(x):
-        return three_products(x, inverse_high[...], inverse_low[...])
-
-    @pl.when(step < PR)
-    def _():
-        panel_ref[...] = times_inverse(rows_ref[:, 0].reshape(BLK, W))
-
-    @pl.when(step >= PR)
-    def _():
-        for other in range(4):
-            for slot in range(2):
-                source = place_ref[0] ^ (slot * 4 + other)
-                start = pl.multiple_of(source * 16, 16)
-                block_ref[pl.ds(start, 16), :] = cols[other][slot, 0]
-        value = times_inverse(block_ref[...])
-        high_ref[...], low_ref[...] = split(value)
-
-
-def make_panels(place, rows_raw, cols_raw, inverses):
-    def in_rows(i):
-        return jnp.minimum(i, PR - 1)
-
-    def in_cols(i):
-        return jnp.maximum(i - PR, 0)
-
+def rows_kernel(rows_ref, high_ref, low_ref, o_ref):
+    o_ref[...] = three_products(rows_ref[:, 0].reshape(BLK, W), high_ref[...], low_ref[...])
+
+
+def make_panel(rows_raw, inverses):
+    whole = pl.BlockSpec((W, W), lambda i: (0, 0))
+    return pl.pallas_call(
+        rows_kernel,
+        name="panel",
+        grid=(PR,),
+        in_specs=[pl.BlockSpec((GROUPS, 1, 8, W), lambda i: (0, i, 0, 0)), whole, whole],
+        out_specs=pl.BlockSpec((BLK, W), lambda i: (i, 0)),
+        out_shape=jax.ShapeDtypeStruct((PR * BLK, W), jnp.float32),
+    )(rows_raw, *inverses)
+
+
+def cols_kernel(place_ref, *refs):
+    pieces = refs[:ROWS]
+    inverse_high, inverse_low, high_ref, low_ref, block_ref = refs[ROWS:]
+    for other in range(ROWS):
+        start = pl.multiple_of((place_ref[0] ^ other) * 16, 16)
+        block_ref[pl.ds(start, 16), :] = pieces[other][0]
+    high_ref[...], low_ref[...] = split(
+        three_products(block_ref[...], inverse_high[...], inverse_low[...])
+    )
+
+
+def make_across(place, pieces, inverses):
     half = jax.ShapeDtypeStruct((PC * BLK, W), jnp.bfloat16)
-    return pl.pallas_call(
-        panel_kernel,
-        name="panels",
+    whole = pl.BlockSpec((W, W), lambda i, p: (0, 0))
+    block = pl.BlockSpec((BLK, W), lambda i, p: (i, 0))
+    return pl.pallas_call(
+        cols_kernel,
+        name="across",
         grid_spec=pltpu.PrefetchScalarGridSpec(
             num_scalar_prefetch=1,
-            grid=(PR + PC,),
-            in_specs=[pl.BlockSpec((GROUPS, 1, 8, W), lambda i, p: (0, in_rows(i), 0, 0))]
-            + [pl.BlockSpec((2, 1, 16, W), lambda i, p: (0, in_cols(i), 0, 0))] * 4
-            + [pl.BlockSpec((W, W), lambda i, p: (0, 0))] * 2,
-            out_specs=[
-                pl.BlockSpec((BLK, W), lambda i, p: (in_rows(i), 0)),
-                pl.BlockSpec((BLK, W), lambda i, p: (in_cols(i), 0)),
-                pl.BlockSpec((BLK, W), lambda i, p: (in_cols(i), 0)),
-            ],
+            grid=(PC,),
+            in_specs=[pl.BlockSpec((1, 16, W), lambda i, p: (i, 0, 0))] * ROWS + [whole, whole],
+            out_specs=[block, block],
             scratch_shapes=[pltpu.VMEM((BLK, W), jnp.float32)],
         ),
-        out_shape=[jax.ShapeDtypeStruct((PR * BLK, W), jnp.float32), half, half],
-        compiler_params=pltpu.CompilerParams(vmem_limit_bytes=32 << 20),
-    )(place, rows_raw, *cols_raw, *inverses)
-
-
-def final_kernel(inv_row_ref, inv_col_ref, lead_ref, *refs):
+        out_shape=[half, half],
+    )(place, *pieces, *inverses)
+
+
+def assemble_kernel(inv_row_ref, inv_col_ref, *refs):
     recvs = refs[:FRONTS]
-    parent_ref, panel_ref, high_ref, low_ref, o_ref = refs[FRONTS:]
+    parent_ref, o_ref = refs[FRONTS:]
     a = pl.program_id(0)
-    o_ref[...] = parent_ref[...] - three_products(panel_ref[...], high_ref[...], low_ref[...])
     for b in range(PC):
         span = slice(b * BLK, (b + 1) * BLK)
-        total = o_ref[:, span]
+        total = parent_ref[:, span]
         for front in range(FRONTS):
             r = inv_row_ref[front, a]
             c = inv_col_ref[front, b]
             ok = jnp.logical_and(r >= 0, c >= 0).astype(jnp.float32)
             total = total + recvs[front][jnp.maximum(c, 0)] * ok
         o_ref[:, span] = total
-    leading_row = jnp.logical_and(lead_ref[0] == 1, a < WB)
-
-    @pl.when(leading_row)
-    def _():
-        o_ref[...] = jnp.zeros_like(o_ref)
-
-    @pl.when(lead_ref[1] == 1)
-    def _():
-        o_ref[:, :W] = jnp.zeros((BLK, W), jnp.float32)
-
-
-def finish(inv_row, inv_col, lead, recv, parent, panel, high, low):
+
+
+def assemble(inv_row, inv_col, recv, parent):
     def recv_map(front):
-        return lambda a, ir, ic, ld: (front * ROWS + jnp.maximum(ir[front, a], 0), 0, 0)
-
-    whole = pl.BlockSpec((PC * BLK, W), lambda a, *_: (0, 0))
-    return pl.pallas_call(
-        final_kernel,
-        name="finish",
+        return lambda a, ir, ic: (front * ROWS + jnp.maximum(ir[front, a], 0), 0, 0)
+
+    block = pl.BlockSpec((BLK, PC * BLK), lambda a, *_: (a, 0))
+    return pl.pallas_call(
+        assemble_kernel,
+        name="assemble",
         grid_spec=pltpu.PrefetchScalarGridSpec(
-            num_scalar_prefetch=3,
+            num_scalar_prefetch=2,
             grid=(PR,),
             in_specs=[
                 pl.BlockSpec((COLS, BLK, BLK), recv_map(front)) for front in range(FRONTS)
             ]
-            + [
-                pl.BlockSpec((BLK, PC * BLK), lambda a, *_: (a, 0)),
-                pl.BlockSpec((BLK, W), lambda a, *_: (a, 0)),
-                whole,
-                whole,
-            ],
-            out_specs=pl.BlockSpec((BLK, PC * BLK), lambda a, *_: (a, 0)),
+            + [block],
+            out_specs=block,
         ),
         out_shape=jax.ShapeDtypeStruct((PR * BLK, PC * BLK), jnp.float32),
-        compiler_params=pltpu.CompilerParams(vmem_limit_bytes=40 << 20),
-    )(inv_row, inv_col, lead, recv, recv, recv, recv, parent, panel, high, low)
+        compiler_params=pltpu.CompilerParams(vmem_limit_bytes=32 << 20),
+    )(inv_row, inv_col, recv, recv, recv, recv, parent)
+
+
+def subtract_kernel(place_ref, whole_ref, panel_ref, high_ref, low_ref, o_ref):
+    step = pl.program_id(0)
+    blocks = o_ref.shape[0] // BLK
+    o_ref[...] = whole_ref[...] - three_products(panel_ref[...], high_ref[...], low_ref[...])
+
+    @pl.when(jnp.logical_and(place_ref[0] == 0, step < WB // blocks))
+    def _():
+        o_ref[...] = jnp.zeros_like(o_ref)
+
+    @pl.when(place_ref[1] == 0)
+    def _():
+        o_ref[:, :W] = jnp.zeros((o_ref.shape[0], W), jnp.float32)
+
+
+def subtract(place, whole, panel, high, low):
+    tall = 2 * BLK
+    block = pl.BlockSpec((tall, PC * BLK), lambda a, p: (a, 0))
+    half = pl.BlockSpec((PC * BLK, W), lambda a, p: (0, 0))
+    return pl.pallas_call(
+        subtract_kernel,
+        name="subtract",
+        grid_spec=pltpu.PrefetchScalarGridSpec(
+            num_scalar_prefetch=1,
+            grid=(PR * BLK // tall,),
+            in_specs=[block, pl.BlockSpec((tall, W), lambda a, p: (a, 0)), half, half],
+            out_specs=block,
+        ),
+        out_shape=jax.ShapeDtypeStruct((PR * BLK, PC * BLK), jnp.float32),
+        input_output_aliases={1: 0},
+        compiler_params=pltpu.CompilerParams(vmem_limit_bytes=32 << 20),
+    )(place, whole, panel, high, low)
 
 
 def inverse_places(places, length):
@@ -352,14 +363,6 @@
     hits = places[:, :, None] == jnp.arange(length, dtype=jnp.int32)
     order = jnp.arange(1, count + 1, dtype=jnp.int32)[None, :, None]
     return jnp.sum(jnp.where(hits, order, 0), axis=1) - 1
-
-
-def scatter_from_first(x, axis, parts):
-    index = lax.axis_index(axis)
-    total = jnp.where(index == 0, parts(x, 0), 0.0)
-    for k in range(1, lax.axis_size(axis)):
-        total = total + lax.ppermute(parts(x, k), axis, [(0, k)])
-    return total
 
 
 def flipped(x, axis, bits):
@@ -396,16 +399,17 @@
     corner_place = jnp.where(inside, p * WB + q, -1)
     holder = (row == 0) & (group == 0)
     info = jnp.stack([corner_place, holder.astype(jnp.int32)]).astype(jnp.int32)
+    first = parent_entries[:, :W].reshape(PR, FRONTS, COLS, 8, W)
+    sent = [lax.ppermute(first[:, :, k], "col", [(0, k)]) for k in range(1, COLS)]
+    sent[-1], info = lax.optimization_barrier((sent[-1], info))
     lead = make_lead(window[:, 0], info, local, parent_entries).reshape(128, 24, BLK)
     lead_recv = lax.all_to_all(lead, ALL, 0, 0, tiled=True)
+    first = jnp.where(col == 0, first[:, :, 0], (sent[0] + sent[1]) + sent[2])
     tiles = jnp.sum(lead_recv[:, 8:], axis=0)
     tiles = jnp.broadcast_to(tiles[None], (128, 16, BLK))
     tiles = lax.all_to_all(tiles, ALL, 0, 0, tiled=True)
-    inverses = factor_inverse(tiles)
-
-    first = parent_entries[:, :W].reshape(PR, FRONTS, COLS, 8, W)
-    first = scatter_from_first(first, "col", lambda x, k: x[:, :, k])
-    first = scatter_from_first(first, "front", lambda x, k: x[:, k])
+    sent = [lax.ppermute(first[:, k], "front", [(0, k)]) for k in range(1, FRONTS)]
+    first = jnp.where(front == 0, first[:, 0], (sent[0] + sent[1]) + sent[2])
 
     column = group // 2 + 8 * (group % 2)
     by_row = lax.dynamic_index_in_dim(child_map.reshape(FRONTS, ROWS, 8), row, 2, keepdims=False)
@@ -420,24 +424,27 @@
 
     place = jnp.stack([row, group]).astype(jnp.int32)
 
-    rows_raw = lax.all_gather(slices.reshape(PR * 8, W), GRP, axis=0, tiled=True)
-    rows_raw = rows_raw.reshape(GROUPS, PR, 8, W)
-
     even = group % 2 == 0
     one = lax.ppermute(jnp.where(even, slices[:PC], slices[PC:]), ALL, swap_pairs(0))
     two = lax.ppermute(jnp.where(even, slices[PC:], slices[:PC]), ALL, swap_pairs(1))
     mine = jnp.stack([jnp.where(even, one, two), jnp.where(even, two, one)], axis=1)
     mine = mine.reshape(PC, 16, W)
-    mine = jnp.stack([mine, flipped(mine, "row", 4)])
-    cols_raw = [mine] + [flipped(mine, "row", bits) for bits in range(1, 4)]
+
+    rows_raw = lax.all_gather(slices.reshape(PR * 8, W), GRP, axis=0, tiled=True)
+    rows_raw = rows_raw.reshape(GROUPS, PR, 8, W)
 
     packed = pack(window, local).reshape(128, BLK, BLK)
-    packed, cols_raw = lax.optimization_barrier((packed, cols_raw))
+    packed, mine, tiles = lax.optimization_barrier((packed, mine, tiles))
     recv = lax.all_to_all(packed, ALL, 0, 0, tiled=True)
 
-    panel, high, low = make_panels(place, rows_raw, cols_raw, inverses)
-    lead_flags = jnp.stack([row == 0, group == 0]).astype(jnp.int32)
-    schur = finish(inv_row, inv_col, lead_flags, recv, parent_entries, panel, high, low)
+    inverses = factor_inverse(tiles)
+    mine, *inverses = lax.optimization_barrier((mine, *inverses))
+    pieces = [mine] + [flipped(mine, "row", bits) for bits in range(1, ROWS)]
+    whole = assemble(inv_row, inv_col, recv, parent_entries)
+    *pieces, rows_raw, whole = lax.optimization_barrier((*pieces, rows_raw, whole))
+    panel = make_panel(rows_raw, inverses)
+    high, low = make_across(place, pieces, inverses)
+    schur = subtract(place, whole, panel, high, low)
     return schur, panel
 
 

time: 344 us -> 329 us (0.956); the launches traced: 337 us -> 326 us
  waiting for transfers between devices: 160 us -> 125 us
  starting transfers between devices: 56.4 us -> 72.9 us
  Pallas kernels: 71.7 us -> 80.7 us
    all_gather x1, waiting for transfers between devices: 95.1 us -> 7.3 us  [body(): lax.all_gather(slices.reshape(PR * 8, W), GRP, axis=0, tiled=True)]
    ppermute x4 -> x7, waiting for transfers between devices: 23.9 us -> 54.5 us  [flipped(): return lax.ppermute(x, axis, [(i, i ^ bits) for i in range(size)])]
    ppermute x6, waiting for transfers between devices: 40.6 us -> 54.1 us  [the longest x3 54.1 us: body(): lax.ppermute(first[:, :, k], 'col', [(0, k)])]
    pallas_call x2 -> x4, Pallas kernels: 30.2 us -> 39.1 us  [the longest x1 11.9 us: make_panel(): pl.pallas_call(rows_kernel, name='panel', grid=(PR,), in_specs=[pl.BlockS...]
    ppermute x4 -> x7, starting transfers between devices: 6.91 us -> 15.1 us  [flipped(): return lax.ppermute(x, axis, [(i, i ^ bits) for i in range(size)])]
    all_to_all x1, waiting for transfers between devices: 0.01 us -> 8.1 us  [body(): recv = lax.all_to_all(packed, ALL, 0, 0, tiled=True)]
    ppermute x6, starting transfers between devices: 13.2 us -> 17.3 us  [the longest x3 13.3 us: body(): lax.ppermute(first[:, :, k], 'col', [(0, k)])]
    select_n x0 -> x2, other arithmetic: none -> 3.82 us  [the longest x1 1.96 us: body(): first = jnp.where(col == 0, first[:, :, 0], sent[0] + sent[1] + sent[2])]
  transfers between devices with their start and end apart: 16 -> 19, of which waited for: 7 -> 7; matrix products, arithmetic and copies ran while one was open for 3% -> 4% of each run, Pallas kernels for 15% -> 15%
where the time goes in v5:
time: 329 us; the launch traced here: 326 us
  waiting for transfers between devices  125 us (38%)
  Pallas kernels  80.7 us (25%)
  starting transfers between devices  72.9 us (22%)
  local copies, waits for them, and re-layouts  23.2 us (7%)
  between operations  16.8 us (5%)
  other arithmetic  7.65 us (2%)
    ppermute x7, waiting for transfers between devices, flipped(): return lax.ppermute(x, axis, [(i, i ^ bits) for i in range(size)])  54.5 us
    ppermute x3, waiting for transfers between devices, body(): lax.ppermute(first[:, :, k], 'col', [(0, k)])  54.1 us
    pallas_call x1, Pallas kernels, factor_inverse(): pl.pallas_call(factor_kernel, name='factor', in_specs=[vmem], out_specs=[...  33.5 us
    unnamed x54, local copies, waits for them, and re-layouts  16.2 us
    ppermute x7, starting transfers between devices, flipped(): return lax.ppermute(x, axis, [(i, i ^ bits) for i in range(size)])  15.1 us
    ppermute x3, starting transfers between devices, body(): lax.ppermute(first[:, :, k], 'col', [(0, k)])  13.3 us
    all_to_all x1, starting transfers between devices, body(): tiles = lax.all_to_all(tiles, ALL, 0, 0, tiled=True)  12.3 us
    pallas_call x1, Pallas kernels, make_panel(): pl.pallas_call(rows_kernel, name='panel', grid=(PR,), in_specs=[pl.BlockS...  11.9 us
  transfers between devices with their start and end apart: 19, of which 7 were waited for; matrix products, arithmetic and copies ran while one was open for 4% of the time, Pallas kernels for 15%

profile of v5, /device:TPU:1, one launch (start us, length us, event | category | flops | bytes accessed | tf_op | source)
XLA Modules:
  0.0 326.0 jit_solution(12462134043222330129)
XLA Ops:
  10.6 6.5 %collective-permute-start = (f32[12,4,8,512]{3,2,0,1:T(8,128)S(1)}, f32[12,4,8,512]{3,2,0,1:T(8,128)S(1)}, u32[]{:S(2)}, u32[]{:S(2)}) collective-permute-start(f32[12,4,8,512]{3,2,0,1:T(8,128)S(1)} %bitcast.55), channel_id=1, source_target_pairs={{0,3},{4,7},{8,11},{12,15},{16,19},{20,23},{24,27},{28,31},{32,35}... | collective-permute-start | bytes 2359304 | tf_op jit(solution)/shard_map/ppermute | solution.py:403
  21.9 11.4 %collective-permute-done = f32[12,4,8,512]{3,2,0,1:T(8,128)S(1)} collective-permute-done((f32[12,4,8,512]{3,2,0,1:T(8,128)S(1)}, f32[12,4,8,512]{3,2,0,1:T(8,128)S(1)}, u32[]{:S(2)}, u32[]{:S(2)}) %collective-permute-start) | collective-permute-done | bytes 786464 | tf_op jit(solution)/shard_map/ppermute | solution.py:403
  33.3 3.4 %lead.1 = f32[4,8,4,24,128]{4,3,2,1,0:T(8,128)} custom-call(s32[8]{0:T(128)} %slice_reduce_fusion.1.keep_ref, s32[2]{0:T(128)} %pad_add_fusion.1.info_ref, f32[1024,2048]{1,0:T(8,128)} %bitcast.48, f32[1536,768]{1,0:T(8,128)} %refs_4_.1), custom_call_target="tpu_custom_call" | custom-call | tf_op jit(solution)/shard_map/lead/pallas_call | solution.py:72
  36.7 11.2 %all-to-all-start = ((f32[128,24,128]{2,1,0:T(8,128)}), f32[128,24,128]{2,1,0:T(8,128)S(1)}, u32[]{:S(2)}, u32[]{:S(2)}) async-start(f32[128,24,128]{2,1,0:T(8,128)} %bitcast.52), calls=%async_computation | async-start | bytes 3145728 | tf_op jit(solution)/shard_map/all_to_all | solution.py:406
  48.9 4.3 %collective-permute-start.1 = (f32[12,4,8,512]{3,2,0,1:T(8,128)}, f32[12,4,8,512]{3,2,0,1:T(8,128)}, u32[]{:S(2)}, u32[]{:S(2)}) collective-permute-start(f32[12,4,8,512]{3,2,0,1:T(8,128)} %bitcast.46), channel_id=1, source_target_pairs={{0,1},{4,5},{8,9},{12,13},{16,17},{20,21},{24,25},{28,29},{32,33},... | collective-permute-start | bytes 2359304 | tf_op jit(solution)/shard_map/ppermute | solution.py:403
  56.7 25.9 %collective-permute-done.1 = f32[12,4,8,512]{3,2,0,1:T(8,128)} collective-permute-done((f32[12,4,8,512]{3,2,0,1:T(8,128)}, f32[12,4,8,512]{3,2,0,1:T(8,128)}, u32[]{:S(2)}, u32[]{:S(2)}) %collective-permute-start.1) | collective-permute-done | bytes 786464 | tf_op jit(solution)/shard_map/ppermute | solution.py:403
  82.7 16.7 %collective-permute-done.2 = f32[12,4,8,512]{3,2,0,1:T(8,128)S(1)} collective-permute-done((f32[12,4,8,512]{3,2,0,1:T(8,128)S(1)}, f32[12,4,8,512]{3,2,0,1:T(8,128)S(1)}, u32[]{:S(2)}, u32[]{:S(2)}) %collective-permute-start.2) | collective-permute-done | bytes 786464 | tf_op jit(solution)/shard_map/ppermute | solution.py:403
  107.6 12.3 %all-to-all-start.1 = ((f32[128,16,128]{2,1,0:T(8,128)}), f32[128,16,128]{2,1,0:T(8,128)S(1)}, u32[]{:S(2)}, u32[]{:S(2)}) async-start(f32[128,16,128]{2,1,0:T(8,128)} %broadcast_in_dim.54), calls=%async_computation.1 | async-start | bytes 2097152 | tf_op jit(solution)/shard_map/all_to_all | solution.py:410
  122.3 2.7 slices.1
  126.0 5.1 %collective-permute-start.6 = (f32[6,8,512]{2,1,0:T(8,128)S(1)}, f32[6,8,512]{2,1,0:T(8,128)S(1)}, u32[]{:S(2)}, u32[]{:S(2)}) collective-permute-start(f32[6,8,512]{2,1,0:T(8,128)S(1)} %get-tuple-element.55), channel_id=1, source_target_pairs={{0,0},{1,1},{2,4},{3,5},{4,2},{5,3},{6,6},{7,7},{8,32},{9,33},{10,... | collective-permute-start | bytes 294920 | tf_op jit(solution)/shard_map/ppermute | solution.py:428
  132.5 3.4 %copy-done.1 = f32[1,1024,2048]{2,1,0:T(8,128)S(1)} copy-done((f32[1,1024,2048]{2,1,0:T(8,128)S(1)}, f32[1,1024,2048]{2,1,0:T(8,128)}, u32[]{:S(2)}) %copy-start.1) | copy-done | bytes 8388632
  137.8 3.2 copy-done.2
  141.1 10.6 %all-to-all-start.2 = ((f32[128,128,128]{2,1,0:T(8,128)}), f32[128,128,128]{2,1,0:T(8,128)}, u32[]{:S(2)}, u32[]{:S(2)}) async-start(f32[128,128,128]{2,1,0:T(8,128)} %bitcast.50), calls=%async_computation.2 | async-start | bytes 16777216 | tf_op jit(solution)/shard_map/all_to_all | solution.py:438
  152.5 33.5 %factor.1 = (bf16[512,512]{1,0:T(8,128)(2,1)S(1)}, bf16[512,512]{1,0:T(8,128)(2,1)S(1)}) custom-call(f32[128,16,128]{2,1,0:T(8,128)S(1)} %all-to-all-done.1.x_ref), custom_call_target="tpu_custom_call" | custom-call | tf_op jit(solution)/shard_map/factor/pallas_call | solution.py:222
  190.3 2.7 collective-permute-start.11
  193.8 3.8 %collective-permute-start.13 = (f32[6,16,512]{2,1,0:T(8,128)S(1)}, f32[6,16,512]{2,1,0:T(8,128)S(1)}, u32[]{:S(2)}, u32[]{:S(2)}) collective-permute-start(f32[6,16,512]{2,1,0:T(8,128)S(1)} %copy_bitcast_fusion.4.refs_0_), channel_id=1, source_target_pairs={{0,24},{4,28},{8,16},{12,20},{16,8},{20,12},{24,0},{28,4},{1,25},{... | collective-permute-start | bytes 589832 | tf_op jit(solution)/shard_map/ppermute | solution.py:370
  200.0 53.7 %collective-permute-done.10.refs_3_ = f32[6,16,512]{2,1,0:T(8,128)S(1)} collective-permute-done((f32[6,16,512]{2,1,0:T(8,128)S(1)}, f32[6,16,512]{2,1,0:T(8,128)S(1)}, u32[]{:S(2)}, u32[]{:S(2)}) %collective-permute-start.10) | collective-permute-done | bytes 196640 | tf_op jit(solution)/shard_map/ppermute | solution.py:370
  254.5 3.4 %collective-permute-start.9 = (f32[6,16,512]{2,1,0:T(8,128)S(1)}, f32[6,16,512]{2,1,0:T(8,128)S(1)}, u32[]{:S(2)}, u32[]{:S(2)}) collective-permute-start(f32[6,16,512]{2,1,0:T(8,128)S(1)} %copy_bitcast_fusion.4.refs_0_), channel_id=1, source_target_pairs={{0,8},{4,12},{8,0},{12,4},{16,24},{20,28},{24,16},{28,20},{1,9},{5... | collective-permute-start | bytes 589832 | tf_op jit(solution)/shard_map/ppermute | solution.py:370
  257.9 8.1 %all-to-all-done.2.refs_0_.refs_1_.refs_2_.refs_3_ = f32[128,128,128]{2,1,0:T(8,128)} async-done(((f32[128,128,128]{2,1,0:T(8,128)}), f32[128,128,128]{2,1,0:T(8,128)}, u32[]{:S(2)}, u32[]{:S(2)}) %all-to-all-start.2) | async-done | bytes 8388640 | tf_op jit(solution)/shard_map/all_to_all | solution.py:438
  268.4 10.8 %assemble.1.whole_ref = f32[1536,768]{1,0:T(8,128)} custom-call(s32[4,12]{1,0:T(4,128)S(1)} %copy-done.9, s32[4,6]{1,0:T(4,128)S(1)} %broadcast_add_fusion.inv_col_ref, f32[128,128,128]{2,1,0:T(8,128)} %all-to-all-done.2.refs_0_.refs_1_.refs_2_.refs_3_, f32[128,128,128]{2,1,0:T(8,128)} %all-to-all-done.2.refs_0_.refs_1_.refs_2_.refs_3_, ...), custom_call_target="tpu_custom_call" | custom-call | tf_op jit(solution)/shard_map/assemble/pallas_call | solution.py:311
  279.3 7.3 %all-gather.2.cloned.1.call-done = f32[1536,512]{1,0:T(8,128)} async-done(((f32[96,512]{1,0:T(8,128)}), f32[1536,512]{1,0:T(8,128)}) %all-gather.2.cloned.1.call-update) | async-done | bytes 3145744 | tf_op jit(solution)/shard_map/all_gather | solution.py:433
  286.7 11.9 %panel.1.panel_ref = f32[1536,512]{1,0:T(8,128)} custom-call(f32[16,12,8,512]{3,2,1,0:T(8,128)} %bitcast.53, bf16[512,512]{1,0:T(8,128)(2,1)} %copy-done.5, bf16[512,512]{1,0:T(8,128)(2,1)} %copy-done.6), custom_call_target="tpu_custom_call" | custom-call | tf_op jit(solution)/shard_map/panel/pallas_call | solution.py:252
  298.6 7.5 %across.1 = (bf16[768,512]{1,0:T(8,128)(2,1)}, bf16[768,512]{1,0:T(8,128)(2,1)}) custom-call(s32[2]{0:T(128)} %pad_add_fusion.place_ref, f32[6,16,512]{2,1,0:T(8,128)} %copy-done.14, f32[6,16,512]{2,1,0:T(8,128)} %copy-done.21, f32[6,16,512]{2,1,0:T(8,128)} %copy-done.22, f32[6,16,512]{2,1,0:T(8,128)} %copy-done.16, f32[6,16,512]{2,1,0:T(8,128)} %copy-done.17, ...), custom_call_target="tpu_custom_call" | custom-call | tf_op jit(solution)/shard_map/across/pallas_call | solution.py:277
  310.2 8.9 %subtract.1 = f32[1536,768]{1,0:T(8,128)} custom-call(s32[2]{0:T(128)S(1)} %copy-done.10, f32[1536,768]{1,0:T(8,128)} %assemble.1.whole_ref, f32[1536,512]{1,0:T(8,128)S(1)} %copy-done.4, bf16[768,512]{1,0:T(8,128)(2,1)S(1)} %copy-done.7, bf16[768,512]{1,0:T(8,128)(2,1)S(1)} %copy-done.8), custom_call_target="tpu_custom_call", output_to_operand_aliasing={{}: (1, {})} | custom-call | tf_op jit(solution)/shard_map/subtract/pallas_call | solution.py:346
  (106 shorter events, 40.8 us)
Async XLA Ops:
  10.6 22.7 %collective-permute-start = (f32[12,4,8,512]{3,2,0,1:T(8,128)S(1)}, f32[12,4,8,512]{3,2,0,1:T(8,128)S(1)}, u32[]{:S(2)}, u32[]{:S(2)}) collective-permute-start(f32[12,4,8,512]{3,2,0,1:T(8,128)S(1)} %bitcast.55), channel_id=1, source_target_pairs={{0,3},{4,7},{8,11},{12,15},{16,19},{20,23},{24,27},{28,31},{32,35}... | collective-permute-start | bytes 2359304 | tf_op jit(solution)/shard_map/ppermute | solution.py:403
  36.7 69.5 %all-to-all-start = ((f32[128,24,128]{2,1,0:T(8,128)}), f32[128,24,128]{2,1,0:T(8,128)S(1)}, u32[]{:S(2)}, u32[]{:S(2)}) async-start(f32[128,24,128]{2,1,0:T(8,128)} %bitcast.52), calls=%async_computation | async-start | bytes 3145728 | tf_op jit(solution)/shard_map/all_to_all | solution.py:406
  48.9 33.8 %collective-permute-start.1 = (f32[12,4,8,512]{3,2,0,1:T(8,128)}, f32[12,4,8,512]{3,2,0,1:T(8,128)}, u32[]{:S(2)}, u32[]{:S(2)}) collective-permute-start(f32[12,4,8,512]{3,2,0,1:T(8,128)} %bitcast.46), channel_id=1, source_target_pairs={{0,1},{4,5},{8,9},{12,13},{16,17},{20,21},{24,25},{28,29},{32,33},... | collective-permute-start | bytes 2359304 | tf_op jit(solution)/shard_map/ppermute | solution.py:403
  53.2 46.2 %collective-permute-start.2 = (f32[12,4,8,512]{3,2,0,1:T(8,128)S(1)}, f32[12,4,8,512]{3,2,0,1:T(8,128)S(1)}, u32[]{:S(2)}, u32[]{:S(2)}) collective-permute-start(f32[12,4,8,512]{3,2,0,1:T(8,128)S(1)} %bitcast.56), channel_id=1, source_target_pairs={{0,2},{4,6},{8,10},{12,14},{16,18},{20,22},{24,26},{28,30},{32,34}... | collective-permute-start | bytes 2359304 | tf_op jit(solution)/shard_map/ppermute | solution.py:403
  102.2 18.2 %collective-permute-start.3 = (f32[12,8,512]{2,1,0:T(8,128)}, f32[12,8,512]{2,1,0:T(8,128)}, u32[]{:S(2)}, u32[]{:S(2)}) collective-permute-start(f32[12,8,512]{2,1,0:T(8,128)} %get-tuple-element.52), channel_id=1, source_target_pairs={{0,32},{1,33},{2,34},{3,35},{4,36},{5,37},{6,38},{7,39},{8,40},{9,... | collective-permute-start | bytes 589832 | tf_op jit(solution)/shard_map/ppermute | solution.py:411
  103.5 16.9 %collective-permute-start.4 = (f32[12,8,512]{2,1,0:T(8,128)}, f32[12,8,512]{2,1,0:T(8,128)}, u32[]{:S(2)}, u32[]{:S(2)}) collective-permute-start(f32[12,8,512]{2,1,0:T(8,128)} %get-tuple-element.50), channel_id=1, source_target_pairs={{0,64},{1,65},{2,66},{3,67},{4,68},{5,69},{6,70},{7,71},{8,72},{9,... | collective-permute-start | bytes 589832 | tf_op jit(solution)/shard_map/ppermute | solution.py:411
  104.9 15.6 %collective-permute-start.5 = (f32[12,8,512]{2,1,0:T(8,128)}, f32[12,8,512]{2,1,0:T(8,128)}, u32[]{:S(2)}, u32[]{:S(2)}) collective-permute-start(f32[12,8,512]{2,1,0:T(8,128)} %get-tuple-element.51), channel_id=1, source_target_pairs={{0,96},{1,97},{2,98},{3,99},{4,100},{5,101},{6,102},{7,103},{8,104... | collective-permute-start | bytes 589832 | tf_op jit(solution)/shard_map/ppermute | solution.py:411
  107.6 33.5 %all-to-all-start.1 = ((f32[128,16,128]{2,1,0:T(8,128)}), f32[128,16,128]{2,1,0:T(8,128)S(1)}, u32[]{:S(2)}, u32[]{:S(2)}) async-start(f32[128,16,128]{2,1,0:T(8,128)} %broadcast_in_dim.54), calls=%async_computation.1 | async-start | bytes 2097152 | tf_op jit(solution)/shard_map/all_to_all | solution.py:410
  126.0 15.0 %collective-permute-start.6 = (f32[6,8,512]{2,1,0:T(8,128)S(1)}, f32[6,8,512]{2,1,0:T(8,128)S(1)}, u32[]{:S(2)}, u32[]{:S(2)}) collective-permute-start(f32[6,8,512]{2,1,0:T(8,128)S(1)} %get-tuple-element.55), channel_id=1, source_target_pairs={{0,0},{1,1},{2,4},{3,5},{4,2},{5,3},{6,6},{7,7},{8,32},{9,33},{10,... | collective-permute-start | bytes 294920 | tf_op jit(solution)/shard_map/ppermute | solution.py:428
  131.1 9.9 %collective-permute-start.7 = (f32[6,8,512]{2,1,0:T(8,128)S(1)}, f32[6,8,512]{2,1,0:T(8,128)S(1)}, u32[]{:S(2)}, u32[]{:S(2)}) collective-permute-start(f32[6,8,512]{2,1,0:T(8,128)S(1)} %get-tuple-element.56), channel_id=1, source_target_pairs={{0,1},{1,0},{2,5},{3,4},{4,3},{5,2},{6,7},{7,6},{8,33},{9,32},{10,... | collective-permute-start | bytes 294920 | tf_op jit(solution)/shard_map/ppermute | solution.py:429
  141.1 113.4 %copy-start.14 = (f32[6,16,512]{2,1,0:T(8,128)}, f32[6,16,512]{2,1,0:T(8,128)S(1)}, u32[]{:S(2)}) copy-start(f32[6,16,512]{2,1,0:T(8,128)S(1)} %copy_bitcast_fusion.4.refs_0_) | copy-start | bytes 589828
  141.1 124.9 %copy-start.9 = (s32[4,12]{1,0:T(4,128)S(1)}, s32[4,12]{1,0:T(4,128)}, u32[]{:S(2)}) copy-start(s32[4,12]{1,0:T(4,128)} %broadcast_add_fusion.2.inv_row_ref) | copy-start | bytes 580
  141.1 124.9 %all-to-all-start.2 = ((f32[128,128,128]{2,1,0:T(8,128)}), f32[128,128,128]{2,1,0:T(8,128)}, u32[]{:S(2)}, u32[]{:S(2)}) async-start(f32[128,128,128]{2,1,0:T(8,128)} %bitcast.50), calls=%async_computation.2 | async-start | bytes 16777216 | tf_op jit(solution)/shard_map/all_to_all | solution.py:438
  151.7 135.0 %all-gather.2.cloned.1.call-start = ((), (), s32[]{:S(2)}) async-start(), calls=%async_computation.3 | async-start | bytes 3342336 | tf_op jit(solution)/shard_map/all_gather | solution.py:433
  187.6 66.0 %collective-permute-start.10 = (f32[6,16,512]{2,1,0:T(8,128)S(1)}, f32[6,16,512]{2,1,0:T(8,128)S(1)}, u32[]{:S(2)}, u32[]{:S(2)}) collective-permute-start(f32[6,16,512]{2,1,0:T(8,128)S(1)} %copy_bitcast_fusion.4.refs_0_), channel_id=1, source_target_pairs={{0,12},{4,8},{8,4},{12,0},{16,28},{20,24},{24,20},{28,16},{1,13},{... | collective-permute-start | bytes 589832 | tf_op jit(solution)/shard_map/ppermute | solution.py:370
  190.3 64.2 %collective-permute-start.11 = (f32[6,16,512]{2,1,0:T(8,128)S(1)}, f32[6,16,512]{2,1,0:T(8,128)S(1)}, u32[]{:S(2)}, u32[]{:S(2)}) collective-permute-start(f32[6,16,512]{2,1,0:T(8,128)S(1)} %copy_bitcast_fusion.4.refs_0_), channel_id=1, source_target_pairs={{0,16},{4,20},{8,24},{12,28},{16,0},{20,4},{24,8},{28,12},{1,17},{... | collective-permute-start | bytes 589832 | tf_op jit(solution)/shard_map/ppermute | solution.py:370
  193.7 85.6 %collective-permute-start.12 = (f32[6,16,512]{2,1,0:T(8,128)S(1)}, f32[6,16,512]{2,1,0:T(8,128)S(1)}, u32[]{:S(2)}, u32[]{:S(2)}) collective-permute-start(f32[6,16,512]{2,1,0:T(8,128)S(1)} %copy_bitcast_fusion.4.refs_0_), channel_id=1, source_target_pairs={{0,20},{4,16},{8,28},{12,24},{16,4},{20,0},{24,12},{28,8},{1,21},{... | collective-permute-start | bytes 589832 | tf_op jit(solution)/shard_map/ppermute | solution.py:370
  193.8 85.5 %collective-permute-start.13 = (f32[6,16,512]{2,1,0:T(8,128)S(1)}, f32[6,16,512]{2,1,0:T(8,128)S(1)}, u32[]{:S(2)}, u32[]{:S(2)}) collective-permute-start(f32[6,16,512]{2,1,0:T(8,128)S(1)} %copy_bitcast_fusion.4.refs_0_), channel_id=1, source_target_pairs={{0,24},{4,28},{8,16},{12,20},{16,8},{20,12},{24,0},{28,4},{1,25},{... | collective-permute-start | bytes 589832 | tf_op jit(solution)/shard_map/ppermute | solution.py:370
  197.5 81.8 %collective-permute-start.14 = (f32[6,16,512]{2,1,0:T(8,128)S(1)}, f32[6,16,512]{2,1,0:T(8,128)S(1)}, u32[]{:S(2)}, u32[]{:S(2)}) collective-permute-start(f32[6,16,512]{2,1,0:T(8,128)S(1)} %copy_bitcast_fusion.4.refs_0_), channel_id=1, source_target_pairs={{0,28},{4,24},{8,20},{12,16},{16,12},{20,8},{24,4},{28,0},{1,29},{... | collective-permute-start | bytes 589832 | tf_op jit(solution)/shard_map/ppermute | solution.py:370
  253.7 25.6 %copy-start.16 = (f32[6,16,512]{2,1,0:T(8,128)}, f32[6,16,512]{2,1,0:T(8,128)S(1)}, u32[]{:S(2)}) copy-start(f32[6,16,512]{2,1,0:T(8,128)S(1)} %collective-permute-done.10.refs_3_) | copy-start | bytes 589828
  253.7 25.7 %collective-permute-start.8 = (f32[6,16,512]{2,1,0:T(8,128)S(1)}, f32[6,16,512]{2,1,0:T(8,128)S(1)}, u32[]{:S(2)}, u32[]{:S(2)}) collective-permute-start(f32[6,16,512]{2,1,0:T(8,128)S(1)} %copy_bitcast_fusion.4.refs_0_), channel_id=1, source_target_pairs={{0,4},{4,0},{8,12},{12,8},{16,20},{20,16},{24,28},{28,24},{1,5},{5... | collective-permute-start | bytes 589832 | tf_op jit(solution)/shard_map/ppermute | solution.py:370
  254.5 24.7 %copy-start.17 = (f32[6,16,512]{2,1,0:T(8,128)}, f32[6,16,512]{2,1,0:T(8,128)S(1)}, u32[]{:S(2)}) copy-start(f32[6,16,512]{2,1,0:T(8,128)S(1)} %collective-permute-done.11.refs_4_) | copy-start | bytes 589828
  254.5 24.8 %collective-permute-start.9 = (f32[6,16,512]{2,1,0:T(8,128)S(1)}, f32[6,16,512]{2,1,0:T(8,128)S(1)}, u32[]{:S(2)}, u32[]{:S(2)}) collective-permute-start(f32[6,16,512]{2,1,0:T(8,128)S(1)} %copy_bitcast_fusion.4.refs_0_), channel_id=1, source_target_pairs={{0,8},{4,12},{8,0},{12,4},{16,24},{20,28},{24,16},{28,20},{1,9},{5... | collective-permute-start | bytes 589832 | tf_op jit(solution)/shard_map/ppermute | solution.py:370
  286.6 19.4 %copy-start.10 = (s32[2]{0:T(128)S(1)}, s32[2]{0:T(128)}, u32[]{:S(2)}) copy-start(s32[2]{0:T(128)} %pad_add_fusion.place_ref) | copy-start | bytes 28
  (20 other events, 182.2 us)
Sparse Core Ops, SparseCore 0:
  154.2 132.4 all-gather.1

commit v6 on v4

--- a/solution.py
+++ b/solution.py
@@ -9,6 +9,7 @@
 
 W = 512
 BLK = 128
+HALF = BLK // 2
 FRONTS = 4
 ROWS = 8
 COLS = 4
@@ -25,16 +26,20 @@
     return group // 2 + 8 * (group % 2)
 
 
-def pack_kernel(mask_ref, x_ref, o_ref):
+def pack_kernel(mask_ref, x_ref, upper_ref, lower_ref):
     step = pl.program_id(0)
     for front in range(FRONTS):
         for col in range(COLS):
             v = group_column(front * COLS + col)
             keep = mask_ref[step, v].astype(jnp.float32)
-            o_ref[front, 0, col] = x_ref[:, v * BLK : (v + 1) * BLK] * keep
+            span = slice(v * BLK, (v + 1) * BLK)
+            upper_ref[front, 0, col] = x_ref[:HALF, span] * keep
+            lower_ref[front, 0, col] = x_ref[HALF:, span] * keep
 
 
 def pack(window, local):
+    half = jax.ShapeDtypeStruct((FRONTS, ROWS, COLS, HALF, BLK), jnp.float32)
+    spec = pl.BlockSpec((FRONTS, 1, COLS, HALF, BLK), lambda i, m: (0, i, 0, 0, 0))
     return pl.pallas_call(
         pack_kernel,
         name="pack",
@@ -42,11 +47,9 @@
             num_scalar_prefetch=1,
             grid=(ROWS,),
             in_specs=[pl.BlockSpec((BLK, GROUPS * BLK), lambda i, m: (i, 0))],
-            out_specs=pl.BlockSpec(
-                (FRONTS, 1, COLS, BLK, BLK), lambda i, m: (0, i, 0, 0, 0)
-            ),
+            out_specs=[spec, spec],
         ),
-        out_shape=jax.ShapeDtypeStruct((FRONTS, ROWS, COLS, BLK, BLK), jnp.float32),
+        out_shape=[half, half],
         compiler_params=pltpu.CompilerParams(vmem_limit_bytes=32 << 20),
     )(window, local)
 
@@ -304,20 +307,21 @@
 
 def final_kernel(inv_row_ref, inv_col_ref, lead_ref, *refs):
     recvs = refs[: PAIR * FRONTS]
-    parent_ref, panel_ref, high_ref, low_ref, o_ref = refs[PAIR * FRONTS :]
+    parent_ref, panel_ref, high_ref, low_ref = refs[PAIR * FRONTS : PAIR * FRONTS + 4]
+    o_ref = refs[-1]
     step = pl.program_id(0)
-    o_ref[...] = parent_ref[...] - three_products(panel_ref[...], high_ref[...], low_ref[...])
-    for half in range(PAIR):
-        rows = slice(half * BLK, (half + 1) * BLK)
+    panel = panel_ref[:, 0].reshape(PAIR * HALF, W)
+    product = three_products(panel, high_ref[...], low_ref[...])
+    for part in range(PAIR):
         for b in range(PC):
             span = slice(b * BLK, (b + 1) * BLK)
-            total = o_ref[rows, span]
+            total = parent_ref[part, 0, :, span] - product[part * HALF : (part + 1) * HALF, span]
             for front in range(FRONTS):
-                r = inv_row_ref[front, step * PAIR + half]
+                r = inv_row_ref[front, step * PAIR + part]
                 c = inv_col_ref[front, b]
                 ok = jnp.logical_and(r >= 0, c >= 0).astype(jnp.float32)
-                total = total + recvs[half * FRONTS + front][jnp.maximum(c, 0)] * ok
-            o_ref[rows, span] = total
+                total = total + recvs[part * FRONTS + front][jnp.maximum(c, 0)] * ok
+            o_ref[part, 0, :, span] = total
 
     @pl.when(jnp.logical_and(lead_ref[0] == 1, step < WB // PAIR))
     def _():
@@ -325,37 +329,46 @@
 
     @pl.when(lead_ref[1] == 1)
     def _():
-        o_ref[:, :W] = jnp.zeros((PAIR * BLK, W), jnp.float32)
-
-
-def finish(inv_row, inv_col, lead, recv, parent, panel, high, low):
-    def recv_map(half, front):
+        o_ref[:, :, :, :W] = jnp.zeros((PAIR, 1, HALF, W), jnp.float32)
+
+
+def finish(place, inv_row, inv_col, lead, recv, parent, panel, high, low, before):
+    def recv_map(part, front):
         return lambda i, ir, ic, ld: (
-            front * ROWS + jnp.maximum(ir[front, i * PAIR + half], 0),
+            front * ROWS + jnp.maximum(ir[front, i * PAIR + part], 0),
             0,
             0,
         )
 
     whole = pl.BlockSpec((PC * BLK, W), lambda a, *_: (0, 0))
-    block = pl.BlockSpec((PAIR * BLK, PC * BLK), lambda a, *_: (a, 0))
-    recv_specs = [
-        pl.BlockSpec((COLS, BLK, BLK), recv_map(half, front))
-        for half in range(PAIR)
+    block = pl.BlockSpec((PAIR, 1, HALF, PC * BLK), lambda a, *_: (a, place, 0, 0))
+    specs = [
+        pl.BlockSpec((COLS, HALF, BLK), recv_map(part, front))
+        for part in range(PAIR)
         for front in range(FRONTS)
     ]
+    operands = [recv] * len(specs) + [
+        parent.reshape(PR, 2, HALF, PC * BLK),
+        panel.reshape(PR, 2, HALF, W),
+        high,
+        low,
+    ]
+    specs += [block, pl.BlockSpec((PAIR, 1, HALF, W), lambda a, *_: (a, place, 0, 0)), whole, whole]
+    aliases = {}
+    if before is not None:
+        aliases = {3 + len(operands): 0}
+        operands.append(before)
+        specs.append(pl.BlockSpec(memory_space=pl.ANY))
     return pl.pallas_call(
         final_kernel,
         name="finish",
         grid_spec=pltpu.PrefetchScalarGridSpec(
-            num_scalar_prefetch=3,
-            grid=(PR // PAIR,),
-            in_specs=recv_specs
-            + [block, pl.BlockSpec((PAIR * BLK, W), lambda a, *_: (a, 0)), whole, whole],
-            out_specs=block,
+            num_scalar_prefetch=3, grid=(PR // PAIR,), in_specs=specs, out_specs=block
         ),
-        out_shape=jax.ShapeDtypeStruct((PR * BLK, PC * BLK), jnp.float32),
+        out_shape=jax.ShapeDtypeStruct((PR, 2, HALF, PC * BLK), jnp.float32),
+        input_output_aliases=aliases,
         compiler_params=pltpu.CompilerParams(vmem_limit_bytes=40 << 20),
-    )(inv_row, inv_col, lead, *([recv] * len(recv_specs)), parent, panel, high, low)
+    )(inv_row, inv_col, lead, *operands)
 
 
 def inverse_places(places, length):
@@ -400,19 +413,25 @@
     holder = (row == 0) & (group == 0)
     info = jnp.stack([corner_place, holder.astype(jnp.int32)]).astype(jnp.int32)
 
+    lead = make_lead(window[:, 0], info, local, parent_entries).reshape(128, 24, BLK)
+    lead_recv = lax.all_to_all(lead, ALL, 0, 0, tiled=True)
+
     first = parent_entries[:, :W].reshape(PR, FRONTS, COLS, 8, W)
     sent = [lax.ppermute(first[:, :, k], "col", [(0, k)]) for k in range(1, COLS)]
-    sent[-1], info = lax.optimization_barrier((sent[-1], info))
     first = jnp.where(col == 0, first[:, :, 0], (sent[0] + sent[1]) + sent[2])
-    sent = [lax.ppermute(first[:, k], "front", [(0, k)]) for k in range(1, FRONTS)]
-    first = jnp.where(front == 0, first[:, 0], (sent[0] + sent[1]) + sent[2])
-
-    lead = make_lead(window[:, 0], info, local, parent_entries).reshape(128, 24, BLK)
-    lead_recv = lax.all_to_all(lead, ALL, 0, 0, tiled=True)
+
     tiles = jnp.sum(lead_recv[:, 8:], axis=0)
     tiles = jnp.broadcast_to(tiles[None], (128, 16, BLK))
     tiles = lax.all_to_all(tiles, ALL, 0, 0, tiled=True)
+
+    upper, lower = pack(window, local)
+    upper, first, tiles = lax.optimization_barrier((upper.reshape(128, HALF, BLK), first, tiles))
+    upper_recv = lax.all_to_all(upper, ALL, 0, 0, tiled=True)
     inverses = factor_inverse(tiles)
+    first, *inverses = lax.optimization_barrier((first, *inverses))
+
+    sent = [lax.ppermute(first[:, k], "front", [(0, k)]) for k in range(1, FRONTS)]
+    first = jnp.where(front == 0, first[:, 0], (sent[0] + sent[1]) + sent[2])
 
     column = group // 2 + 8 * (group % 2)
     by_row = lax.dynamic_index_in_dim(child_map.reshape(FRONTS, ROWS, 8), row, 2, keepdims=False)
@@ -438,14 +457,16 @@
     mine = mine.reshape(PC, 16, W)
     cols_raw = [mine] + [flipped(mine, "row", bits) for bits in range(1, ROWS)]
 
-    packed = pack(window, local).reshape(128, BLK, BLK)
-    packed, cols_raw, rows_raw = lax.optimization_barrier((packed, cols_raw, rows_raw))
-    recv = lax.all_to_all(packed, ALL, 0, 0, tiled=True)
-
+    lower, cols_raw, rows_raw = lax.optimization_barrier(
+        (lower.reshape(128, HALF, BLK), cols_raw, rows_raw)
+    )
+    lower_recv = lax.all_to_all(lower, ALL, 0, 0, tiled=True)
     panel, high, low = make_panels(place, rows_raw, cols_raw, inverses)
     lead_flags = jnp.stack([row == 0, group == 0]).astype(jnp.int32)
-    schur = finish(inv_row, inv_col, lead_flags, recv, parent_entries, panel, high, low)
-    return schur, panel
+    args = (parent_entries, panel, high, low)
+    schur = finish(0, inv_row, inv_col, lead_flags, upper_recv, *args, None)
+    schur = finish(1, inv_row, inv_col, lead_flags, lower_recv, *args, schur)
+    return schur.reshape(PR * BLK, PC * BLK), panel
 
 
 def solution(mesh):

time: 283 us -> 282 us (level)
  waiting for transfers between devices: 85.2 us -> 57.1 us
  starting transfers between devices: 80.7 us -> 95.9 us
  Pallas kernels: 67.4 us -> 75.7 us
  local copies, waits for them, and re-layouts: 35.4 us -> 39.8 us
    all_to_all x1 -> x2, waiting for transfers between devices: 43.4 us -> 11.3 us  [the longest x1 11.3 us: body(): lower_recv = lax.all_to_all(lower, ALL, 0, 0, tiled=True)]
    all_to_all x1 -> x2, starting transfers between devices: 9.15 us -> 23.3 us  [the longest x1 14.1 us: body(): lower_recv = lax.all_to_all(lower, ALL, 0, 0, tiled=True)]
    all_to_all x1, waiting for transfers between devices: 0.01 us -> 9.3 us  [body(): lead_recv = lax.all_to_all(lead, ALL, 0, 0, tiled=True)]
    pallas_call x1 -> x2, Pallas kernels: 11.3 us -> 19.6 us  [finish(): pl.pallas_call(final_kernel, name='finish', grid_spec=pltpu.PrefetchScala...]
    ppermute x1, starting transfers between devices: 3.6 us -> 11.6 us  [body(): lax.ppermute(jnp.where(even, slices[:PC], slices[PC:]), ALL, swap_pairs(0))]
    ppermute x15, waiting for transfers between devices: 16 us -> 8.34 us  [flipped(): return lax.ppermute(x, axis, [(i, i ^ bits) for i in range(size)])]
    all_to_all x1, starting transfers between devices: 12.5 us -> 5.78 us  [body(): tiles = lax.all_to_all(tiles, ALL, 0, 0, tiled=True)]
    unnamed x72, local copies, waits for them, and re-layouts: 29.7 us -> 35.2 us
  transfers between devices with their start and end apart: 26 -> 27, of which waited for: 7 -> 10; matrix products, arithmetic and copies ran while one was open for 4% -> 4% of each run, Pallas kernels for 19% -> 22%
where the time goes in v6:
time: 282 us; the launch traced here: 280 us
  starting transfers between devices  95.9 us (34%)
  Pallas kernels  75.7 us (27%)
  waiting for transfers between devices  57.1 us (20%)
  local copies, waits for them, and re-layouts  39.8 us (14%)
  other arithmetic  8.17 us (3%)
  between operations  3.59 us (1%)
    unnamed x72, local copies, waits for them, and re-layouts  35.2 us
    pallas_call x1, Pallas kernels, factor_inverse(): pl.pallas_call(factor_kernel, name='factor', in_specs=[vmem], out_specs=[...  33.5 us
    ppermute x15, starting transfers between devices, flipped(): return lax.ppermute(x, axis, [(i, i ^ bits) for i in range(size)])  29.1 us
    ppermute x3, waiting for transfers between devices, body(): lax.ppermute(first[:, :, k], 'col', [(0, k)])  21.6 us
    pallas_call x2, Pallas kernels, finish(): pl.pallas_call(final_kernel, name='finish', grid_spec=pltpu.PrefetchScala...  19.6 us
    pallas_call x1, Pallas kernels, make_panels(): pl.pallas_call(panel_kernel, name='panels', grid_spec=pltpu.PrefetchScala...  14.6 us
    all_to_all x1, starting transfers between devices, body(): lower_recv = lax.all_to_all(lower, ALL, 0, 0, tiled=True)  14.1 us
    all_to_all x1, starting transfers between devices, body(): lead_recv = lax.all_to_all(lead, ALL, 0, 0, tiled=True)  11.9 us
  transfers between devices with their start and end apart: 27, of which 10 were waited for; matrix products, arithmetic and copies ran while one was open for 4% of the time, Pallas kernels for 22%

profile of v6, /device:TPU:1, one launch (start us, length us, event | category | flops | bytes accessed | tf_op | source)
XLA Modules:
  0.0 280.3 jit_solution(12983964639963334745)
XLA Ops:
  6.3 3.4 %lead.1 = f32[4,8,4,24,128]{4,3,2,1,0:T(8,128)} custom-call(s32[8]{0:T(128)} %slice_reduce_fusion.1.keep_ref, s32[2]{0:T(128)} %get-tuple-element.77.info_ref, f32[1024,2048]{1,0:T(8,128)} %bitcast.55, f32[1536,768]{1,0:T(8,128)} %parent_ref.1), custom_call_target="tpu_custom_call" | custom-call | tf_op jit(solution)/shard_map/lead/pallas_call | solution.py:75
  9.7 11.9 %all-to-all-start = ((f32[128,24,128]{2,1,0:T(8,128)}), f32[128,24,128]{2,1,0:T(8,128)}, u32[]{:S(2)}, u32[]{:S(2)}) async-start(f32[128,24,128]{2,1,0:T(8,128)} %bitcast.62), calls=%async_computation | async-start | bytes 3145728 | tf_op jit(solution)/shard_map/all_to_all | solution.py:417
  22.9 6.1 %collective-permute-start.2 = (f32[12,4,8,512]{3,2,0,1:T(8,128)S(1)}, f32[12,4,8,512]{3,2,0,1:T(8,128)}, u32[]{:S(2)}, u32[]{:S(2)}) collective-permute-start(f32[12,4,8,512]{3,2,0,1:T(8,128)S(1)} %bitcast.64), channel_id=1, source_target_pairs={{0,3},{4,7},{8,11},{12,15},{16,19},{20,23},{24,27},{28,31},{32,35}... | collective-permute-start | bytes 2359304 | tf_op jit(solution)/shard_map/ppermute | solution.py:420
  35.2 9.3 %all-to-all-done.recv_ref = f32[128,24,128]{2,1,0:T(8,128)} async-done(((f32[128,24,128]{2,1,0:T(8,128)}), f32[128,24,128]{2,1,0:T(8,128)}, u32[]{:S(2)}, u32[]{:S(2)}) %all-to-all-start) | async-done | bytes 1572896 | tf_op jit(solution)/shard_map/all_to_all | solution.py:417
  46.9 5.8 %all-to-all-start.1 = ((f32[128,16,128]{2,1,0:T(8,128)}), f32[128,16,128]{2,1,0:T(8,128)S(1)}, u32[]{:S(2)}, u32[]{:S(2)}) async-start(f32[128,16,128]{2,1,0:T(8,128)} %broadcast_in_dim.56), calls=%async_computation.1 | async-start | bytes 2097152 | tf_op jit(solution)/shard_map/all_to_all | solution.py:425
  52.7 3.4 %copy-done.3 = f32[1,1024,2048]{2,1,0:T(8,128)S(1)} copy-done((f32[1,1024,2048]{2,1,0:T(8,128)S(1)}, f32[1,1024,2048]{2,1,0:T(8,128)}, u32[]{:S(2)}) %copy-start.3) | copy-done | bytes 8388632
  62.1 5.2 %collective-permute-done.2 = f32[12,4,8,512]{3,2,0,1:T(8,128)} collective-permute-done((f32[12,4,8,512]{3,2,0,1:T(8,128)S(1)}, f32[12,4,8,512]{3,2,0,1:T(8,128)}, u32[]{:S(2)}, u32[]{:S(2)}) %collective-permute-start.2) | collective-permute-done | bytes 786464 | tf_op jit(solution)/shard_map/ppermute | solution.py:420
  67.3 16.4 %collective-permute-done.1 = f32[12,4,8,512]{3,2,0,1:T(8,128)} collective-permute-done((f32[12,4,8,512]{3,2,0,1:T(8,128)}, f32[12,4,8,512]{3,2,0,1:T(8,128)}, u32[]{:S(2)}, u32[]{:S(2)}) %collective-permute-start.1) | collective-permute-done | bytes 786464 | tf_op jit(solution)/shard_map/ppermute | solution.py:420
  85.7 9.2 %all-to-all-start.3 = ((f32[128,64,128]{2,1,0:T(8,128)}), f32[128,64,128]{2,1,0:T(8,128)}, u32[]{:S(2)}, u32[]{:S(2)}) async-start(f32[128,64,128]{2,1,0:T(8,128)} %bitcast.60), calls=%async_computation.3 | async-start | bytes 8388608 | tf_op jit(solution)/shard_map/all_to_all | solution.py:429
  95.9 33.5 %factor.1 = (bf16[512,512]{1,0:T(8,128)(2,1)S(1)}, bf16[512,512]{1,0:T(8,128)(2,1)S(1)}) custom-call(f32[128,16,128]{2,1,0:T(8,128)S(1)} %all-to-all-done.1.x_ref), custom_call_target="tpu_custom_call" | custom-call | tf_op jit(solution)/shard_map/factor/pallas_call | solution.py:225
  132.7 4.3 %collective-permute-done.3 = f32[12,8,512]{2,1,0:T(8,128)S(1)} collective-permute-done((f32[12,8,512]{2,1,0:T(8,128)S(1)}, f32[12,8,512]{2,1,0:T(8,128)S(1)}, u32[]{:S(2)}, u32[]{:S(2)}) %collective-permute-start.3) | collective-permute-done | bytes 196640 | tf_op jit(solution)/shard_map/ppermute | solution.py:433
  137.6 2.7 slices.1
  141.3 11.6 %collective-permute-start.6 = (f32[6,8,512]{2,1,0:T(8,128)S(1)}, f32[6,8,512]{2,1,0:T(8,128)S(1)}, u32[]{:S(2)}, u32[]{:S(2)}) collective-permute-start(f32[6,8,512]{2,1,0:T(8,128)S(1)} %get-tuple-element.71), channel_id=1, source_target_pairs={{0,0},{1,1},{2,4},{3,5},{4,2},{5,3},{6,6},{7,7},{8,32},{9,33},{10,... | collective-permute-start | bytes 294920 | tf_op jit(solution)/shard_map/ppermute | solution.py:454
  154.2 3.1 %collective-permute-start.15 = (f32[12,8,512]{2,1,0:T(8,128)}, f32[12,8,512]{2,1,0:T(8,128)S(1)}, u32[]{:S(2)}, u32[]{:S(2)}) collective-permute-start(f32[12,8,512]{2,1,0:T(8,128)} %slices.1), channel_id=1, source_target_pairs={{0,64},{32,96},{64,0},{96,32},{1,65},{33,97},{65,1},{97,33},{2,66}... | collective-permute-start | bytes 589832 | tf_op jit(solution)/shard_map/ppermute | solution.py:383
  159.6 6.7 %collective-permute-start.14 = (f32[6,16,512]{2,1,0:T(8,128)S(1)}, f32[6,16,512]{2,1,0:T(8,128)S(1)}, u32[]{:S(2)}, u32[]{:S(2)}) collective-permute-start(f32[6,16,512]{2,1,0:T(8,128)S(1)} %copy_bitcast_fusion.4.refs_8_), channel_id=1, source_target_pairs={{0,28},{4,24},{8,20},{12,16},{16,12},{20,8},{24,4},{28,0},{1,29},{... | collective-permute-start | bytes 589832 | tf_op jit(solution)/shard_map/ppermute | solution.py:383
  169.1 4.8 %collective-permute-start.18 = (f32[2,12,8,512]{3,2,1,0:T(8,128)S(1)}, f32[2,12,8,512]{3,2,1,0:T(8,128)S(1)}, u32[]{:S(2)}, u32[]{:S(2)}) collective-permute-start(f32[2,12,8,512]{3,2,1,0:T(8,128)S(1)} %pad_maximum_fusion.refs_0_), channel_id=1, source_target_pairs={{0,3},{1,2},{2,1},{3,0},{4,7},{5,6},{6,5},{7,4},{8,11},{9,10},{10,... | collective-permute-start | bytes 1179656 | tf_op jit(solution)/shard_map/ppermute | solution.py:383
  175.8 3.9 %collective-permute-start.11 = (f32[6,16,512]{2,1,0:T(8,128)S(1)}, f32[6,16,512]{2,1,0:T(8,128)S(1)}, u32[]{:S(2)}, u32[]{:S(2)}) collective-permute-start(f32[6,16,512]{2,1,0:T(8,128)S(1)} %copy_bitcast_fusion.4.refs_8_), channel_id=1, source_target_pairs={{0,16},{4,20},{8,24},{12,28},{16,0},{20,4},{24,8},{28,12},{1,17},{... | collective-permute-start | bytes 589832 | tf_op jit(solution)/shard_map/ppermute | solution.py:383
  187.1 4.6 %collective-permute-start.19 = (f32[2,12,8,512]{3,2,1,0:T(8,128)S(1)}, f32[2,12,8,512]{3,2,1,0:T(8,128)S(1)}, u32[]{:S(2)}, u32[]{:S(2)}) collective-permute-start(f32[2,12,8,512]{3,2,1,0:T(8,128)S(1)} %pad_maximum_fusion.refs_0_), channel_id=1, source_target_pairs={{0,32},{32,0},{64,96},{96,64},{1,33},{33,1},{65,97},{97,65},{2,34}... | collective-permute-start | bytes 1179656 | tf_op jit(solution)/shard_map/ppermute | solution.py:383
  194.5 3.7 %collective-permute-done.8.refs_9_ = f32[6,16,512]{2,1,0:T(8,128)S(1)} collective-permute-done((f32[6,16,512]{2,1,0:T(8,128)S(1)}, f32[6,16,512]{2,1,0:T(8,128)S(1)}, u32[]{:S(2)}, u32[]{:S(2)}) %collective-permute-start.8) | collective-permute-done | bytes 196640 | tf_op jit(solution)/shard_map/ppermute | solution.py:383
  201.2 14.1 %all-to-all-start.2 = ((f32[128,64,128]{2,1,0:T(8,128)}), f32[128,64,128]{2,1,0:T(8,128)}, u32[]{:S(2)}, u32[]{:S(2)}) async-start(f32[128,64,128]{2,1,0:T(8,128)} %bitcast.59), calls=%async_computation.2 | async-start | bytes 8388608 | tf_op jit(solution)/shard_map/all_to_all | solution.py:463
  224.1 14.6 %panels.1 = (f32[1536,512]{1,0:T(8,128)}, bf16[768,512]{1,0:T(8,128)(2,1)S(1)}, bf16[768,512]{1,0:T(8,128)(2,1)S(1)}) custom-call(s32[2]{0:T(128)S(1)} %get-tuple-element.78.place_ref, f32[2,12,8,512]{3,2,1,0:T(8,128)S(1)} %pad_maximum_fusion.refs_0_, f32[2,12,8,512]{3,2,1,0:T(8,128)S(1)} %collective-permute-done.16.refs_1_, ...), custom_call_target="tpu_custom_call" | custom-call | tf_op jit(solution)/shard_map/panels/pallas_call | solution.py:284
  243.0 9.9 %finish.2.refs_12_ = f32[12,2,64,768]{3,2,1,0:T(8,128)} custom-call(s32[4,12]{1,0:T(4,128)S(1)} %copy-done.30, s32[4,6]{1,0:T(4,128)S(1)} %broadcast_add_fusion.1.inv_col_ref, s32[2]{0:T(128)S(1)} %add_convert_fusion.lead_ref, f32[128,64,128]{2,1,0:T(8,128)} %all-to-all-done.3.refs_0_.refs_1_.refs_2_.refs_3_.refs_4_.refs_5_.refs_6_.refs_7_, ...), custom_call_target="tpu_custom_call" | custom-call | tf_op jit(solution)/shard_map/finish/pallas_call | solution.py:362
  254.7 11.3 %all-to-all-done.2.refs_0_.refs_1_.refs_2_.refs_3_.refs_4_.refs_5_.refs_6_.refs_7_ = f32[128,64,128]{2,1,0:T(8,128)} async-done(((f32[128,64,128]{2,1,0:T(8,128)}), f32[128,64,128]{2,1,0:T(8,128)}, u32[]{:S(2)}, u32[]{:S(2)}) %all-to-all-start.2) | async-done | bytes 4194336 | tf_op jit(solution)/shard_map/all_to_all | solution.py:463
  270.6 9.7 %finish.3 = f32[12,2,64,768]{3,2,1,0:T(8,128)} custom-call(s32[4,12]{1,0:T(4,128)S(1)} %copy-done.30, s32[4,6]{1,0:T(4,128)S(1)} %broadcast_add_fusion.1.inv_col_ref, s32[2]{0:T(128)S(1)} %add_convert_fusion.lead_ref, f32[128,64,128]{2,1,0:T(8,128)} %all-to-all-done.2.refs_0_.refs_1_.refs_2_.refs_3_.refs_4_.refs_5_.refs_6_.refs_7_, ...), custom_call_target="tpu_custom_call", output_to_operand_aliasing={{}: (15, {})} | custom-call | tf_op jit(solution)/shard_map/finish/pallas_call | solution.py:362
  (139 shorter events, 67.7 us)
Async XLA Ops:
  9.7 34.8 %all-to-all-start = ((f32[128,24,128]{2,1,0:T(8,128)}), f32[128,24,128]{2,1,0:T(8,128)}, u32[]{:S(2)}, u32[]{:S(2)}) async-start(f32[128,24,128]{2,1,0:T(8,128)} %bitcast.62), calls=%async_computation | async-start | bytes 3145728 | tf_op jit(solution)/shard_map/all_to_all | solution.py:417
  22.9 44.4 %collective-permute-start.2 = (f32[12,4,8,512]{3,2,0,1:T(8,128)S(1)}, f32[12,4,8,512]{3,2,0,1:T(8,128)}, u32[]{:S(2)}, u32[]{:S(2)}) collective-permute-start(f32[12,4,8,512]{3,2,0,1:T(8,128)S(1)} %bitcast.64), channel_id=1, source_target_pairs={{0,3},{4,7},{8,11},{12,15},{16,19},{20,23},{24,27},{28,31},{32,35}... | collective-permute-start | bytes 2359304 | tf_op jit(solution)/shard_map/ppermute | solution.py:420
  29.9 37.4 %collective-permute-start = (f32[12,4,8,512]{3,2,0,1:T(8,128)}, f32[12,4,8,512]{3,2,0,1:T(8,128)}, u32[]{:S(2)}, u32[]{:S(2)}) collective-permute-start(f32[12,4,8,512]{3,2,0,1:T(8,128)} %bitcast.51), channel_id=1, source_target_pairs={{0,1},{4,5},{8,9},{12,13},{16,17},{20,21},{24,25},{28,29},{32,33},... | collective-permute-start | bytes 2359304 | tf_op jit(solution)/shard_map/ppermute | solution.py:420
  33.0 50.6 %collective-permute-start.1 = (f32[12,4,8,512]{3,2,0,1:T(8,128)}, f32[12,4,8,512]{3,2,0,1:T(8,128)}, u32[]{:S(2)}, u32[]{:S(2)}) collective-permute-start(f32[12,4,8,512]{3,2,0,1:T(8,128)} %bitcast.50), channel_id=1, source_target_pairs={{0,2},{4,6},{8,10},{12,14},{16,18},{20,22},{24,26},{28,30},{32,34}... | collective-permute-start | bytes 2359304 | tf_op jit(solution)/shard_map/ppermute | solution.py:420
  46.9 38.7 %all-to-all-start.1 = ((f32[128,16,128]{2,1,0:T(8,128)}), f32[128,16,128]{2,1,0:T(8,128)S(1)}, u32[]{:S(2)}, u32[]{:S(2)}) async-start(f32[128,16,128]{2,1,0:T(8,128)} %broadcast_in_dim.56), calls=%async_computation.1 | async-start | bytes 2097152 | tf_op jit(solution)/shard_map/all_to_all | solution.py:425
  85.7 115.5 %all-to-all-start.3 = ((f32[128,64,128]{2,1,0:T(8,128)}), f32[128,64,128]{2,1,0:T(8,128)}, u32[]{:S(2)}, u32[]{:S(2)}) async-start(f32[128,64,128]{2,1,0:T(8,128)} %bitcast.60), calls=%async_computation.3 | async-start | bytes 8388608 | tf_op jit(solution)/shard_map/all_to_all | solution.py:429
  130.8 6.1 %collective-permute-start.3 = (f32[12,8,512]{2,1,0:T(8,128)S(1)}, f32[12,8,512]{2,1,0:T(8,128)S(1)}, u32[]{:S(2)}, u32[]{:S(2)}) collective-permute-start(f32[12,8,512]{2,1,0:T(8,128)S(1)} %get-tuple-element.68), channel_id=1, source_target_pairs={{0,32},{1,33},{2,34},{3,35},{4,36},{5,37},{6,38},{7,39},{8,40},{9,... | collective-permute-start | bytes 589832 | tf_op jit(solution)/shard_map/ppermute | solution.py:433
  141.3 16.0 %collective-permute-start.6 = (f32[6,8,512]{2,1,0:T(8,128)S(1)}, f32[6,8,512]{2,1,0:T(8,128)S(1)}, u32[]{:S(2)}, u32[]{:S(2)}) collective-permute-start(f32[6,8,512]{2,1,0:T(8,128)S(1)} %get-tuple-element.71), channel_id=1, source_target_pairs={{0,0},{1,1},{2,4},{3,5},{4,2},{5,3},{6,6},{7,7},{8,32},{9,33},{10,... | collective-permute-start | bytes 294920 | tf_op jit(solution)/shard_map/ppermute | solution.py:454
  153.0 6.6 %collective-permute-start.7 = (f32[6,8,512]{2,1,0:T(8,128)S(1)}, f32[6,8,512]{2,1,0:T(8,128)S(1)}, u32[]{:S(2)}, u32[]{:S(2)}) collective-permute-start(f32[6,8,512]{2,1,0:T(8,128)S(1)} %get-tuple-element.72), channel_id=1, source_target_pairs={{0,1},{1,0},{2,5},{3,4},{4,3},{5,2},{6,7},{7,6},{8,33},{9,32},{10,... | collective-permute-start | bytes 294920 | tf_op jit(solution)/shard_map/ppermute | solution.py:455
  154.2 13.9 %collective-permute-start.15 = (f32[12,8,512]{2,1,0:T(8,128)}, f32[12,8,512]{2,1,0:T(8,128)S(1)}, u32[]{:S(2)}, u32[]{:S(2)}) collective-permute-start(f32[12,8,512]{2,1,0:T(8,128)} %slices.1), channel_id=1, source_target_pairs={{0,64},{32,96},{64,0},{96,32},{1,65},{33,97},{65,1},{97,33},{2,66}... | collective-permute-start | bytes 589832 | tf_op jit(solution)/shard_map/ppermute | solution.py:383
  159.6 14.3 %collective-permute-start.14 = (f32[6,16,512]{2,1,0:T(8,128)S(1)}, f32[6,16,512]{2,1,0:T(8,128)S(1)}, u32[]{:S(2)}, u32[]{:S(2)}) collective-permute-start(f32[6,16,512]{2,1,0:T(8,128)S(1)} %copy_bitcast_fusion.4.refs_8_), channel_id=1, source_target_pairs={{0,28},{4,24},{8,20},{12,16},{16,12},{20,8},{24,4},{28,0},{1,29},{... | collective-permute-start | bytes 589832 | tf_op jit(solution)/shard_map/ppermute | solution.py:383
  166.3 8.9 %collective-permute-start.13 = (f32[6,16,512]{2,1,0:T(8,128)S(1)}, f32[6,16,512]{2,1,0:T(8,128)S(1)}, u32[]{:S(2)}, u32[]{:S(2)}) collective-permute-start(f32[6,16,512]{2,1,0:T(8,128)S(1)} %copy_bitcast_fusion.4.refs_8_), channel_id=1, source_target_pairs={{0,24},{4,28},{8,16},{12,20},{16,8},{20,12},{24,0},{28,4},{1,25},{... | collective-permute-start | bytes 589832 | tf_op jit(solution)/shard_map/ppermute | solution.py:383
  167.3 12.4 %collective-permute-start.12 = (f32[6,16,512]{2,1,0:T(8,128)S(1)}, f32[6,16,512]{2,1,0:T(8,128)S(1)}, u32[]{:S(2)}, u32[]{:S(2)}) collective-permute-start(f32[6,16,512]{2,1,0:T(8,128)S(1)} %copy_bitcast_fusion.4.refs_8_), channel_id=1, source_target_pairs={{0,20},{4,16},{8,28},{12,24},{16,4},{20,0},{24,12},{28,8},{1,21},{... | collective-permute-start | bytes 589832 | tf_op jit(solution)/shard_map/ppermute | solution.py:383
  169.1 22.7 %collective-permute-start.18 = (f32[2,12,8,512]{3,2,1,0:T(8,128)S(1)}, f32[2,12,8,512]{3,2,1,0:T(8,128)S(1)}, u32[]{:S(2)}, u32[]{:S(2)}) collective-permute-start(f32[2,12,8,512]{3,2,1,0:T(8,128)S(1)} %pad_maximum_fusion.refs_0_), channel_id=1, source_target_pairs={{0,3},{1,2},{2,1},{3,0},{4,7},{5,6},{6,5},{7,4},{8,11},{9,10},{10,... | collective-permute-start | bytes 1179656 | tf_op jit(solution)/shard_map/ppermute | solution.py:383
  173.8 18.5 %collective-permute-start.17 = (f32[2,12,8,512]{3,2,1,0:T(8,128)S(1)}, f32[2,12,8,512]{3,2,1,0:T(8,128)S(1)}, u32[]{:S(2)}, u32[]{:S(2)}) collective-permute-start(f32[2,12,8,512]{3,2,1,0:T(8,128)S(1)} %pad_maximum_fusion.refs_0_), channel_id=1, source_target_pairs={{0,2},{1,3},{2,0},{3,1},{4,6},{5,7},{6,4},{7,5},{8,10},{9,11},{10,... | collective-permute-start | bytes 1179656 | tf_op jit(solution)/shard_map/ppermute | solution.py:383
  173.8 18.5 %collective-permute-start.16 = (f32[2,12,8,512]{3,2,1,0:T(8,128)S(1)}, f32[2,12,8,512]{3,2,1,0:T(8,128)S(1)}, u32[]{:S(2)}, u32[]{:S(2)}) collective-permute-start(f32[2,12,8,512]{3,2,1,0:T(8,128)S(1)} %pad_maximum_fusion.refs_0_), channel_id=1, source_target_pairs={{0,1},{1,0},{2,3},{3,2},{4,5},{5,4},{6,7},{7,6},{8,9},{9,8},{10,11... | collective-permute-start | bytes 1179656 | tf_op jit(solution)/shard_map/ppermute | solution.py:383
  175.8 7.3 %collective-permute-start.11 = (f32[6,16,512]{2,1,0:T(8,128)S(1)}, f32[6,16,512]{2,1,0:T(8,128)S(1)}, u32[]{:S(2)}, u32[]{:S(2)}) collective-permute-start(f32[6,16,512]{2,1,0:T(8,128)S(1)} %copy_bitcast_fusion.4.refs_8_), channel_id=1, source_target_pairs={{0,16},{4,20},{8,24},{12,28},{16,0},{20,4},{24,8},{28,12},{1,17},{... | collective-permute-start | bytes 589832 | tf_op jit(solution)/shard_map/ppermute | solution.py:383
  180.4 6.0 %collective-permute-start.10 = (f32[6,16,512]{2,1,0:T(8,128)S(1)}, f32[6,16,512]{2,1,0:T(8,128)S(1)}, u32[]{:S(2)}, u32[]{:S(2)}) collective-permute-start(f32[6,16,512]{2,1,0:T(8,128)S(1)} %copy_bitcast_fusion.4.refs_8_), channel_id=1, source_target_pairs={{0,12},{4,8},{8,4},{12,0},{16,28},{20,24},{24,20},{28,16},{1,13},{... | collective-permute-start | bytes 589832 | tf_op jit(solution)/shard_map/ppermute | solution.py:383
  183.8 9.3 %collective-permute-start.9 = (f32[6,16,512]{2,1,0:T(8,128)S(1)}, f32[6,16,512]{2,1,0:T(8,128)S(1)}, u32[]{:S(2)}, u32[]{:S(2)}) collective-permute-start(f32[6,16,512]{2,1,0:T(8,128)S(1)} %copy_bitcast_fusion.4.refs_8_), channel_id=1, source_target_pairs={{0,8},{4,12},{8,0},{12,4},{16,24},{20,28},{24,16},{28,20},{1,9},{5... | collective-permute-start | bytes 589832 | tf_op jit(solution)/shard_map/ppermute | solution.py:383
  187.1 11.8 %collective-permute-start.19 = (f32[2,12,8,512]{3,2,1,0:T(8,128)S(1)}, f32[2,12,8,512]{3,2,1,0:T(8,128)S(1)}, u32[]{:S(2)}, u32[]{:S(2)}) collective-permute-start(f32[2,12,8,512]{3,2,1,0:T(8,128)S(1)} %pad_maximum_fusion.refs_0_), channel_id=1, source_target_pairs={{0,32},{32,0},{64,96},{96,64},{1,33},{33,1},{65,97},{97,65},{2,34}... | collective-permute-start | bytes 1179656 | tf_op jit(solution)/shard_map/ppermute | solution.py:383
  191.7 7.2 %collective-permute-start.22 = (f32[2,12,8,512]{3,2,1,0:T(8,128)S(1)}, f32[2,12,8,512]{3,2,1,0:T(8,128)S(1)}, u32[]{:S(2)}, u32[]{:S(2)}) collective-permute-start(f32[2,12,8,512]{3,2,1,0:T(8,128)S(1)} %collective-permute-done.18.refs_3_), channel_id=1, source_target_pairs={{0,32},{32,0},{64,96},{96,64},{1,33},{33,1},{65,97},{97,65},{2,34}... | collective-permute-start | bytes 1179656 | tf_op jit(solution)/shard_map/ppermute | solution.py:383
  192.3 7.3 %collective-permute-start.21 = (f32[2,12,8,512]{3,2,1,0:T(8,128)S(1)}, f32[2,12,8,512]{3,2,1,0:T(8,128)S(1)}, u32[]{:S(2)}, u32[]{:S(2)}) collective-permute-start(f32[2,12,8,512]{3,2,1,0:T(8,128)S(1)} %collective-permute-done.17.refs_2_), channel_id=1, source_target_pairs={{0,32},{32,0},{64,96},{96,64},{1,33},{33,1},{65,97},{97,65},{2,34}... | collective-permute-start | bytes 1179656 | tf_op jit(solution)/shard_map/ppermute | solution.py:383
  192.3 8.1 %collective-permute-start.20 = (f32[2,12,8,512]{3,2,1,0:T(8,128)S(1)}, f32[2,12,8,512]{3,2,1,0:T(8,128)S(1)}, u32[]{:S(2)}, u32[]{:S(2)}) collective-permute-start(f32[2,12,8,512]{3,2,1,0:T(8,128)S(1)} %collective-permute-done.16.refs_1_), channel_id=1, source_target_pairs={{0,32},{32,0},{64,96},{96,64},{1,33},{33,1},{65,97},{97,65},{2,34}... | collective-permute-start | bytes 1179656 | tf_op jit(solution)/shard_map/ppermute | solution.py:383
  201.2 64.8 %all-to-all-start.2 = ((f32[128,64,128]{2,1,0:T(8,128)}), f32[128,64,128]{2,1,0:T(8,128)}, u32[]{:S(2)}, u32[]{:S(2)}) async-start(f32[128,64,128]{2,1,0:T(8,128)} %bitcast.59), calls=%async_computation.2 | async-start | bytes 8388608 | tf_op jit(solution)/shard_map/all_to_all | solution.py:463
  (37 other events, 141.3 us)

commit v7 on v6

--- a/solution.py
+++ b/solution.py
@@ -247,8 +247,8 @@
 
 
 def panel_kernel(place_ref, *refs):
-    rows, cols = refs[:8], refs[8:16]
-    inverse_high, inverse_low, panel_ref, high_ref, low_ref, block_ref = refs[16:]
+    rows, cols_ref = refs[:8], refs[8]
+    inverse_high, inverse_low, panel_ref, high_ref, low_ref, block_ref = refs[9:]
     step = pl.program_id(0)
 
     def times_inverse(x):
@@ -266,10 +266,7 @@
 
     @pl.when(step >= PR)
     def _():
-        for other in range(ROWS):
-            start = pl.multiple_of((place_ref[0] ^ other) * 16, 16)
-            block_ref[pl.ds(start, 16), :] = cols[other][0]
-        value = times_inverse(block_ref[...])
+        value = times_inverse(cols_ref[:, 0].reshape(BLK, W))
         high_ref[...], low_ref[...] = split(value)
 
 
@@ -288,7 +285,7 @@
             num_scalar_prefetch=1,
             grid=(PR + PC,),
             in_specs=[pl.BlockSpec((2, 1, 8, W), lambda i, p: (0, in_rows(i), 0, 0))] * 8
-            + [pl.BlockSpec((1, 16, W), lambda i, p: (in_cols(i), 0, 0))] * ROWS
+            + [pl.BlockSpec((ROWS, 1, 16, W), lambda i, p: (0, in_cols(i), 0, 0))]
             + [pl.BlockSpec((W, W), lambda i, p: (0, 0))] * 2,
             out_specs=[
                 pl.BlockSpec((BLK, W), lambda i, p: (in_rows(i), 0)),
@@ -299,10 +296,10 @@
         ),
         out_shape=[jax.ShapeDtypeStruct((PR * BLK, W), jnp.float32), half, half],
         compiler_params=pltpu.CompilerParams(vmem_limit_bytes=32 << 20),
-    )(place, *rows_raw, *cols_raw, *inverses)
-
-
-PAIR = 2
+    )(place, *rows_raw, cols_raw, *inverses)
+
+
+PAIR = 4
 
 
 def final_kernel(inv_row_ref, inv_col_ref, lead_ref, *refs):
@@ -367,7 +364,7 @@
         ),
         out_shape=jax.ShapeDtypeStruct((PR, 2, HALF, PC * BLK), jnp.float32),
         input_output_aliases=aliases,
-        compiler_params=pltpu.CompilerParams(vmem_limit_bytes=40 << 20),
+        compiler_params=pltpu.CompilerParams(vmem_limit_bytes=56 << 20),
     )(inv_row, inv_col, lead, *operands)
 
 
@@ -414,21 +411,22 @@
     info = jnp.stack([corner_place, holder.astype(jnp.int32)]).astype(jnp.int32)
 
     lead = make_lead(window[:, 0], info, local, parent_entries).reshape(128, 24, BLK)
-    lead_recv = lax.all_to_all(lead, ALL, 0, 0, tiled=True)
 
     first = parent_entries[:, :W].reshape(PR, FRONTS, COLS, 8, W)
     sent = [lax.ppermute(first[:, :, k], "col", [(0, k)]) for k in range(1, COLS)]
-    first = jnp.where(col == 0, first[:, :, 0], (sent[0] + sent[1]) + sent[2])
+    first = first[:, :, 0]
+
+    upper, lower = pack(window, local)
+    upper, sent[0], sent[1], sent[2] = lax.optimization_barrier((upper, *sent))
+    upper_recv = lax.all_to_all(upper.reshape(128, HALF, BLK), ALL, 0, 0, tiled=True)
+    first = jnp.where(col == 0, first, (sent[0] + sent[1]) + sent[2])
+
+    lead, upper_recv = lax.optimization_barrier((lead, upper_recv))
+    lead_recv = lax.all_to_all(lead, ALL, 0, 0, tiled=True)
 
     tiles = jnp.sum(lead_recv[:, 8:], axis=0)
     tiles = jnp.broadcast_to(tiles[None], (128, 16, BLK))
     tiles = lax.all_to_all(tiles, ALL, 0, 0, tiled=True)
-
-    upper, lower = pack(window, local)
-    upper, first, tiles = lax.optimization_barrier((upper.reshape(128, HALF, BLK), first, tiles))
-    upper_recv = lax.all_to_all(upper, ALL, 0, 0, tiled=True)
-    inverses = factor_inverse(tiles)
-    first, *inverses = lax.optimization_barrier((first, *inverses))
 
     sent = [lax.ppermute(first[:, k], "front", [(0, k)]) for k in range(1, FRONTS)]
     first = jnp.where(front == 0, first[:, 0], (sent[0] + sent[1]) + sent[2])
@@ -455,11 +453,13 @@
     two = lax.ppermute(jnp.where(even, slices[PC:], slices[:PC]), ALL, swap_pairs(1))
     mine = jnp.stack([jnp.where(even, one, two), jnp.where(even, two, one)], axis=1)
     mine = mine.reshape(PC, 16, W)
-    cols_raw = [mine] + [flipped(mine, "row", bits) for bits in range(1, ROWS)]
-
-    lower, cols_raw, rows_raw = lax.optimization_barrier(
-        (lower.reshape(128, HALF, BLK), cols_raw, rows_raw)
+    mine = jnp.broadcast_to(mine.reshape(1, PC * 16, W), (ROWS, PC * 16, W))
+    cols_raw = lax.all_to_all(mine, "row", 0, 0, tiled=True).reshape(ROWS, PC, 16, W)
+
+    lower, tiles, cols_raw, rows_raw = lax.optimization_barrier(
+        (lower.reshape(128, HALF, BLK), tiles, cols_raw, rows_raw)
     )
+    inverses = factor_inverse(tiles)
     lower_recv = lax.all_to_all(lower, ALL, 0, 0, tiled=True)
     panel, high, low = make_panels(place, rows_raw, cols_raw, inverses)
     lead_flags = jnp.stack([row == 0, group == 0]).astype(jnp.int32)

time: 282 us -> 304 us (1.078)
  waiting for transfers between devices: 57.1 us -> 118 us
  starting transfers between devices: 95.9 us -> 71.1 us
  local copies, waits for them, and re-layouts: 39.8 us -> 28.2 us
    all_to_all x1 -> x2, waiting for transfers between devices: 0.01 us -> 42.3 us  [the longest x1 42.3 us: body(): lax.all_to_all(upper.reshape(128, HALF, BLK), ALL, 0, 0, tiled=True)]
    ppermute x15 -> x8, waiting for transfers between devices: 8.34 us -> 36.2 us  [flipped(): return lax.ppermute(x, axis, [(i, i ^ bits) for i in range(size)])]
    ppermute x15 -> x8, starting transfers between devices: 29.1 us -> 8.5 us  [flipped(): return lax.ppermute(x, axis, [(i, i ^ bits) for i in range(size)])]
    unnamed x72 -> x52, local copies, waits for them, and re-layouts: 35.2 us -> 20.1 us
    all_to_all x1, waiting for transfers between devices: 11.3 us -> 0.01 us  [body(): lower_recv = lax.all_to_all(lower, ALL, 0, 0, tiled=True)]
    all_to_all x1 -> x2, starting transfers between devices: 9.22 us -> 18.9 us  [the longest x1 12.1 us: body(): lax.all_to_all(upper.reshape(128, HALF, BLK), ALL, 0, 0, tiled=True)]
    ppermute x1, starting transfers between devices: 11.6 us -> 5.05 us  [body(): lax.ppermute(jnp.where(even, slices[:PC], slices[PC:]), ALL, swap_pairs(0))]
    all_to_all x1, waiting for transfers between devices: 9.3 us -> 15.5 us  [body(): lead_recv = lax.all_to_all(lead, ALL, 0, 0, tiled=True)]
  transfers between devices with their start and end apart: 27 -> 21, of which waited for: 10 -> 8; matrix products, arithmetic and copies ran while one was open for 4% -> 4% of each run, Pallas kernels for 22% -> 21%
where the time goes in v7:
time: 304 us; the launch traced here: 303 us
  waiting for transfers between devices  118 us (39%)
  Pallas kernels  73.6 us (24%)
  starting transfers between devices  71.1 us (23%)
  local copies, waits for them, and re-layouts  28.2 us (9%)
  other arithmetic  8.35 us (3%)
  between operations  3.76 us (1%)
    all_to_all x1, waiting for transfers between devices, body(): lax.all_to_all(upper.reshape(128, HALF, BLK), ALL, 0, 0, tiled=True)  42.3 us
    ppermute x8, waiting for transfers between devices, flipped(): return lax.ppermute(x, axis, [(i, i ^ bits) for i in range(size)])  36.2 us
    pallas_call x1, Pallas kernels, factor_inverse(): pl.pallas_call(factor_kernel, name='factor', in_specs=[vmem], out_specs=[...  33.5 us
    unnamed x52, local copies, waits for them, and re-layouts  20.1 us
    ppermute x3, waiting for transfers between devices, body(): lax.ppermute(first[:, :, k], 'col', [(0, k)])  17.8 us
    pallas_call x2, Pallas kernels, finish(): pl.pallas_call(final_kernel, name='finish', grid_spec=pltpu.PrefetchScala...  17.2 us
    all_to_all x1, waiting for transfers between devices, body(): lead_recv = lax.all_to_all(lead, ALL, 0, 0, tiled=True)  15.5 us
    pallas_call x1, Pallas kernels, make_panels(): pl.pallas_call(panel_kernel, name='panels', grid_spec=pltpu.PrefetchScala...  14.7 us
  transfers between devices with their start and end apart: 21, of which 8 were waited for; matrix products, arithmetic and copies ran while one was open for 4% of the time, Pallas kernels for 21%

profile of v7, /device:TPU:1, one launch (start us, length us, event | category | flops | bytes accessed | tf_op | source)
XLA Modules:
  0.0 302.7 jit_solution(18385171246680812682)
XLA Ops:
  3.8 4.4 %collective-permute-start = (f32[12,4,8,512]{3,2,0,1:T(8,128)S(1)}, f32[12,4,8,512]{3,2,0,1:T(8,128)S(1)}, u32[]{:S(2)}, u32[]{:S(2)}) collective-permute-start(f32[12,4,8,512]{3,2,0,1:T(8,128)S(1)} %bitcast.68), channel_id=1, source_target_pairs={{0,1},{4,5},{8,9},{12,13},{16,17},{20,21},{24,25},{28,29},{32,33},... | collective-permute-start | bytes 2359304 | tf_op jit(solution)/shard_map/ppermute | solution.py:416
  8.3 3.5 %collective-permute-start.1 = (f32[12,4,8,512]{3,2,0,1:T(8,128)S(1)}, f32[12,4,8,512]{3,2,0,1:T(8,128)}, u32[]{:S(2)}, u32[]{:S(2)}) collective-permute-start(f32[12,4,8,512]{3,2,0,1:T(8,128)S(1)} %bitcast.69), channel_id=1, source_target_pairs={{0,2},{4,6},{8,10},{12,14},{16,18},{20,22},{24,26},{28,30},{32,34}... | collective-permute-start | bytes 2359304 | tf_op jit(solution)/shard_map/ppermute | solution.py:416
  11.9 2.2 collective-permute-start.2
  14.2 3.4 %copy-done.1 = f32[1,1024,2048]{2,1,0:T(8,128)S(1)} copy-done((f32[1,1024,2048]{2,1,0:T(8,128)S(1)}, f32[1,1024,2048]{2,1,0:T(8,128)}, u32[]{:S(2)}) %copy-start.1) | copy-done | bytes 8388632
  24.4 16.9 %collective-permute-done.1 = f32[12,4,8,512]{3,2,0,1:T(8,128)} collective-permute-done((f32[12,4,8,512]{3,2,0,1:T(8,128)S(1)}, f32[12,4,8,512]{3,2,0,1:T(8,128)}, u32[]{:S(2)}, u32[]{:S(2)}) %collective-permute-start.1) | collective-permute-done | bytes 786464 | tf_op jit(solution)/shard_map/ppermute | solution.py:416
  41.3 12.1 %all-to-all-start = ((f32[128,64,128]{2,1,0:T(8,128)}), f32[128,64,128]{2,1,0:T(8,128)}, u32[]{:S(2)}, u32[]{:S(2)}) async-start(f32[128,64,128]{2,1,0:T(8,128)} %bitcast.58), calls=%async_computation | async-start | bytes 8388608 | tf_op jit(solution)/shard_map/all_to_all | solution.py:421
  58.3 3.5 %lead.1 = f32[4,8,4,24,128]{4,3,2,1,0:T(8,128)} custom-call(s32[8]{0:T(128)} %slice_reduce_fusion.1.keep_ref, s32[2]{0:T(128)} %get-tuple-element.65.info_ref, f32[1024,2048]{1,0:T(8,128)} %bitcast.54, f32[1536,768]{1,0:T(8,128)} %parent_ref.1), custom_call_target="tpu_custom_call" | custom-call | tf_op jit(solution)/shard_map/lead/pallas_call | solution.py:75
  61.8 42.3 %all-to-all-done.refs_0_.refs_1_.refs_2_.refs_3_.refs_4_.refs_5_.refs_6_.refs_7_.refs_8_.refs_9_.refs_10_.refs_11_.refs_12_.refs_13_.refs_14_.refs_15_ = f32[128,64,128]{2,1,0:T(8,128)} async-done(((f32[128,64,128]{2,1,0:T(8,128)}), f32[128,64,128]{2,1,0:T(8,128)}, u32[]{:S(2)}, u32[]{:S(2)}) %all-to-all-start) | async-done | bytes 4194336 | tf_op jit(solution)/shard_map/all_to_all | solution.py:421
  104.1 7.5 %all-to-all-start.1 = ((f32[128,24,128]{2,1,0:T(8,128)}), f32[128,24,128]{2,1,0:T(8,128)S(1)}, u32[]{:S(2)}, u32[]{:S(2)}) async-start(f32[128,24,128]{2,1,0:T(8,128)} %bitcast.65), calls=%async_computation.1 | async-start | bytes 3145728 | tf_op jit(solution)/shard_map/all_to_all | solution.py:425
  119.3 15.5 %all-to-all-done.1.recv_ref = f32[128,24,128]{2,1,0:T(8,128)S(1)} async-done(((f32[128,24,128]{2,1,0:T(8,128)}), f32[128,24,128]{2,1,0:T(8,128)S(1)}, u32[]{:S(2)}, u32[]{:S(2)}) %all-to-all-start.1) | async-done | bytes 1572896 | tf_op jit(solution)/shard_map/all_to_all | solution.py:425
  136.1 5.8 %all-to-all-start.2 = ((f32[128,16,128]{2,1,0:T(8,128)}), f32[128,16,128]{2,1,0:T(8,128)S(1)}, u32[]{:S(2)}, u32[]{:S(2)}) async-start(f32[128,16,128]{2,1,0:T(8,128)} %broadcast_in_dim.61), calls=%async_computation.2 | async-start | bytes 2097152 | tf_op jit(solution)/shard_map/all_to_all | solution.py:429
  144.4 2.7 slices.1
  148.1 5.1 %collective-permute-start.6 = (f32[6,8,512]{2,1,0:T(8,128)S(1)}, f32[6,8,512]{2,1,0:T(8,128)S(1)}, u32[]{:S(2)}, u32[]{:S(2)}) collective-permute-start(f32[6,8,512]{2,1,0:T(8,128)S(1)} %get-tuple-element.59), channel_id=1, source_target_pairs={{0,0},{1,1},{2,4},{3,5},{4,2},{5,3},{6,6},{7,7},{8,32},{9,33},{10,... | collective-permute-start | bytes 294920 | tf_op jit(solution)/shard_map/ppermute | solution.py:452
  154.6 2.7 collective-permute-done.6
  157.2 3.3 %collective-permute-done.7 = f32[6,8,512]{2,1,0:T(8,128)S(1)} collective-permute-done((f32[6,8,512]{2,1,0:T(8,128)S(1)}, f32[6,8,512]{2,1,0:T(8,128)S(1)}, u32[]{:S(2)}, u32[]{:S(2)}) %collective-permute-start.7) | collective-permute-done | bytes 98336 | tf_op jit(solution)/shard_map/ppermute | solution.py:453
  161.9 6.8 %all-to-all-start.3 = ((f32[8,96,512]{2,1,0:T(8,128)}), f32[8,96,512]{2,1,0:T(8,128)S(1)}, u32[]{:S(2)}, u32[]{:S(2)}) async-start(f32[8,96,512]{2,1,0:T(8,128)} %broadcast_in_dim.65), calls=%async_computation.3 | async-start | bytes 3145728 | tf_op jit(solution)/shard_map/all_to_all | solution.py:457
  169.1 20.5 %collective-permute-done.8 = f32[12,8,512]{2,1,0:T(8,128)S(1)} collective-permute-done((f32[12,8,512]{2,1,0:T(8,128)S(1)}, f32[12,8,512]{2,1,0:T(8,128)S(1)}, u32[]{:S(2)}, u32[]{:S(2)}) %collective-permute-start.8) | collective-permute-done | bytes 196640 | tf_op jit(solution)/shard_map/ppermute | solution.py:380
  189.7 4.7 %collective-permute-start.11 = (f32[2,12,8,512]{3,2,1,0:T(8,128)S(1)}, f32[2,12,8,512]{3,2,1,0:T(8,128)S(1)}, u32[]{:S(2)}, u32[]{:S(2)}) collective-permute-start(f32[2,12,8,512]{3,2,1,0:T(8,128)S(1)} %pad_maximum_fusion.refs_0_), channel_id=1, source_target_pairs={{0,3},{1,2},{2,1},{3,0},{4,7},{5,6},{6,5},{7,4},{8,11},{9,10},{10,... | collective-permute-start | bytes 1179656 | tf_op jit(solution)/shard_map/ppermute | solution.py:380
  196.2 15.6 %collective-permute-done.11.refs_3_ = f32[2,12,8,512]{3,2,1,0:T(8,128)S(1)} collective-permute-done((f32[2,12,8,512]{3,2,1,0:T(8,128)S(1)}, f32[2,12,8,512]{3,2,1,0:T(8,128)S(1)}, u32[]{:S(2)}, u32[]{:S(2)}) %collective-permute-start.11) | collective-permute-done | bytes 393248 | tf_op jit(solution)/shard_map/ppermute | solution.py:380
  217.9 9.9 %all-to-all-start.4 = ((f32[128,64,128]{2,1,0:T(8,128)}), f32[128,64,128]{2,1,0:T(8,128)}, u32[]{:S(2)}, u32[]{:S(2)}) async-start(f32[128,64,128]{2,1,0:T(8,128)} %bitcast.57), calls=%async_computation.4 | async-start | bytes 8388608 | tf_op jit(solution)/shard_map/all_to_all | solution.py:463
  229.3 33.5 %factor.1 = (bf16[512,512]{1,0:T(8,128)(2,1)S(1)}, bf16[512,512]{1,0:T(8,128)(2,1)S(1)}) custom-call(f32[128,16,128]{2,1,0:T(8,128)S(1)} %all-to-all-done.2.x_ref), custom_call_target="tpu_custom_call" | custom-call | tf_op jit(solution)/shard_map/factor/pallas_call | solution.py:225
  268.8 14.7 %panels.1 = (f32[1536,512]{1,0:T(8,128)}, bf16[768,512]{1,0:T(8,128)(2,1)S(1)}, bf16[768,512]{1,0:T(8,128)(2,1)S(1)}) custom-call(s32[2]{0:T(128)S(1)} %get-tuple-element.66.place_ref, f32[2,12,8,512]{3,2,1,0:T(8,128)S(1)} %pad_maximum_fusion.refs_0_, f32[2,12,8,512]{3,2,1,0:T(8,128)S(1)} %copy-done.9, f32[2,12,8,512]{3,2,1,0:T(8,128)S(1)} %copy-done.7, ...), custom_call_target="tpu_custom_call" | custom-call | tf_op jit(solution)/shard_map/panels/pallas_call | solution.py:281
  285.3 8.6 %finish.2.refs_20_ = f32[12,2,64,768]{3,2,1,0:T(8,128)} custom-call(s32[4,12]{1,0:T(4,128)} %broadcast_add_fusion.2.inv_row_ref, s32[4,6]{1,0:T(4,128)} %broadcast_add_fusion.1.inv_col_ref, s32[2]{0:T(128)} %add_convert_fusion.lead_ref, ...), custom_call_target="tpu_custom_call" | custom-call | tf_op jit(solution)/shard_map/finish/pallas_call | solution.py:359
  293.9 8.6 %finish.3 = f32[12,2,64,768]{3,2,1,0:T(8,128)} custom-call(s32[4,12]{1,0:T(4,128)} %broadcast_add_fusion.2.inv_row_ref, s32[4,6]{1,0:T(4,128)} %broadcast_add_fusion.1.inv_col_ref, s32[2]{0:T(128)} %add_convert_fusion.lead_ref, ...), custom_call_target="tpu_custom_call", output_to_operand_aliasing={{}: (23, {})} | custom-call | tf_op jit(solution)/shard_map/finish/pallas_call | solution.py:359
  (109 shorter events, 45.2 us)
Async XLA Ops:
  3.8 20.6 %collective-permute-start = (f32[12,4,8,512]{3,2,0,1:T(8,128)S(1)}, f32[12,4,8,512]{3,2,0,1:T(8,128)S(1)}, u32[]{:S(2)}, u32[]{:S(2)}) collective-permute-start(f32[12,4,8,512]{3,2,0,1:T(8,128)S(1)} %bitcast.68), channel_id=1, source_target_pairs={{0,1},{4,5},{8,9},{12,13},{16,17},{20,21},{24,25},{28,29},{32,33},... | collective-permute-start | bytes 2359304 | tf_op jit(solution)/shard_map/ppermute | solution.py:416
  8.3 32.9 %collective-permute-start.1 = (f32[12,4,8,512]{3,2,0,1:T(8,128)S(1)}, f32[12,4,8,512]{3,2,0,1:T(8,128)}, u32[]{:S(2)}, u32[]{:S(2)}) collective-permute-start(f32[12,4,8,512]{3,2,0,1:T(8,128)S(1)} %bitcast.69), channel_id=1, source_target_pairs={{0,2},{4,6},{8,10},{12,14},{16,18},{20,22},{24,26},{28,30},{32,34}... | collective-permute-start | bytes 2359304 | tf_op jit(solution)/shard_map/ppermute | solution.py:416
  11.9 29.3 %collective-permute-start.2 = (f32[12,4,8,512]{3,2,0,1:T(8,128)S(1)}, f32[12,4,8,512]{3,2,0,1:T(8,128)}, u32[]{:S(2)}, u32[]{:S(2)}) collective-permute-start(f32[12,4,8,512]{3,2,0,1:T(8,128)S(1)} %bitcast.70), channel_id=1, source_target_pairs={{0,3},{4,7},{8,11},{12,15},{16,19},{20,23},{24,27},{28,31},{32,35}... | collective-permute-start | bytes 2359304 | tf_op jit(solution)/shard_map/ppermute | solution.py:416
  24.4 16.9 %copy-start.21 = (f32[12,4,8,512]{3,2,0,1:T(8,128)}, f32[12,4,8,512]{3,2,0,1:T(8,128)S(1)}, u32[]{:S(2)}) copy-start(f32[12,4,8,512]{3,2,0,1:T(8,128)S(1)} %collective-permute-done) | copy-start | bytes 2359300
  41.3 62.8 %all-to-all-start = ((f32[128,64,128]{2,1,0:T(8,128)}), f32[128,64,128]{2,1,0:T(8,128)}, u32[]{:S(2)}, u32[]{:S(2)}) async-start(f32[128,64,128]{2,1,0:T(8,128)} %bitcast.58), calls=%async_computation | async-start | bytes 8388608 | tf_op jit(solution)/shard_map/all_to_all | solution.py:421
  58.3 54.3 %copy-start.19 = (f32[12,4,1,8,512]{4,3,2,1,0:T(8,128)S(1)}, f32[12,4,1,8,512]{4,3,2,1,0:T(8,128)}, u32[]{:S(2)}) copy-start(f32[12,4,1,8,512]{4,3,2,1,0:T(8,128)} %get-tuple-element.50) | copy-start | bytes 2359300
  104.1 30.7 %all-to-all-start.1 = ((f32[128,24,128]{2,1,0:T(8,128)}), f32[128,24,128]{2,1,0:T(8,128)S(1)}, u32[]{:S(2)}, u32[]{:S(2)}) async-start(f32[128,24,128]{2,1,0:T(8,128)} %bitcast.65), calls=%async_computation.1 | async-start | bytes 3145728 | tf_op jit(solution)/shard_map/all_to_all | solution.py:425
  115.4 27.1 %collective-permute-start.4 = (f32[12,8,512]{2,1,0:T(8,128)}, f32[12,8,512]{2,1,0:T(8,128)}, u32[]{:S(2)}, u32[]{:S(2)}) collective-permute-start(f32[12,8,512]{2,1,0:T(8,128)} %get-tuple-element.54), channel_id=1, source_target_pairs={{0,64},{1,65},{2,66},{3,67},{4,68},{5,69},{6,70},{7,71},{8,72},{9,... | collective-permute-start | bytes 589832 | tf_op jit(solution)/shard_map/ppermute | solution.py:431
  116.7 25.8 %collective-permute-start.5 = (f32[12,8,512]{2,1,0:T(8,128)}, f32[12,8,512]{2,1,0:T(8,128)}, u32[]{:S(2)}, u32[]{:S(2)}) collective-permute-start(f32[12,8,512]{2,1,0:T(8,128)} %get-tuple-element.55), channel_id=1, source_target_pairs={{0,96},{1,97},{2,98},{3,99},{4,100},{5,101},{6,102},{7,103},{8,104... | collective-permute-start | bytes 589832 | tf_op jit(solution)/shard_map/ppermute | solution.py:431
  118.1 24.5 %collective-permute-start.3 = (f32[12,8,512]{2,1,0:T(8,128)}, f32[12,8,512]{2,1,0:T(8,128)}, u32[]{:S(2)}, u32[]{:S(2)}) collective-permute-start(f32[12,8,512]{2,1,0:T(8,128)} %get-tuple-element.56), channel_id=1, source_target_pairs={{0,32},{1,33},{2,34},{3,35},{4,36},{5,37},{6,38},{7,39},{8,40},{9,... | collective-permute-start | bytes 589832 | tf_op jit(solution)/shard_map/ppermute | solution.py:431
  136.1 24.4 %all-to-all-start.2 = ((f32[128,16,128]{2,1,0:T(8,128)}), f32[128,16,128]{2,1,0:T(8,128)S(1)}, u32[]{:S(2)}, u32[]{:S(2)}) async-start(f32[128,16,128]{2,1,0:T(8,128)} %broadcast_in_dim.61), calls=%async_computation.2 | async-start | bytes 2097152 | tf_op jit(solution)/shard_map/all_to_all | solution.py:429
  147.1 21.6 %copy-start.20 = (f32[12,8,512]{2,1,0:T(8,128)S(1)}, f32[12,8,512]{2,1,0:T(8,128)}, u32[]{:S(2)}) copy-start(f32[12,8,512]{2,1,0:T(8,128)} %slices.1) | copy-start | bytes 589828
  148.1 9.1 %collective-permute-start.6 = (f32[6,8,512]{2,1,0:T(8,128)S(1)}, f32[6,8,512]{2,1,0:T(8,128)S(1)}, u32[]{:S(2)}, u32[]{:S(2)}) collective-permute-start(f32[6,8,512]{2,1,0:T(8,128)S(1)} %get-tuple-element.59), channel_id=1, source_target_pairs={{0,0},{1,1},{2,4},{3,5},{4,2},{5,3},{6,6},{7,7},{8,32},{9,33},{10,... | collective-permute-start | bytes 294920 | tf_op jit(solution)/shard_map/ppermute | solution.py:452
  153.2 7.3 %collective-permute-start.7 = (f32[6,8,512]{2,1,0:T(8,128)S(1)}, f32[6,8,512]{2,1,0:T(8,128)S(1)}, u32[]{:S(2)}, u32[]{:S(2)}) collective-permute-start(f32[6,8,512]{2,1,0:T(8,128)S(1)} %get-tuple-element.60), channel_id=1, source_target_pairs={{0,1},{1,0},{2,5},{3,4},{4,3},{5,2},{6,7},{7,6},{8,33},{9,32},{10,... | collective-permute-start | bytes 294920 | tf_op jit(solution)/shard_map/ppermute | solution.py:453
  161.9 56.0 %all-to-all-start.3 = ((f32[8,96,512]{2,1,0:T(8,128)}), f32[8,96,512]{2,1,0:T(8,128)S(1)}, u32[]{:S(2)}, u32[]{:S(2)}) async-start(f32[8,96,512]{2,1,0:T(8,128)} %broadcast_in_dim.65), calls=%async_computation.3 | async-start | bytes 3145728 | tf_op jit(solution)/shard_map/all_to_all | solution.py:457
  168.7 20.9 %collective-permute-start.8 = (f32[12,8,512]{2,1,0:T(8,128)S(1)}, f32[12,8,512]{2,1,0:T(8,128)S(1)}, u32[]{:S(2)}, u32[]{:S(2)}) collective-permute-start(f32[12,8,512]{2,1,0:T(8,128)S(1)} %copy-done.20), channel_id=1, source_target_pairs={{0,64},{32,96},{64,0},{96,32},{1,65},{33,97},{65,1},{97,33},{2,66}... | collective-permute-start | bytes 589832 | tf_op jit(solution)/shard_map/ppermute | solution.py:380
  189.7 22.1 %collective-permute-start.11 = (f32[2,12,8,512]{3,2,1,0:T(8,128)S(1)}, f32[2,12,8,512]{3,2,1,0:T(8,128)S(1)}, u32[]{:S(2)}, u32[]{:S(2)}) collective-permute-start(f32[2,12,8,512]{3,2,1,0:T(8,128)S(1)} %pad_maximum_fusion.refs_0_), channel_id=1, source_target_pairs={{0,3},{1,2},{2,1},{3,0},{4,7},{5,6},{6,5},{7,4},{8,11},{9,10},{10,... | collective-permute-start | bytes 1179656 | tf_op jit(solution)/shard_map/ppermute | solution.py:380
  194.4 18.5 %collective-permute-start.10 = (f32[2,12,8,512]{3,2,1,0:T(8,128)S(1)}, f32[2,12,8,512]{3,2,1,0:T(8,128)S(1)}, u32[]{:S(2)}, u32[]{:S(2)}) collective-permute-start(f32[2,12,8,512]{3,2,1,0:T(8,128)S(1)} %pad_maximum_fusion.refs_0_), channel_id=1, source_target_pairs={{0,2},{1,3},{2,0},{3,1},{4,6},{5,7},{6,4},{7,5},{8,10},{9,11},{10,... | collective-permute-start | bytes 1179656 | tf_op jit(solution)/shard_map/ppermute | solution.py:380
  194.4 19.3 %collective-permute-start.9 = (f32[2,12,8,512]{3,2,1,0:T(8,128)S(1)}, f32[2,12,8,512]{3,2,1,0:T(8,128)S(1)}, u32[]{:S(2)}, u32[]{:S(2)}) collective-permute-start(f32[2,12,8,512]{3,2,1,0:T(8,128)S(1)} %pad_maximum_fusion.refs_0_), channel_id=1, source_target_pairs={{0,1},{1,0},{2,3},{3,2},{4,5},{5,4},{6,7},{7,6},{8,9},{9,8},{10,11... | collective-permute-start | bytes 1179656 | tf_op jit(solution)/shard_map/ppermute | solution.py:380
  195.1 19.8 %collective-permute-start.12 = (f32[2,12,8,512]{3,2,1,0:T(8,128)S(1)}, f32[2,12,8,512]{3,2,1,0:T(8,128)S(1)}, u32[]{:S(2)}, u32[]{:S(2)}) collective-permute-start(f32[2,12,8,512]{3,2,1,0:T(8,128)S(1)} %pad_maximum_fusion.refs_0_), channel_id=1, source_target_pairs={{0,32},{32,0},{64,96},{96,64},{1,33},{33,1},{65,97},{97,65},{2,34}... | collective-permute-start | bytes 1179656 | tf_op jit(solution)/shard_map/ppermute | solution.py:380
  211.8 3.9 %collective-permute-start.15 = (f32[2,12,8,512]{3,2,1,0:T(8,128)S(1)}, f32[2,12,8,512]{3,2,1,0:T(8,128)S(1)}, u32[]{:S(2)}, u32[]{:S(2)}) collective-permute-start(f32[2,12,8,512]{3,2,1,0:T(8,128)S(1)} %collective-permute-done.11.refs_3_), channel_id=1, source_target_pairs={{0,32},{32,0},{64,96},{96,64},{1,33},{33,1},{65,97},{97,65},{2,34}... | collective-permute-start | bytes 1179656 | tf_op jit(solution)/shard_map/ppermute | solution.py:380
  212.9 3.5 %collective-permute-start.14 = (f32[2,12,8,512]{3,2,1,0:T(8,128)S(1)}, f32[2,12,8,512]{3,2,1,0:T(8,128)S(1)}, u32[]{:S(2)}, u32[]{:S(2)}) collective-permute-start(f32[2,12,8,512]{3,2,1,0:T(8,128)S(1)} %collective-permute-done.10.refs_2_), channel_id=1, source_target_pairs={{0,32},{32,0},{64,96},{96,64},{1,33},{33,1},{65,97},{97,65},{2,34}... | collective-permute-start | bytes 1179656 | tf_op jit(solution)/shard_map/ppermute | solution.py:380
  213.7 3.5 %collective-permute-start.13 = (f32[2,12,8,512]{3,2,1,0:T(8,128)S(1)}, f32[2,12,8,512]{3,2,1,0:T(8,128)S(1)}, u32[]{:S(2)}, u32[]{:S(2)}) collective-permute-start(f32[2,12,8,512]{3,2,1,0:T(8,128)S(1)} %collective-permute-done.9.refs_1_), channel_id=1, source_target_pairs={{0,32},{32,0},{64,96},{96,64},{1,33},{33,1},{65,97},{97,65},{2,34}... | collective-permute-start | bytes 1179656 | tf_op jit(solution)/shard_map/ppermute | solution.py:380
  217.9 75.9 %all-to-all-start.4 = ((f32[128,64,128]{2,1,0:T(8,128)}), f32[128,64,128]{2,1,0:T(8,128)}, u32[]{:S(2)}, u32[]{:S(2)}) async-start(f32[128,64,128]{2,1,0:T(8,128)} %bitcast.57), calls=%async_computation.4 | async-start | bytes 8388608 | tf_op jit(solution)/shard_map/all_to_all | solution.py:463
  (21 other events, 56.7 us)

commit v8 on v7

--- a/solution.py
+++ b/solution.py
@@ -411,22 +411,21 @@
     info = jnp.stack([corner_place, holder.astype(jnp.int32)]).astype(jnp.int32)
 
     lead = make_lead(window[:, 0], info, local, parent_entries).reshape(128, 24, BLK)
+    lead_recv = lax.all_to_all(lead, ALL, 0, 0, tiled=True)
 
     first = parent_entries[:, :W].reshape(PR, FRONTS, COLS, 8, W)
     sent = [lax.ppermute(first[:, :, k], "col", [(0, k)]) for k in range(1, COLS)]
-    first = first[:, :, 0]
-
-    upper, lower = pack(window, local)
-    upper, sent[0], sent[1], sent[2] = lax.optimization_barrier((upper, *sent))
-    upper_recv = lax.all_to_all(upper.reshape(128, HALF, BLK), ALL, 0, 0, tiled=True)
-    first = jnp.where(col == 0, first, (sent[0] + sent[1]) + sent[2])
-
-    lead, upper_recv = lax.optimization_barrier((lead, upper_recv))
-    lead_recv = lax.all_to_all(lead, ALL, 0, 0, tiled=True)
+    first = jnp.where(col == 0, first[:, :, 0], (sent[0] + sent[1]) + sent[2])
 
     tiles = jnp.sum(lead_recv[:, 8:], axis=0)
     tiles = jnp.broadcast_to(tiles[None], (128, 16, BLK))
     tiles = lax.all_to_all(tiles, ALL, 0, 0, tiled=True)
+
+    upper, lower = pack(window, local)
+    upper, first, tiles = lax.optimization_barrier((upper.reshape(128, HALF, BLK), first, tiles))
+    upper_recv = lax.all_to_all(upper, ALL, 0, 0, tiled=True)
+    inverses = factor_inverse(tiles)
+    first, *inverses = lax.optimization_barrier((first, *inverses))
 
     sent = [lax.ppermute(first[:, k], "front", [(0, k)]) for k in range(1, FRONTS)]
     first = jnp.where(front == 0, first[:, 0], (sent[0] + sent[1]) + sent[2])
@@ -444,22 +443,23 @@
 
     place = jnp.stack([row, group]).astype(jnp.int32)
 
-    pair = jnp.stack([slices, flipped(slices, "front", 2)])
-    pair = [pair] + [flipped(pair, "col", bits) for bits in range(1, COLS)]
-    rows_raw = pair + [flipped(x, "front", 1) for x in pair]
-
     even = group % 2 == 0
     one = lax.ppermute(jnp.where(even, slices[:PC], slices[PC:]), ALL, swap_pairs(0))
     two = lax.ppermute(jnp.where(even, slices[PC:], slices[:PC]), ALL, swap_pairs(1))
     mine = jnp.stack([jnp.where(even, one, two), jnp.where(even, two, one)], axis=1)
     mine = mine.reshape(PC, 16, W)
+    pair = jnp.stack([slices, flipped(slices, "front", 2)])
+    pair = [pair] + [flipped(pair, "col", bits) for bits in range(1, COLS)]
+    mine, *pair = lax.optimization_barrier((mine, *pair))
+    rows_raw = pair + [flipped(x, "front", 1) for x in pair]
+
+    mine, upper_recv = lax.optimization_barrier((mine, upper_recv))
     mine = jnp.broadcast_to(mine.reshape(1, PC * 16, W), (ROWS, PC * 16, W))
     cols_raw = lax.all_to_all(mine, "row", 0, 0, tiled=True).reshape(ROWS, PC, 16, W)
 
-    lower, tiles, cols_raw, rows_raw = lax.optimization_barrier(
-        (lower.reshape(128, HALF, BLK), tiles, cols_raw, rows_raw)
+    lower, cols_raw, rows_raw = lax.optimization_barrier(
+        (lower.reshape(128, HALF, BLK), cols_raw, rows_raw)
     )
-    inverses = factor_inverse(tiles)
     lower_recv = lax.all_to_all(lower, ALL, 0, 0, tiled=True)
     panel, high, low = make_panels(place, rows_raw, cols_raw, inverses)
     lead_flags = jnp.stack([row == 0, group == 0]).astype(jnp.int32)

time: 304 us -> 279 us (0.918)
  waiting for transfers between devices: 118 us -> 86.2 us
  starting transfers between devices: 71.1 us -> 76.9 us
    all_to_all x1, waiting for transfers between devices: 42.3 us -> 0.01 us  [body(): upper_recv = lax.all_to_all(upper, ALL, 0, 0, tiled=True)]
    ppermute x8, waiting for transfers between devices: 36.2 us -> 17.4 us  [flipped(): return lax.ppermute(x, axis, [(i, i ^ bits) for i in range(size)])]
    all_to_all x1, waiting for transfers between devices: 0.01 us -> 18.6 us  [body(): lower_recv = lax.all_to_all(lower, ALL, 0, 0, tiled=True)]
    all_to_all x1, waiting for transfers between devices: 0.01 us -> 15.1 us  [body(): lax.all_to_all(mine, 'row', 0, 0, tiled=True).reshape(ROWS, PC, 16, W)]
    ppermute x8, starting transfers between devices: 8.5 us -> 14.9 us  [flipped(): return lax.ppermute(x, axis, [(i, i ^ bits) for i in range(size)])]
    all_to_all x1, waiting for transfers between devices: 15.5 us -> 9.22 us  [body(): lead_recv = lax.all_to_all(lead, ALL, 0, 0, tiled=True)]
    all_to_all x1, starting transfers between devices: 7.48 us -> 11.9 us  [body(): lead_recv = lax.all_to_all(lead, ALL, 0, 0, tiled=True)]
    ppermute x3, waiting for transfers between devices: 0.01 us -> 4.21 us  [body(): lax.ppermute(first[:, k], 'front', [(0, k)])]
  transfers between devices with their start and end apart: 21 -> 21, of which waited for: 8 -> 9; matrix products, arithmetic and copies ran while one was open for 4% -> 5% of each run, Pallas kernels for 21% -> 22%
where the time goes in v8:
time: 279 us; the launch traced here: 276 us
  waiting for transfers between devices  86.2 us (31%)
  starting transfers between devices  76.9 us (28%)
  Pallas kernels  74.2 us (27%)
  local copies, waits for them, and re-layouts  26.1 us (9%)
  other arithmetic  9.39 us (3%)
  between operations  3.72 us (1%)
    pallas_call x1, Pallas kernels, factor_inverse(): pl.pallas_call(factor_kernel, name='factor', in_specs=[vmem], out_specs=[...  33.5 us
    ppermute x3, waiting for transfers between devices, body(): lax.ppermute(first[:, :, k], 'col', [(0, k)])  21.7 us
    unnamed x42, local copies, waits for them, and re-layouts  20.2 us
    all_to_all x1, waiting for transfers between devices, body(): lower_recv = lax.all_to_all(lower, ALL, 0, 0, tiled=True)  18.6 us
    ppermute x8, waiting for transfers between devices, flipped(): return lax.ppermute(x, axis, [(i, i ^ bits) for i in range(size)])  17.4 us
    pallas_call x2, Pallas kernels, finish(): pl.pallas_call(final_kernel, name='finish', grid_spec=pltpu.PrefetchScala...  17.3 us
    pallas_call x1, Pallas kernels, make_panels(): pl.pallas_call(panel_kernel, name='panels', grid_spec=pltpu.PrefetchScala...  15.4 us
    all_to_all x1, waiting for transfers between devices, body(): lax.all_to_all(mine, 'row', 0, 0, tiled=True).reshape(ROWS, PC, 16, W)  15.1 us
  transfers between devices with their start and end apart: 21, of which 9 were waited for; matrix products, arithmetic and copies ran while one was open for 5% of the time, Pallas kernels for 22%

profile of v8, /device:TPU:1, one launch (start us, length us, event | category | flops | bytes accessed | tf_op | source)
XLA Modules:
  0.0 276.5 jit_solution(811832075780429131)
XLA Ops:
  6.3 3.4 %lead.1 = f32[4,8,4,24,128]{4,3,2,1,0:T(8,128)} custom-call(s32[8]{0:T(128)} %slice_reduce_fusion.1.keep_ref, s32[2]{0:T(128)} %get-tuple-element.77.info_ref, f32[1024,2048]{1,0:T(8,128)} %bitcast.54, f32[1536,768]{1,0:T(8,128)} %parent_ref.1), custom_call_target="tpu_custom_call" | custom-call | tf_op jit(solution)/shard_map/lead/pallas_call | solution.py:75
  9.6 11.9 %all-to-all-start = ((f32[128,24,128]{2,1,0:T(8,128)}), f32[128,24,128]{2,1,0:T(8,128)}, u32[]{:S(2)}, u32[]{:S(2)}) async-start(f32[128,24,128]{2,1,0:T(8,128)} %bitcast.65), calls=%async_computation | async-start | bytes 3145728 | tf_op jit(solution)/shard_map/all_to_all | solution.py:414
  22.8 6.1 %collective-permute-start.2 = (f32[12,4,8,512]{3,2,0,1:T(8,128)S(1)}, f32[12,4,8,512]{3,2,0,1:T(8,128)}, u32[]{:S(2)}, u32[]{:S(2)}) collective-permute-start(f32[12,4,8,512]{3,2,0,1:T(8,128)S(1)} %bitcast.68), channel_id=1, source_target_pairs={{0,3},{4,7},{8,11},{12,15},{16,19},{20,23},{24,27},{28,31},{32,35}... | collective-permute-start | bytes 2359304 | tf_op jit(solution)/shard_map/ppermute | solution.py:417
  35.2 9.2 %all-to-all-done.recv_ref = f32[128,24,128]{2,1,0:T(8,128)} async-done(((f32[128,24,128]{2,1,0:T(8,128)}), f32[128,24,128]{2,1,0:T(8,128)}, u32[]{:S(2)}, u32[]{:S(2)}) %all-to-all-start) | async-done | bytes 1572896 | tf_op jit(solution)/shard_map/all_to_all | solution.py:414
  46.9 5.8 %all-to-all-start.1 = ((f32[128,16,128]{2,1,0:T(8,128)}), f32[128,16,128]{2,1,0:T(8,128)S(1)}, u32[]{:S(2)}, u32[]{:S(2)}) async-start(f32[128,16,128]{2,1,0:T(8,128)} %broadcast_in_dim.63), calls=%async_computation.1 | async-start | bytes 2097152 | tf_op jit(solution)/shard_map/all_to_all | solution.py:422
  52.7 3.4 %copy-done.1 = f32[1,1024,2048]{2,1,0:T(8,128)S(1)} copy-done((f32[1,1024,2048]{2,1,0:T(8,128)S(1)}, f32[1,1024,2048]{2,1,0:T(8,128)}, u32[]{:S(2)}) %copy-start.1) | copy-done | bytes 8388632
  61.9 5.3 %collective-permute-done.2 = f32[12,4,8,512]{3,2,0,1:T(8,128)} collective-permute-done((f32[12,4,8,512]{3,2,0,1:T(8,128)S(1)}, f32[12,4,8,512]{3,2,0,1:T(8,128)}, u32[]{:S(2)}, u32[]{:S(2)}) %collective-permute-start.2) | collective-permute-done | bytes 786464 | tf_op jit(solution)/shard_map/ppermute | solution.py:417
  67.2 16.4 %collective-permute-done.1 = f32[12,4,8,512]{3,2,0,1:T(8,128)} collective-permute-done((f32[12,4,8,512]{3,2,0,1:T(8,128)}, f32[12,4,8,512]{3,2,0,1:T(8,128)}, u32[]{:S(2)}, u32[]{:S(2)}) %collective-permute-start.1) | collective-permute-done | bytes 786464 | tf_op jit(solution)/shard_map/ppermute | solution.py:417
  85.6 9.2 %all-to-all-start.2 = ((f32[128,64,128]{2,1,0:T(8,128)}), f32[128,64,128]{2,1,0:T(8,128)}, u32[]{:S(2)}, u32[]{:S(2)}) async-start(f32[128,64,128]{2,1,0:T(8,128)} %bitcast.58), calls=%async_computation.2 | async-start | bytes 8388608 | tf_op jit(solution)/shard_map/all_to_all | solution.py:426
  95.8 33.5 %factor.1 = (bf16[512,512]{1,0:T(8,128)(2,1)S(1)}, bf16[512,512]{1,0:T(8,128)(2,1)S(1)}) custom-call(f32[128,16,128]{2,1,0:T(8,128)S(1)} %all-to-all-done.1.x_ref), custom_call_target="tpu_custom_call" | custom-call | tf_op jit(solution)/shard_map/factor/pallas_call | solution.py:225
  132.7 4.2 %collective-permute-done.3 = f32[12,8,512]{2,1,0:T(8,128)S(1)} collective-permute-done((f32[12,8,512]{2,1,0:T(8,128)S(1)}, f32[12,8,512]{2,1,0:T(8,128)S(1)}, u32[]{:S(2)}, u32[]{:S(2)}) %collective-permute-start.3) | collective-permute-done | bytes 196640 | tf_op jit(solution)/shard_map/ppermute | solution.py:430
  137.6 2.7 slices.1
  140.4 8.9 %collective-permute-start.8 = (f32[12,8,512]{2,1,0:T(8,128)}, f32[12,8,512]{2,1,0:T(8,128)S(1)}, u32[]{:S(2)}, u32[]{:S(2)}) collective-permute-start(f32[12,8,512]{2,1,0:T(8,128)} %slices.1), channel_id=1, source_target_pairs={{0,64},{32,96},{64,0},{96,32},{1,65},{33,97},{65,1},{97,33},{2,66}... | collective-permute-start | bytes 589832 | tf_op jit(solution)/shard_map/ppermute | solution.py:380
  150.2 3.1 %collective-permute-start.6 = (f32[6,8,512]{2,1,0:T(8,128)S(1)}, f32[6,8,512]{2,1,0:T(8,128)S(1)}, u32[]{:S(2)}, u32[]{:S(2)}) collective-permute-start(f32[6,8,512]{2,1,0:T(8,128)S(1)} %get-tuple-element.71), channel_id=1, source_target_pairs={{0,0},{1,1},{2,4},{3,5},{4,2},{5,3},{6,6},{7,7},{8,32},{9,33},{10,... | collective-permute-start | bytes 294920 | tf_op jit(solution)/shard_map/ppermute | solution.py:447
  153.3 3.1 %collective-permute-start.7 = (f32[6,8,512]{2,1,0:T(8,128)S(1)}, f32[6,8,512]{2,1,0:T(8,128)S(1)}, u32[]{:S(2)}, u32[]{:S(2)}) collective-permute-start(f32[6,8,512]{2,1,0:T(8,128)S(1)} %get-tuple-element.72), channel_id=1, source_target_pairs={{0,1},{1,0},{2,5},{3,4},{4,3},{5,2},{6,7},{7,6},{8,33},{9,32},{10,... | collective-permute-start | bytes 294920 | tf_op jit(solution)/shard_map/ppermute | solution.py:448
  157.3 4.0 %collective-permute-start.11 = (f32[2,12,8,512]{3,2,1,0:T(8,128)S(1)}, f32[2,12,8,512]{3,2,1,0:T(8,128)S(1)}, u32[]{:S(2)}, u32[]{:S(2)}) collective-permute-start(f32[2,12,8,512]{3,2,1,0:T(8,128)S(1)} %pad_maximum_fusion.refs_0_), channel_id=1, source_target_pairs={{0,3},{1,2},{2,1},{3,0},{4,7},{5,6},{6,5},{7,4},{8,11},{9,10},{10,... | collective-permute-start | bytes 1179656 | tf_op jit(solution)/shard_map/ppermute | solution.py:380
  162.1 16.2 %collective-permute-done.11.refs_3_ = f32[2,12,8,512]{3,2,1,0:T(8,128)S(1)} collective-permute-done((f32[2,12,8,512]{3,2,1,0:T(8,128)S(1)}, f32[2,12,8,512]{3,2,1,0:T(8,128)S(1)}, u32[]{:S(2)}, u32[]{:S(2)}) %collective-permute-start.11) | collective-permute-done | bytes 393248 | tf_op jit(solution)/shard_map/ppermute | solution.py:380
  180.4 7.8 %all-to-all-start.3 = ((f32[8,96,512]{2,1,0:T(8,128)}), f32[8,96,512]{2,1,0:T(8,128)S(1)}, u32[]{:S(2)}, u32[]{:S(2)}) async-start(f32[8,96,512]{2,1,0:T(8,128)} %broadcast_in_dim.65), calls=%async_computation.3 | async-start | bytes 3145728 | tf_op jit(solution)/shard_map/all_to_all | solution.py:458
  193.7 15.1 %all-to-all-done.3 = f32[8,96,512]{2,1,0:T(8,128)S(1)} async-done(((f32[8,96,512]{2,1,0:T(8,128)}), f32[8,96,512]{2,1,0:T(8,128)S(1)}, u32[]{:S(2)}, u32[]{:S(2)}) %all-to-all-start.3) | async-done | bytes 1572896 | tf_op jit(solution)/shard_map/all_to_all | solution.py:458
  208.7 8.2 %all-to-all-start.4 = ((f32[128,64,128]{2,1,0:T(8,128)}), f32[128,64,128]{2,1,0:T(8,128)}, u32[]{:S(2)}, u32[]{:S(2)}) async-start(f32[128,64,128]{2,1,0:T(8,128)} %bitcast.57), calls=%async_computation.4 | async-start | bytes 8388608 | tf_op jit(solution)/shard_map/all_to_all | solution.py:463
  223.3 15.4 %panels.1 = (f32[1536,512]{1,0:T(8,128)}, bf16[768,512]{1,0:T(8,128)(2,1)S(1)}, bf16[768,512]{1,0:T(8,128)(2,1)S(1)}) custom-call(s32[2]{0:T(128)S(1)} %get-tuple-element.78.place_ref, f32[2,12,8,512]{3,2,1,0:T(8,128)S(1)} %pad_maximum_fusion.refs_0_, f32[2,12,8,512]{3,2,1,0:T(8,128)} %collective-permute-done.9.refs_1_, f32[2,12,8,512]{3,2,1,0:T(8,128)S(1)} %copy-done.7, ...), custom_call_target="tpu_custom_call" | custom-call | tf_op jit(solution)/shard_map/panels/pallas_call | solution.py:281
  240.4 8.6 %finish.2.refs_20_ = f32[12,2,64,768]{3,2,1,0:T(8,128)} custom-call(s32[4,12]{1,0:T(4,128)} %broadcast_add_fusion.2.inv_row_ref, s32[4,6]{1,0:T(4,128)} %broadcast_add_fusion.1.inv_col_ref, s32[2]{0:T(128)} %add_convert_fusion.lead_ref, ...), custom_call_target="tpu_custom_call" | custom-call | tf_op jit(solution)/shard_map/finish/pallas_call | solution.py:359
  249.1 18.6 %all-to-all-done.4.refs_0_.refs_1_.refs_2_.refs_3_.refs_4_.refs_5_.refs_6_.refs_7_.refs_8_.refs_9_.refs_10_.refs_11_.refs_12_.refs_13_.refs_14_.refs_15_ = f32[128,64,128]{2,1,0:T(8,128)} async-done(((f32[128,64,128]{2,1,0:T(8,128)}), f32[128,64,128]{2,1,0:T(8,128)}, u32[]{:S(2)}, u32[]{:S(2)}) %all-to-all-start.4) | async-done | bytes 4194336 | tf_op jit(solution)/shard_map/all_to_all | solution.py:463
  267.7 8.6 %finish.3 = f32[12,2,64,768]{3,2,1,0:T(8,128)} custom-call(s32[4,12]{1,0:T(4,128)} %broadcast_add_fusion.2.inv_row_ref, s32[4,6]{1,0:T(4,128)} %broadcast_add_fusion.1.inv_col_ref, s32[2]{0:T(128)} %add_convert_fusion.lead_ref, ...), custom_call_target="tpu_custom_call", output_to_operand_aliasing={{}: (23, {})} | custom-call | tf_op jit(solution)/shard_map/finish/pallas_call | solution.py:359
  (98 shorter events, 44.3 us)
Async XLA Ops:
  9.6 11.9 %slice-start = ((f32[1536,768]{1,0:T(8,128)}), f32[1536,512]{1,0:T(8,128)S(1)}, s32[]{:S(2)}) async-start(f32[1536,768]{1,0:T(8,128)} %parent_ref.1), calls=%async_computation.5 | async-start | bytes 6291456 | tf_op jit(solution)/shard_map/slice | solution.py:416
  9.6 34.8 %all-to-all-start = ((f32[128,24,128]{2,1,0:T(8,128)}), f32[128,24,128]{2,1,0:T(8,128)}, u32[]{:S(2)}, u32[]{:S(2)}) async-start(f32[128,24,128]{2,1,0:T(8,128)} %bitcast.65), calls=%async_computation | async-start | bytes 3145728 | tf_op jit(solution)/shard_map/all_to_all | solution.py:414
  22.8 44.4 %collective-permute-start.2 = (f32[12,4,8,512]{3,2,0,1:T(8,128)S(1)}, f32[12,4,8,512]{3,2,0,1:T(8,128)}, u32[]{:S(2)}, u32[]{:S(2)}) collective-permute-start(f32[12,4,8,512]{3,2,0,1:T(8,128)S(1)} %bitcast.68), channel_id=1, source_target_pairs={{0,3},{4,7},{8,11},{12,15},{16,19},{20,23},{24,27},{28,31},{32,35}... | collective-permute-start | bytes 2359304 | tf_op jit(solution)/shard_map/ppermute | solution.py:417
  29.9 37.3 %collective-permute-start = (f32[12,4,8,512]{3,2,0,1:T(8,128)}, f32[12,4,8,512]{3,2,0,1:T(8,128)}, u32[]{:S(2)}, u32[]{:S(2)}) collective-permute-start(f32[12,4,8,512]{3,2,0,1:T(8,128)} %bitcast.53), channel_id=1, source_target_pairs={{0,1},{4,5},{8,9},{12,13},{16,17},{20,21},{24,25},{28,29},{32,33},... | collective-permute-start | bytes 2359304 | tf_op jit(solution)/shard_map/ppermute | solution.py:417
  33.1 50.6 %collective-permute-start.1 = (f32[12,4,8,512]{3,2,0,1:T(8,128)}, f32[12,4,8,512]{3,2,0,1:T(8,128)}, u32[]{:S(2)}, u32[]{:S(2)}) collective-permute-start(f32[12,4,8,512]{3,2,0,1:T(8,128)} %bitcast.52), channel_id=1, source_target_pairs={{0,2},{4,6},{8,10},{12,14},{16,18},{20,22},{24,26},{28,30},{32,34}... | collective-permute-start | bytes 2359304 | tf_op jit(solution)/shard_map/ppermute | solution.py:417
  46.9 38.7 %all-to-all-start.1 = ((f32[128,16,128]{2,1,0:T(8,128)}), f32[128,16,128]{2,1,0:T(8,128)S(1)}, u32[]{:S(2)}, u32[]{:S(2)}) async-start(f32[128,16,128]{2,1,0:T(8,128)} %broadcast_in_dim.63), calls=%async_computation.1 | async-start | bytes 2097152 | tf_op jit(solution)/shard_map/all_to_all | solution.py:422
  56.0 27.6 %copy-start.16 = (f32[12,4,1,8,512]{4,3,2,1,0:T(8,128)S(1)}, f32[12,4,1,8,512]{4,3,2,1,0:T(8,128)}, u32[]{:S(2)}) copy-start(f32[12,4,1,8,512]{4,3,2,1,0:T(8,128)} %get-tuple-element.64) | copy-start | bytes 2359300
  85.6 9.2 %copy-start.17 = (s32[4,64]{1,0:T(4,128)S(1)}, s32[4,64]{1,0:T(4,128)}, u32[]{:S(2)}) copy-start(s32[4,64]{1,0:T(4,128)} %param.6) | copy-start | bytes 3076
  85.6 93.4 %all-to-all-start.2 = ((f32[128,64,128]{2,1,0:T(8,128)}), f32[128,64,128]{2,1,0:T(8,128)}, u32[]{:S(2)}, u32[]{:S(2)}) async-start(f32[128,64,128]{2,1,0:T(8,128)} %bitcast.58), calls=%async_computation.2 | async-start | bytes 8388608 | tf_op jit(solution)/shard_map/all_to_all | solution.py:426
  129.4 3.3 %collective-permute-start.4 = (f32[12,8,512]{2,1,0:T(8,128)S(1)}, f32[12,8,512]{2,1,0:T(8,128)S(1)}, u32[]{:S(2)}, u32[]{:S(2)}) collective-permute-start(f32[12,8,512]{2,1,0:T(8,128)S(1)} %get-tuple-element.66), channel_id=1, source_target_pairs={{0,64},{1,65},{2,66},{3,67},{4,68},{5,69},{6,70},{7,71},{8,72},{9,... | collective-permute-start | bytes 589832 | tf_op jit(solution)/shard_map/ppermute | solution.py:430
  130.1 2.6 collective-permute-start.5
  130.8 6.1 %collective-permute-start.3 = (f32[12,8,512]{2,1,0:T(8,128)S(1)}, f32[12,8,512]{2,1,0:T(8,128)S(1)}, u32[]{:S(2)}, u32[]{:S(2)}) collective-permute-start(f32[12,8,512]{2,1,0:T(8,128)S(1)} %get-tuple-element.68), channel_id=1, source_target_pairs={{0,32},{1,33},{2,34},{3,35},{4,36},{5,37},{6,38},{7,39},{8,40},{9,... | collective-permute-start | bytes 589832 | tf_op jit(solution)/shard_map/ppermute | solution.py:430
  140.4 16.0 %collective-permute-start.8 = (f32[12,8,512]{2,1,0:T(8,128)}, f32[12,8,512]{2,1,0:T(8,128)S(1)}, u32[]{:S(2)}, u32[]{:S(2)}) collective-permute-start(f32[12,8,512]{2,1,0:T(8,128)} %slices.1), channel_id=1, source_target_pairs={{0,64},{32,96},{64,0},{96,32},{1,65},{33,97},{65,1},{97,33},{2,66}... | collective-permute-start | bytes 589832 | tf_op jit(solution)/shard_map/ppermute | solution.py:380
  150.2 11.8 %collective-permute-start.6 = (f32[6,8,512]{2,1,0:T(8,128)S(1)}, f32[6,8,512]{2,1,0:T(8,128)S(1)}, u32[]{:S(2)}, u32[]{:S(2)}) collective-permute-start(f32[6,8,512]{2,1,0:T(8,128)S(1)} %get-tuple-element.71), channel_id=1, source_target_pairs={{0,0},{1,1},{2,4},{3,5},{4,2},{5,3},{6,6},{7,7},{8,32},{9,33},{10,... | collective-permute-start | bytes 294920 | tf_op jit(solution)/shard_map/ppermute | solution.py:447
  153.3 8.7 %collective-permute-start.7 = (f32[6,8,512]{2,1,0:T(8,128)S(1)}, f32[6,8,512]{2,1,0:T(8,128)S(1)}, u32[]{:S(2)}, u32[]{:S(2)}) collective-permute-start(f32[6,8,512]{2,1,0:T(8,128)S(1)} %get-tuple-element.72), channel_id=1, source_target_pairs={{0,1},{1,0},{2,5},{3,4},{4,3},{5,2},{6,7},{7,6},{8,33},{9,32},{10,... | collective-permute-start | bytes 294920 | tf_op jit(solution)/shard_map/ppermute | solution.py:448
  157.3 20.9 %collective-permute-start.11 = (f32[2,12,8,512]{3,2,1,0:T(8,128)S(1)}, f32[2,12,8,512]{3,2,1,0:T(8,128)S(1)}, u32[]{:S(2)}, u32[]{:S(2)}) collective-permute-start(f32[2,12,8,512]{3,2,1,0:T(8,128)S(1)} %pad_maximum_fusion.refs_0_), channel_id=1, source_target_pairs={{0,3},{1,2},{2,1},{3,0},{4,7},{5,6},{6,5},{7,4},{8,11},{9,10},{10,... | collective-permute-start | bytes 1179656 | tf_op jit(solution)/shard_map/ppermute | solution.py:380
  161.4 16.9 %collective-permute-start.10 = (f32[2,12,8,512]{3,2,1,0:T(8,128)S(1)}, f32[2,12,8,512]{3,2,1,0:T(8,128)S(1)}, u32[]{:S(2)}, u32[]{:S(2)}) collective-permute-start(f32[2,12,8,512]{3,2,1,0:T(8,128)S(1)} %pad_maximum_fusion.refs_0_), channel_id=1, source_target_pairs={{0,2},{1,3},{2,0},{3,1},{4,6},{5,7},{6,4},{7,5},{8,10},{9,11},{10,... | collective-permute-start | bytes 1179656 | tf_op jit(solution)/shard_map/ppermute | solution.py:380
  161.4 17.7 %collective-permute-start.9 = (f32[2,12,8,512]{3,2,1,0:T(8,128)S(1)}, f32[2,12,8,512]{3,2,1,0:T(8,128)}, u32[]{:S(2)}, u32[]{:S(2)}) collective-permute-start(f32[2,12,8,512]{3,2,1,0:T(8,128)S(1)} %pad_maximum_fusion.refs_0_), channel_id=1, source_target_pairs={{0,1},{1,0},{2,3},{3,2},{4,5},{5,4},{6,7},{7,6},{8,9},{9,8},{10,11... | collective-permute-start | bytes 1179656 | tf_op jit(solution)/shard_map/ppermute | solution.py:380
  180.4 28.3 %all-to-all-start.3 = ((f32[8,96,512]{2,1,0:T(8,128)}), f32[8,96,512]{2,1,0:T(8,128)S(1)}, u32[]{:S(2)}, u32[]{:S(2)}) async-start(f32[8,96,512]{2,1,0:T(8,128)} %broadcast_in_dim.65), calls=%async_computation.3 | async-start | bytes 3145728 | tf_op jit(solution)/shard_map/all_to_all | solution.py:458
  188.2 2.1 collective-permute-start.12
  188.9 2.1 collective-permute-start.13
  189.0 3.2 %collective-permute-start.14 = (f32[2,12,8,512]{3,2,1,0:T(8,128)}, f32[2,12,8,512]{3,2,1,0:T(8,128)S(1)}, u32[]{:S(2)}, u32[]{:S(2)}) collective-permute-start(f32[2,12,8,512]{3,2,1,0:T(8,128)} %copy-done.6), channel_id=1, source_target_pairs={{0,32},{32,0},{64,96},{96,64},{1,33},{33,1},{65,97},{97,65},{2,34}... | collective-permute-start | bytes 1179656 | tf_op jit(solution)/shard_map/ppermute | solution.py:380
  189.4 3.5 %collective-permute-start.15 = (f32[2,12,8,512]{3,2,1,0:T(8,128)S(1)}, f32[2,12,8,512]{3,2,1,0:T(8,128)S(1)}, u32[]{:S(2)}, u32[]{:S(2)}) collective-permute-start(f32[2,12,8,512]{3,2,1,0:T(8,128)S(1)} %collective-permute-done.11.refs_3_), channel_id=1, source_target_pairs={{0,32},{32,0},{64,96},{96,64},{1,33},{33,1},{65,97},{97,65},{2,34}... | collective-permute-start | bytes 1179656 | tf_op jit(solution)/shard_map/ppermute | solution.py:380
  208.7 58.9 %all-to-all-start.4 = ((f32[128,64,128]{2,1,0:T(8,128)}), f32[128,64,128]{2,1,0:T(8,128)}, u32[]{:S(2)}, u32[]{:S(2)}) async-start(f32[128,64,128]{2,1,0:T(8,128)} %bitcast.57), calls=%async_computation.4 | async-start | bytes 8388608 | tf_op jit(solution)/shard_map/all_to_all | solution.py:463
  (16 other events, 20.8 us)

commit v9 on v8

--- a/solution.py
+++ b/solution.py
@@ -449,8 +449,8 @@
     mine = jnp.stack([jnp.where(even, one, two), jnp.where(even, two, one)], axis=1)
     mine = mine.reshape(PC, 16, W)
     pair = jnp.stack([slices, flipped(slices, "front", 2)])
+    pair, mine = lax.optimization_barrier((pair, mine))
     pair = [pair] + [flipped(pair, "col", bits) for bits in range(1, COLS)]
-    mine, *pair = lax.optimization_barrier((mine, *pair))
     rows_raw = pair + [flipped(x, "front", 1) for x in pair]
 
     mine, upper_recv = lax.optimization_barrier((mine, upper_recv))

time: 279 us -> 267 us (0.957)
  waiting for transfers between devices: 86.2 us -> 68.5 us
  local copies, waits for them, and re-layouts: 26.1 us -> 30.8 us
  starting transfers between devices: 76.9 us -> 81.4 us
    all_to_all x1, waiting for transfers between devices: 15.1 us -> 0.01 us  [body(): lax.all_to_all(mine, 'row', 0, 0, tiled=True).reshape(ROWS, PC, 16, W)]
    ppermute x1, starting transfers between devices: 3.07 us -> 11.6 us  [body(): lax.ppermute(jnp.where(even, slices[:PC], slices[PC:]), ALL, swap_pairs(0))]
    ppermute x8, waiting for transfers between devices: 17.4 us -> 13.8 us  [flipped(): return lax.ppermute(x, axis, [(i, i ^ bits) for i in range(size)])]
    ppermute x8, starting transfers between devices: 14.9 us -> 12 us  [flipped(): return lax.ppermute(x, axis, [(i, i ^ bits) for i in range(size)])]
    unnamed x42 -> x48, local copies, waits for them, and re-layouts: 20.2 us -> 22.7 us
  transfers between devices with their start and end apart: 21 -> 21, of which waited for: 9 -> 8; matrix products, arithmetic and copies ran while one was open for 5% -> 5% of each run, Pallas kernels for 22% -> 23%
where the time goes in v9:
time: 267 us; the launch traced here: 266 us
  starting transfers between devices  81.4 us (30%)
  Pallas kernels  73.4 us (27%)
  waiting for transfers between devices  68.5 us (26%)
  local copies, waits for them, and re-layouts  30.8 us (12%)
  other arithmetic  8.01 us (3%)
  between operations  3.73 us (1%)
    pallas_call x1, Pallas kernels, factor_inverse(): pl.pallas_call(factor_kernel, name='factor', in_specs=[vmem], out_specs=[...  33.5 us
    ppermute x3, waiting for transfers between devices, body(): lax.ppermute(first[:, :, k], 'col', [(0, k)])  23.1 us
    unnamed x48, local copies, waits for them, and re-layouts  22.7 us
    all_to_all x1, waiting for transfers between devices, body(): lower_recv = lax.all_to_all(lower, ALL, 0, 0, tiled=True)  18.3 us
    pallas_call x2, Pallas kernels, finish(): pl.pallas_call(final_kernel, name='finish', grid_spec=pltpu.PrefetchScala...  17.2 us
    pallas_call x1, Pallas kernels, make_panels(): pl.pallas_call(panel_kernel, name='panels', grid_spec=pltpu.PrefetchScala...  14.7 us
    ppermute x8, waiting for transfers between devices, flipped(): return lax.ppermute(x, axis, [(i, i ^ bits) for i in range(size)])  13.8 us
    ppermute x8, starting transfers between devices, flipped(): return lax.ppermute(x, axis, [(i, i ^ bits) for i in range(size)])  12 us
  transfers between devices with their start and end apart: 21, of which 8 were waited for; matrix products, arithmetic and copies ran while one was open for 5% of the time, Pallas kernels for 23%

profile of v9, /device:TPU:1, one launch (start us, length us, event | category | flops | bytes accessed | tf_op | source)
XLA Modules:
  0.0 265.9 jit_solution(2413904778144674142)
XLA Ops:
  6.2 3.4 %lead.1 = f32[4,8,4,24,128]{4,3,2,1,0:T(8,128)} custom-call(s32[8]{0:T(128)} %slice_reduce_fusion.1.keep_ref, s32[2]{0:T(128)} %get-tuple-element.71.info_ref, f32[1024,2048]{1,0:T(8,128)} %bitcast.54, f32[1536,768]{1,0:T(8,128)} %parent_ref.1), custom_call_target="tpu_custom_call" | custom-call | tf_op jit(solution)/shard_map/lead/pallas_call | solution.py:75
  9.6 11.5 %all-to-all-start = ((f32[128,24,128]{2,1,0:T(8,128)}), f32[128,24,128]{2,1,0:T(8,128)S(1)}, u32[]{:S(2)}, u32[]{:S(2)}) async-start(f32[128,24,128]{2,1,0:T(8,128)} %bitcast.65), calls=%async_computation | async-start | bytes 3145728 | tf_op jit(solution)/shard_map/all_to_all | solution.py:414
  25.2 6.1 %collective-permute-start.2 = (f32[12,4,8,512]{3,2,0,1:T(8,128)}, f32[12,4,8,512]{3,2,0,1:T(8,128)}, u32[]{:S(2)}, u32[]{:S(2)}) collective-permute-start(f32[12,4,8,512]{3,2,0,1:T(8,128)} %bitcast.51), channel_id=1, source_target_pairs={{0,3},{4,7},{8,11},{12,15},{16,19},{20,23},{24,27},{28,31},{32,35}... | collective-permute-start | bytes 2359304 | tf_op jit(solution)/shard_map/ppermute | solution.py:417
  37.6 6.7 %all-to-all-done.recv_ref = f32[128,24,128]{2,1,0:T(8,128)S(1)} async-done(((f32[128,24,128]{2,1,0:T(8,128)}), f32[128,24,128]{2,1,0:T(8,128)S(1)}, u32[]{:S(2)}, u32[]{:S(2)}) %all-to-all-start) | async-done | bytes 1572896 | tf_op jit(solution)/shard_map/all_to_all | solution.py:414
  45.7 5.8 %all-to-all-start.1 = ((f32[128,16,128]{2,1,0:T(8,128)}), f32[128,16,128]{2,1,0:T(8,128)S(1)}, u32[]{:S(2)}, u32[]{:S(2)}) async-start(f32[128,16,128]{2,1,0:T(8,128)} %broadcast_in_dim.63), calls=%async_computation.1 | async-start | bytes 2097152 | tf_op jit(solution)/shard_map/all_to_all | solution.py:422
  51.5 3.4 %copy-done.1 = f32[1,1024,2048]{2,1,0:T(8,128)S(1)} copy-done((f32[1,1024,2048]{2,1,0:T(8,128)S(1)}, f32[1,1024,2048]{2,1,0:T(8,128)}, u32[]{:S(2)}) %copy-start.1) | copy-done | bytes 8388632
  60.8 7.0 %collective-permute-done.2 = f32[12,4,8,512]{3,2,0,1:T(8,128)} collective-permute-done((f32[12,4,8,512]{3,2,0,1:T(8,128)}, f32[12,4,8,512]{3,2,0,1:T(8,128)}, u32[]{:S(2)}, u32[]{:S(2)}) %collective-permute-start.2) | collective-permute-done | bytes 786464 | tf_op jit(solution)/shard_map/ppermute | solution.py:417
  67.8 16.1 %collective-permute-done.1 = f32[12,4,8,512]{3,2,0,1:T(8,128)} collective-permute-done((f32[12,4,8,512]{3,2,0,1:T(8,128)}, f32[12,4,8,512]{3,2,0,1:T(8,128)}, u32[]{:S(2)}, u32[]{:S(2)}) %collective-permute-start.1) | collective-permute-done | bytes 786464 | tf_op jit(solution)/shard_map/ppermute | solution.py:417
  85.9 9.2 %all-to-all-start.2 = ((f32[128,64,128]{2,1,0:T(8,128)}), f32[128,64,128]{2,1,0:T(8,128)}, u32[]{:S(2)}, u32[]{:S(2)}) async-start(f32[128,64,128]{2,1,0:T(8,128)} %bitcast.58), calls=%async_computation.2 | async-start | bytes 8388608 | tf_op jit(solution)/shard_map/all_to_all | solution.py:426
  96.1 33.5 %factor.1 = (bf16[512,512]{1,0:T(8,128)(2,1)S(1)}, bf16[512,512]{1,0:T(8,128)(2,1)S(1)}) custom-call(f32[128,16,128]{2,1,0:T(8,128)S(1)} %all-to-all-done.1.x_ref), custom_call_target="tpu_custom_call" | custom-call | tf_op jit(solution)/shard_map/factor/pallas_call | solution.py:225
  132.9 4.2 %collective-permute-done.3 = f32[12,8,512]{2,1,0:T(8,128)S(1)} collective-permute-done((f32[12,8,512]{2,1,0:T(8,128)S(1)}, f32[12,8,512]{2,1,0:T(8,128)S(1)}, u32[]{:S(2)}, u32[]{:S(2)}) %collective-permute-start.3) | collective-permute-done | bytes 196640 | tf_op jit(solution)/shard_map/ppermute | solution.py:430
  137.9 2.7 %slices.1 = f32[12,8,512]{2,1,0:T(8,128)} custom-call(s32[4,12]{1,0:T(4,128)} %broadcast_add_fusion.2.inv_row_ref, s32[4,4]{1,0:T(4,128)} %broadcast_add_fusion.inv_lead_ref, f32[128,24,128]{2,1,0:T(8,128)} %copy-done.18, f32[12,8,512]{2,1,0:T(8,128)} %bitcast_select_fusion.parent_ref), custom_call_target="tpu_custom_call" | custom-call | tf_op jit(solution)/shard_map/slices/pallas_call | solution.py:107
  141.6 11.6 %collective-permute-start.7 = (f32[6,8,512]{2,1,0:T(8,128)S(1)}, f32[6,8,512]{2,1,0:T(8,128)S(1)}, u32[]{:S(2)}, u32[]{:S(2)}) collective-permute-start(f32[6,8,512]{2,1,0:T(8,128)S(1)} %get-tuple-element.65), channel_id=1, source_target_pairs={{0,0},{1,1},{2,4},{3,5},{4,2},{5,3},{6,6},{7,7},{8,32},{9,33},{10,... | collective-permute-start | bytes 294920 | tf_op jit(solution)/shard_map/ppermute | solution.py:447
  154.4 3.1 %collective-permute-start.6 = (f32[12,8,512]{2,1,0:T(8,128)}, f32[12,8,512]{2,1,0:T(8,128)S(1)}, u32[]{:S(2)}, u32[]{:S(2)}) collective-permute-start(f32[12,8,512]{2,1,0:T(8,128)} %slices.1), channel_id=1, source_target_pairs={{0,64},{32,96},{64,0},{96,32},{1,65},{33,97},{65,1},{97,33},{2,66}... | collective-permute-start | bytes 589832 | tf_op jit(solution)/shard_map/ppermute | solution.py:380
  157.5 2.2 collective-permute-done.8
  163.1 6.7 %all-to-all-start.3 = ((f32[8,96,512]{2,1,0:T(8,128)}), f32[8,96,512]{2,1,0:T(8,128)S(1)}, u32[]{:S(2)}, u32[]{:S(2)}) async-start(f32[8,96,512]{2,1,0:T(8,128)} %broadcast_in_dim.65), calls=%async_computation.3 | async-start | bytes 3145728 | tf_op jit(solution)/shard_map/all_to_all | solution.py:458
  169.8 2.8 %collective-permute-start.11 = (f32[2,12,8,512]{3,2,1,0:T(8,128)S(1)}, f32[2,12,8,512]{3,2,1,0:T(8,128)S(1)}, u32[]{:S(2)}, u32[]{:S(2)}) collective-permute-start(f32[2,12,8,512]{3,2,1,0:T(8,128)S(1)} %pad_maximum_fusion.refs_0_), channel_id=1, source_target_pairs={{0,3},{1,2},{2,1},{3,0},{4,7},{5,6},{6,5},{7,4},{8,11},{9,10},{10,... | collective-permute-start | bytes 1179656 | tf_op jit(solution)/shard_map/ppermute | solution.py:380
  173.2 3.3 %collective-permute-start.12 = (f32[2,12,8,512]{3,2,1,0:T(8,128)S(1)}, f32[2,12,8,512]{3,2,1,0:T(8,128)S(1)}, u32[]{:S(2)}, u32[]{:S(2)}) collective-permute-start(f32[2,12,8,512]{3,2,1,0:T(8,128)S(1)} %pad_maximum_fusion.refs_0_), channel_id=1, source_target_pairs={{0,32},{32,0},{64,96},{96,64},{1,33},{33,1},{65,97},{97,65},{2,34}... | collective-permute-start | bytes 1179656 | tf_op jit(solution)/shard_map/ppermute | solution.py:380
  176.5 12.9 %collective-permute-done.11.refs_3_ = f32[2,12,8,512]{3,2,1,0:T(8,128)S(1)} collective-permute-done((f32[2,12,8,512]{3,2,1,0:T(8,128)S(1)}, f32[2,12,8,512]{3,2,1,0:T(8,128)S(1)}, u32[]{:S(2)}, u32[]{:S(2)}) %collective-permute-start.11) | collective-permute-done | bytes 393248 | tf_op jit(solution)/shard_map/ppermute | solution.py:380
  196.1 10.2 %all-to-all-start.4 = ((f32[128,64,128]{2,1,0:T(8,128)}), f32[128,64,128]{2,1,0:T(8,128)}, u32[]{:S(2)}, u32[]{:S(2)}) async-start(f32[128,64,128]{2,1,0:T(8,128)} %bitcast.57), calls=%async_computation.4 | async-start | bytes 8388608 | tf_op jit(solution)/shard_map/all_to_all | solution.py:463
  213.7 14.7 %panels.1 = (f32[1536,512]{1,0:T(8,128)}, bf16[768,512]{1,0:T(8,128)(2,1)S(1)}, bf16[768,512]{1,0:T(8,128)(2,1)S(1)}) custom-call(s32[2]{0:T(128)S(1)} %get-tuple-element.72.place_ref, f32[2,12,8,512]{3,2,1,0:T(8,128)S(1)} %pad_maximum_fusion.refs_0_, f32[2,12,8,512]{3,2,1,0:T(8,128)S(1)} %copy-done.9, f32[2,12,8,512]{3,2,1,0:T(8,128)S(1)} %copy-done.7, ...), custom_call_target="tpu_custom_call" | custom-call | tf_op jit(solution)/shard_map/panels/pallas_call | solution.py:281
  230.1 8.6 %finish.2.refs_20_ = f32[12,2,64,768]{3,2,1,0:T(8,128)} custom-call(s32[4,12]{1,0:T(4,128)} %broadcast_add_fusion.2.inv_row_ref, s32[4,6]{1,0:T(4,128)} %broadcast_add_fusion.1.inv_col_ref, s32[2]{0:T(128)} %add_convert_fusion.lead_ref, ...), custom_call_target="tpu_custom_call" | custom-call | tf_op jit(solution)/shard_map/finish/pallas_call | solution.py:359
  238.8 18.3 %all-to-all-done.4.refs_0_.refs_1_.refs_2_.refs_3_.refs_4_.refs_5_.refs_6_.refs_7_.refs_8_.refs_9_.refs_10_.refs_11_.refs_12_.refs_13_.refs_14_.refs_15_ = f32[128,64,128]{2,1,0:T(8,128)} async-done(((f32[128,64,128]{2,1,0:T(8,128)}), f32[128,64,128]{2,1,0:T(8,128)}, u32[]{:S(2)}, u32[]{:S(2)}) %all-to-all-start.4) | async-done | bytes 4194336 | tf_op jit(solution)/shard_map/all_to_all | solution.py:463
  257.1 8.6 %finish.3 = f32[12,2,64,768]{3,2,1,0:T(8,128)} custom-call(s32[4,12]{1,0:T(4,128)} %broadcast_add_fusion.2.inv_row_ref, s32[4,6]{1,0:T(4,128)} %broadcast_add_fusion.1.inv_col_ref, s32[2]{0:T(128)} %add_convert_fusion.lead_ref, ...), custom_call_target="tpu_custom_call", output_to_operand_aliasing={{}: (23, {})} | custom-call | tf_op jit(solution)/shard_map/finish/pallas_call | solution.py:359
  (104 shorter events, 49.5 us)
Async XLA Ops:
  9.6 34.7 %all-to-all-start = ((f32[128,24,128]{2,1,0:T(8,128)}), f32[128,24,128]{2,1,0:T(8,128)S(1)}, u32[]{:S(2)}, u32[]{:S(2)}) async-start(f32[128,24,128]{2,1,0:T(8,128)} %bitcast.65), calls=%async_computation | async-start | bytes 3145728 | tf_op jit(solution)/shard_map/all_to_all | solution.py:414
  25.2 42.6 %collective-permute-start.2 = (f32[12,4,8,512]{3,2,0,1:T(8,128)}, f32[12,4,8,512]{3,2,0,1:T(8,128)}, u32[]{:S(2)}, u32[]{:S(2)}) collective-permute-start(f32[12,4,8,512]{3,2,0,1:T(8,128)} %bitcast.51), channel_id=1, source_target_pairs={{0,3},{4,7},{8,11},{12,15},{16,19},{20,23},{24,27},{28,31},{32,35}... | collective-permute-start | bytes 2359304 | tf_op jit(solution)/shard_map/ppermute | solution.py:417
  32.2 35.6 %collective-permute-start = (f32[12,4,8,512]{3,2,0,1:T(8,128)}, f32[12,4,8,512]{3,2,0,1:T(8,128)}, u32[]{:S(2)}, u32[]{:S(2)}) collective-permute-start(f32[12,4,8,512]{3,2,0,1:T(8,128)} %bitcast.53), channel_id=1, source_target_pairs={{0,1},{4,5},{8,9},{12,13},{16,17},{20,21},{24,25},{28,29},{32,33},... | collective-permute-start | bytes 2359304 | tf_op jit(solution)/shard_map/ppermute | solution.py:417
  35.3 48.5 %collective-permute-start.1 = (f32[12,4,8,512]{3,2,0,1:T(8,128)}, f32[12,4,8,512]{3,2,0,1:T(8,128)}, u32[]{:S(2)}, u32[]{:S(2)}) collective-permute-start(f32[12,4,8,512]{3,2,0,1:T(8,128)} %bitcast.52), channel_id=1, source_target_pairs={{0,2},{4,6},{8,10},{12,14},{16,18},{20,22},{24,26},{28,30},{32,34}... | collective-permute-start | bytes 2359304 | tf_op jit(solution)/shard_map/ppermute | solution.py:417
  44.3 12.5 %copy-start.18 = (f32[128,24,128]{2,1,0:T(8,128)}, f32[128,24,128]{2,1,0:T(8,128)S(1)}, u32[]{:S(2)}) copy-start(f32[128,24,128]{2,1,0:T(8,128)S(1)} %all-to-all-done.recv_ref) | copy-start | bytes 4718596
  45.7 40.2 %all-to-all-start.1 = ((f32[128,16,128]{2,1,0:T(8,128)}), f32[128,16,128]{2,1,0:T(8,128)S(1)}, u32[]{:S(2)}, u32[]{:S(2)}) async-start(f32[128,16,128]{2,1,0:T(8,128)} %broadcast_in_dim.63), calls=%async_computation.1 | async-start | bytes 2097152 | tf_op jit(solution)/shard_map/all_to_all | solution.py:422
  54.8 29.0 %copy-start.19 = (f32[12,4,1,8,512]{4,3,2,1,0:T(8,128)S(1)}, f32[12,4,1,8,512]{4,3,2,1,0:T(8,128)}, u32[]{:S(2)}) copy-start(f32[12,4,1,8,512]{4,3,2,1,0:T(8,128)} %get-tuple-element.58) | copy-start | bytes 2359300
  85.8 9.2 %copy-start.20 = (s32[4,64]{1,0:T(4,128)S(1)}, s32[4,64]{1,0:T(4,128)}, u32[]{:S(2)}) copy-start(s32[4,64]{1,0:T(4,128)} %param.6) | copy-start | bytes 3076
  85.9 75.9 %all-to-all-start.2 = ((f32[128,64,128]{2,1,0:T(8,128)}), f32[128,64,128]{2,1,0:T(8,128)}, u32[]{:S(2)}, u32[]{:S(2)}) async-start(f32[128,64,128]{2,1,0:T(8,128)} %bitcast.58), calls=%async_computation.2 | async-start | bytes 8388608 | tf_op jit(solution)/shard_map/all_to_all | solution.py:426
  129.7 3.2 %collective-permute-start.4 = (f32[12,8,512]{2,1,0:T(8,128)S(1)}, f32[12,8,512]{2,1,0:T(8,128)S(1)}, u32[]{:S(2)}, u32[]{:S(2)}) collective-permute-start(f32[12,8,512]{2,1,0:T(8,128)S(1)} %get-tuple-element.60), channel_id=1, source_target_pairs={{0,64},{1,65},{2,66},{3,67},{4,68},{5,69},{6,70},{7,71},{8,72},{9,... | collective-permute-start | bytes 589832 | tf_op jit(solution)/shard_map/ppermute | solution.py:430
  130.3 2.6 collective-permute-start.5
  131.0 6.1 %collective-permute-start.3 = (f32[12,8,512]{2,1,0:T(8,128)S(1)}, f32[12,8,512]{2,1,0:T(8,128)S(1)}, u32[]{:S(2)}, u32[]{:S(2)}) collective-permute-start(f32[12,8,512]{2,1,0:T(8,128)S(1)} %get-tuple-element.62), channel_id=1, source_target_pairs={{0,32},{1,33},{2,34},{3,35},{4,36},{5,37},{6,38},{7,39},{8,40},{9,... | collective-permute-start | bytes 589832 | tf_op jit(solution)/shard_map/ppermute | solution.py:430
  141.6 15.9 %collective-permute-start.7 = (f32[6,8,512]{2,1,0:T(8,128)S(1)}, f32[6,8,512]{2,1,0:T(8,128)S(1)}, u32[]{:S(2)}, u32[]{:S(2)}) collective-permute-start(f32[6,8,512]{2,1,0:T(8,128)S(1)} %get-tuple-element.65), channel_id=1, source_target_pairs={{0,0},{1,1},{2,4},{3,5},{4,2},{5,3},{6,6},{7,7},{8,32},{9,33},{10,... | collective-permute-start | bytes 294920 | tf_op jit(solution)/shard_map/ppermute | solution.py:447
  153.2 6.6 %collective-permute-start.8 = (f32[6,8,512]{2,1,0:T(8,128)S(1)}, f32[6,8,512]{2,1,0:T(8,128)S(1)}, u32[]{:S(2)}, u32[]{:S(2)}) collective-permute-start(f32[6,8,512]{2,1,0:T(8,128)S(1)} %get-tuple-element.66), channel_id=1, source_target_pairs={{0,1},{1,0},{2,5},{3,4},{4,3},{5,2},{6,7},{7,6},{8,33},{9,32},{10,... | collective-permute-start | bytes 294920 | tf_op jit(solution)/shard_map/ppermute | solution.py:448
  154.4 6.4 %collective-permute-start.6 = (f32[12,8,512]{2,1,0:T(8,128)}, f32[12,8,512]{2,1,0:T(8,128)S(1)}, u32[]{:S(2)}, u32[]{:S(2)}) collective-permute-start(f32[12,8,512]{2,1,0:T(8,128)} %slices.1), channel_id=1, source_target_pairs={{0,64},{32,96},{64,0},{96,32},{1,65},{33,97},{65,1},{97,33},{2,66}... | collective-permute-start | bytes 589832 | tf_op jit(solution)/shard_map/ppermute | solution.py:380
  163.1 33.0 %all-to-all-start.3 = ((f32[8,96,512]{2,1,0:T(8,128)}), f32[8,96,512]{2,1,0:T(8,128)S(1)}, u32[]{:S(2)}, u32[]{:S(2)}) async-start(f32[8,96,512]{2,1,0:T(8,128)} %broadcast_in_dim.65), calls=%async_computation.3 | async-start | bytes 3145728 | tf_op jit(solution)/shard_map/all_to_all | solution.py:458
  169.8 19.6 %collective-permute-start.11 = (f32[2,12,8,512]{3,2,1,0:T(8,128)S(1)}, f32[2,12,8,512]{3,2,1,0:T(8,128)S(1)}, u32[]{:S(2)}, u32[]{:S(2)}) collective-permute-start(f32[2,12,8,512]{3,2,1,0:T(8,128)S(1)} %pad_maximum_fusion.refs_0_), channel_id=1, source_target_pairs={{0,3},{1,2},{2,1},{3,0},{4,7},{5,6},{6,5},{7,4},{8,11},{9,10},{10,... | collective-permute-start | bytes 1179656 | tf_op jit(solution)/shard_map/ppermute | solution.py:380
  172.6 18.5 %collective-permute-start.10 = (f32[2,12,8,512]{3,2,1,0:T(8,128)S(1)}, f32[2,12,8,512]{3,2,1,0:T(8,128)S(1)}, u32[]{:S(2)}, u32[]{:S(2)}) collective-permute-start(f32[2,12,8,512]{3,2,1,0:T(8,128)S(1)} %pad_maximum_fusion.refs_0_), channel_id=1, source_target_pairs={{0,2},{1,3},{2,0},{3,1},{4,6},{5,7},{6,4},{7,5},{8,10},{9,11},{10,... | collective-permute-start | bytes 1179656 | tf_op jit(solution)/shard_map/ppermute | solution.py:380
  172.6 19.3 %collective-permute-start.9 = (f32[2,12,8,512]{3,2,1,0:T(8,128)S(1)}, f32[2,12,8,512]{3,2,1,0:T(8,128)S(1)}, u32[]{:S(2)}, u32[]{:S(2)}) collective-permute-start(f32[2,12,8,512]{3,2,1,0:T(8,128)S(1)} %pad_maximum_fusion.refs_0_), channel_id=1, source_target_pairs={{0,1},{1,0},{2,3},{3,2},{4,5},{5,4},{6,7},{7,6},{8,9},{9,8},{10,11... | collective-permute-start | bytes 1179656 | tf_op jit(solution)/shard_map/ppermute | solution.py:380
  173.2 19.9 %collective-permute-start.12 = (f32[2,12,8,512]{3,2,1,0:T(8,128)S(1)}, f32[2,12,8,512]{3,2,1,0:T(8,128)S(1)}, u32[]{:S(2)}, u32[]{:S(2)}) collective-permute-start(f32[2,12,8,512]{3,2,1,0:T(8,128)S(1)} %pad_maximum_fusion.refs_0_), channel_id=1, source_target_pairs={{0,32},{32,0},{64,96},{96,64},{1,33},{33,1},{65,97},{97,65},{2,34}... | collective-permute-start | bytes 1179656 | tf_op jit(solution)/shard_map/ppermute | solution.py:380
  189.4 4.5 %collective-permute-start.15 = (f32[2,12,8,512]{3,2,1,0:T(8,128)S(1)}, f32[2,12,8,512]{3,2,1,0:T(8,128)S(1)}, u32[]{:S(2)}, u32[]{:S(2)}) collective-permute-start(f32[2,12,8,512]{3,2,1,0:T(8,128)S(1)} %collective-permute-done.11.refs_3_), channel_id=1, source_target_pairs={{0,32},{32,0},{64,96},{96,64},{1,33},{33,1},{65,97},{97,65},{2,34}... | collective-permute-start | bytes 1179656 | tf_op jit(solution)/shard_map/ppermute | solution.py:380
  191.1 3.5 %collective-permute-start.14 = (f32[2,12,8,512]{3,2,1,0:T(8,128)S(1)}, f32[2,12,8,512]{3,2,1,0:T(8,128)S(1)}, u32[]{:S(2)}, u32[]{:S(2)}) collective-permute-start(f32[2,12,8,512]{3,2,1,0:T(8,128)S(1)} %collective-permute-done.10.refs_2_), channel_id=1, source_target_pairs={{0,32},{32,0},{64,96},{96,64},{1,33},{33,1},{65,97},{97,65},{2,34}... | collective-permute-start | bytes 1179656 | tf_op jit(solution)/shard_map/ppermute | solution.py:380
  191.8 3.5 %collective-permute-start.13 = (f32[2,12,8,512]{3,2,1,0:T(8,128)S(1)}, f32[2,12,8,512]{3,2,1,0:T(8,128)S(1)}, u32[]{:S(2)}, u32[]{:S(2)}) collective-permute-start(f32[2,12,8,512]{3,2,1,0:T(8,128)S(1)} %collective-permute-done.9.refs_1_), channel_id=1, source_target_pairs={{0,32},{32,0},{64,96},{96,64},{1,33},{33,1},{65,97},{97,65},{2,34}... | collective-permute-start | bytes 1179656 | tf_op jit(solution)/shard_map/ppermute | solution.py:380
  196.1 61.0 %all-to-all-start.4 = ((f32[128,64,128]{2,1,0:T(8,128)}), f32[128,64,128]{2,1,0:T(8,128)}, u32[]{:S(2)}, u32[]{:S(2)}) async-start(f32[128,64,128]{2,1,0:T(8,128)} %bitcast.57), calls=%async_computation.4 | async-start | bytes 8388608 | tf_op jit(solution)/shard_map/all_to_all | solution.py:463
  (19 other events, 24.4 us)
